TPU v7x, 32 devices: a whole 2x2x4 slice. The times are simulated.
32 devices in a mesh: sec: 4 (over y, x), ta: 8 (over z, core).
Axes of the slice: x: 2, y: 2, z: 4, core: 2. Of those that a mesh axis runs over, the one named last changes fastest.
Arguments:
- sink_vectors: bfloat16 [2, 8, 4096, 512], P(None, 'ta', 'sec'), may hold values from -0.0625 to 0.0625
- propagators: bfloat16 [3, 2, 8, 4096, 512], P(None, None, 'ta', 'sec'), may hold values from -6 to 6
- live_rows: int32 [4], replicated, may hold values from 512 to 1024, as said below
- source_times: int32 [3], replicated, may hold values from 0 to 7
Outputs:
- sandwich: bfloat16 [3, 3, 3, 2, 8, 512, 512], P(None, None, None, None, 'ta', 'sec')
Inputs may be any that keep to these rules, and one draw needn't show every extreme that they name: `live_rows`: some section has exactly 1024 live rows in every draw.
All inputs are finite; a program needn't handle non-finite values.
Results may differ from a plain program's by a relative error of at most 0.02.
Values may be sent and summed in bfloat16 or wider, within the bound.
No kernel may reach another device: no remote copies, remote signals or barrier semaphores. Data moves between devices by JAX's collectives and lax.ppermute only.
A program may use at most 64 MiB of HBM per device.

v0:
```python
import functools

import jax
import jax.numpy as jnp
from jax import lax
from jax.experimental import pallas as pl
from jax.experimental.pallas import tpu as pltpu
from jax.sharding import PartitionSpec as P

STOPS = 3
dot = functools.partial(jnp.dot, preferred_element_type=jnp.float32)


def shifted(value, steps):
    count = lax.axis_size("ta")
    pairs = [(source, (source + steps) % count) for source in range(count)]
    return lax.ppermute(value, "ta", pairs)


def exchanged(value, axis, bit):
    count = lax.axis_size(axis)
    return lax.ppermute(value, axis, [(source, source ^ bit) for source in range(count)])


def reversed_bits(value, width):
    return sum(((value >> place) & 1) << (width - 1 - place) for place in range(width))


def over_rows(left, right):
    return lax.dot_general(
        left, right, (((0,), (0,)), ((), ())), preferred_element_type=jnp.float32
    )


def product_kernel(
    sections, source, live_rows, source_times, sink_hbm, prop_hbm,
    keep_real, send_real, keep_imag, send_imag, sink, prop, real, imag, sems,
):
    section = lax.axis_index("sec")
    copies = []
    for part in range(2):
        copies.append(pltpu.make_async_copy(sink_hbm.at[part, 0], sink.at[part], sems.at[part, 0]))
        copies.append(
            pltpu.make_async_copy(prop_hbm.at[source, part, 0], prop.at[part], sems.at[part, 1])
        )
    for copy in copies:
        copy.start()
    depth, order = sink.shape[1:]
    live = lax.broadcasted_iota(jnp.int32, (depth, order), 0) < live_rows[section]
    sign = jnp.where(lax.axis_index("ta") < source_times[source], -1.0, 1.0).astype(jnp.float32)
    none = jnp.zeros((depth, order), jnp.bfloat16)
    copies[0].wait()
    sink_real = jnp.where(live, sink[0], none)
    copies[1].wait()
    first = over_rows(sink_real, prop[0])
    copies[2].wait()
    sink_imag = jnp.where(live, sink[1], none)
    copies[3].wait()
    real[...] = ((first + over_rows(sink_imag, prop[1])) * sign).astype(jnp.bfloat16)
    imag[...] = (
        (over_rows(sink_real, prop[1]) - over_rows(sink_imag, prop[0])) * sign
    ).astype(jnp.bfloat16)
    half = sections // 2
    width = sections.bit_length() - 1
    rows = order // sections
    for q in range(sections):
        window = pl.ds(pl.multiple_of((section ^ q) * rows, rows), rows)
        slot = reversed_bits(q, width)
        (keep_real if slot < half else send_real)[slot % half] = real[window, :]
        (keep_imag if q < half else send_imag)[q % half] = imag[window, :]


def products(live_rows, source_times, sink_vectors, propagators, source, sections):
    _, _, depth, order = sink_vectors.shape
    columns = propagators.shape[4]
    half = jax.ShapeDtypeStruct((sections // 2, order // sections, columns), jnp.bfloat16)
    scalar = pl.BlockSpec(memory_space=pltpu.SMEM)
    return pl.pallas_call(
        functools.partial(product_kernel, sections, source),
        in_specs=[scalar, scalar]
        + [pl.BlockSpec(memory_space=pltpu.HBM)] * 2,
        out_specs=[pl.BlockSpec(memory_space=pltpu.VMEM)] * 4,
        out_shape=[half] * 4,
        scratch_shapes=[
            pltpu.VMEM((2, depth, order), jnp.bfloat16),
            pltpu.VMEM((2, depth, columns), jnp.bfloat16),
            pltpu.VMEM((order, columns), jnp.bfloat16),
            pltpu.VMEM((order, columns), jnp.bfloat16),
            pltpu.SemaphoreType.DMA((2, 2)),
        ],
        compiler_params=pltpu.CompilerParams(vmem_limit_bytes=20 << 20),
        cost_estimate=pl.CostEstimate(
            flops=8 * order * depth * columns,
            bytes_accessed=4 * depth * (order + columns) + 4 * order * columns,
            transcendentals=0,
        ),
    )(live_rows, source_times, sink_vectors, propagators)


def reduced(keep_real, send_real, keep_imag, send_imag, width):
    for step in range(width):
        got_real = exchanged(send_real, "sec", 1 << step)
        got_imag = exchanged(send_imag, "sec", 1 << (width - 1 - step))
        real = keep_real.astype(jnp.float32) + got_real.astype(jnp.float32)
        imag = keep_imag.astype(jnp.float32) + got_imag.astype(jnp.float32)
        real, imag = real.astype(jnp.bfloat16), imag.astype(jnp.bfloat16)
        half = real.shape[0] // 2
        if half:
            keep_real, send_real = real[:half], real[half:]
            keep_imag, send_imag = imag[:half], imag[half:]
    return jnp.concatenate((real, imag), 0)


def gathered(own, width):
    pieces = [own]
    for q in range(1, 1 << width):
        high = 1 << (q.bit_length() - 1)
        low = q & -q
        if high == low:
            pieces.append(exchanged(own, "sec", high))
        else:
            first, second = pieces[q ^ high], pieces[q ^ low]
            pieces.append((exchanged(first[0], "sec", high), exchanged(second[1], "sec", low)))
    return pieces


def sandwich_kernel(scale, paired, names, source, kind, aliased, *refs):
    left_real, left_imag = refs[0], refs[1]
    blocks = list(refs[2 : 2 + names])
    out, tile, sems = refs[2 + names + aliased :]
    real, imag = [], []
    for pair in paired:
        if pair:
            real.append(blocks.pop(0)[...])
            imag.append(blocks.pop(0)[...])
        else:
            block = blocks.pop(0)
            real.append(block[0])
            imag.append(block[1])
    right_real, right_imag = jnp.concatenate(real, 0), jnp.concatenate(imag, 0)
    one, two = left_real[...], left_imag[...]
    parity = lax.axis_index("ta") % 2
    stop = (2 * parity, 1, 2 - 2 * parity)[kind]
    shape = tile.shape[1:]
    copies = []
    for part in range(2):
        if part == 0:
            value = dot(one, right_real) - dot(two, right_imag)
        else:
            value = dot(one, right_imag) + dot(two, right_real)
        tile[part] = (value * scale).astype(jnp.bfloat16).reshape(shape)
        copies.append(
            pltpu.make_async_copy(tile.at[part], out.at[stop, :, source, part, 0], sems.at[part])
        )
        copies[-1].start()
    for copy in copies:
        copy.wait()


def sandwich(buffer, kind, source, left_real, left_imag, pieces, shape):
    paired = tuple(isinstance(piece, tuple) for piece in pieces)
    blocks = [part for piece in pieces for part in (piece if isinstance(piece, tuple) else (piece,))]
    order = left_real.shape[1]
    operands = [left_real, left_imag, *blocks]
    in_specs = [pl.BlockSpec(memory_space=pltpu.VMEM)] * len(operands)
    aliases = {}
    if buffer is not None:
        aliases = {len(operands): 0}
        in_specs.append(pl.BlockSpec(memory_space=pltpu.HBM))
        operands.append(buffer)
    return pl.pallas_call(
        functools.partial(
            sandwich_kernel, 0.5 * order ** (-0.5), paired, len(blocks), source, kind,
            len(aliases),
        ),
        in_specs=in_specs,
        out_specs=pl.BlockSpec(memory_space=pltpu.HBM),
        out_shape=jax.ShapeDtypeStruct(shape, jnp.bfloat16),
        scratch_shapes=[
            pltpu.VMEM((2, shape[1]) + tuple(shape[5:]), jnp.bfloat16),
            pltpu.SemaphoreType.DMA((2,)),
        ],
        input_output_aliases=aliases,
        compiler_params=pltpu.CompilerParams(vmem_limit_bytes=12 << 20),
        cost_estimate=pl.CostEstimate(
            flops=8 * left_real.shape[0] * order * shape[6],
            bytes_accessed=4 * order * shape[6] + 8 * left_real.size,
            transcendentals=0,
        ),
    )(*operands)


def body(sink_vectors, propagators, live_rows, source_times):
    sections = lax.axis_size("sec")
    width = sections.bit_length() - 1
    section = lax.axis_index("sec")
    first_core = lax.axis_index("ta") % 2 == 0
    sources = propagators.shape[0]
    order = sink_vectors.shape[3]
    rows = order // sections

    own = []
    for s in range(sources):
        halves = products(live_rows, source_times, sink_vectors, propagators, s, sections)
        own.append(reduced(*halves, width))
    second = [shifted(own[s], 2) for s in range(sources)]
    other = [shifted(jnp.where(first_core, own[s], second[s]), 1) for s in range(sources)]

    left = jnp.stack(own, 1)
    left = jnp.concatenate(
        [
            lax.dynamic_slice_in_dim(left, (section ^ q) * rows, rows, axis=3)
            for q in range(sections)
        ],
        3,
    ).reshape(2, sources * rows, order)
    left_real, left_imag = left[0], left[1]

    shape = (STOPS, sources, sources, 2, 1, rows, order)
    result = None
    for s in range(sources):
        pieces = gathered(second[s], width)
        leaves, tree = jax.tree.flatten(pieces)
        swapped = tree.unflatten([exchanged(leaf, "ta", 1) for leaf in leaves])
        result = sandwich(result, 1, s, left_real, left_imag, pieces, shape)
        result = sandwich(result, 0, s, left_real, left_imag, swapped, shape)
    for s in range(sources):
        pieces = gathered(other[s], width)
        result = sandwich(result, 2, s, left_real, left_imag, pieces, shape)
    return result


def solution(mesh):
    return jax.shard_map(
        body,
        mesh=mesh,
        in_specs=(P(None, "ta", "sec", None), P(None, None, "ta", "sec", None), P(), P()),
        out_specs=P(None, None, None, None, "ta", "sec", None),
        check_vma=False,
    )
```

profile of v0, /device:TPU:0, one launch (start us, length us, event | category | flops | bytes accessed | tf_op | source)
XLA Modules:
  0.0 133.6 jit_solution(5874844741764844472)
XLA Ops:
  0.0 2.8 %copy-done = bf16[3,2,1,1024,512]{4,3,2,1,0:T(8,128)(2,1)S(1)} copy-done((bf16[3,2,1,1024,512]{4,3,2,1,0:T(8,128)(2,1)S(1)}, bf16[3,2,1,1024,512]{4,3,2,1,0:T(8,128)(2,1)}, u32[]{:S(2)}) %copy-start) | copy-done | bytes 6291480
  2.8 1.6 %copy-done.1 = bf16[2,1,1024,512]{3,2,1,0:T(8,128)(2,1)S(1)} copy-done((bf16[2,1,1024,512]{3,2,1,0:T(8,128)(2,1)S(1)}, bf16[2,1,1024,512]{3,2,1,0:T(8,128)(2,1)}, u32[]{:S(2)}) %copy-start.1) | copy-done | bytes 2097176
  5.7 3.7 %shard_map.46 = (bf16[2,128,512]{2,1,0:T(8,128)(2,1)S(1)}, bf16[2,128,512]{2,1,0:T(8,128)(2,1)S(1)}, bf16[2,128,512]{2,1,0:T(8,128)(2,1)S(1)}, bf16[2,128,512]{2,1,0:T(8,128)(2,1)S(1)}) custom-call(s32[4]{0:T(128)S(1)} %copy-done.2, s32[3]{0:T(128)S(1)} %copy-done.3, bf16[2,1,1024,512]{3,2,1,0:T(8,128)(2,1)S(1)} %copy-done.1, ...), custom_call_target="tpu_custom_call" | custom-call | flops 2147483648 | bytes 5242880 | tf_op jit(solution)/shard_map/pallas_call | solution.py:78
  9.4 3.1 %collective-permute-start.2 = (bf16[2,128,512]{2,1,0:T(8,128)(2,1)S(1)}, bf16[2,128,512]{2,1,0:T(8,128)(2,1)}, u32[]{:S(2)}, u32[]{:S(2)}) collective-permute-start(bf16[2,128,512]{2,1,0:T(8,128)(2,1)S(1)} %get-tuple-element.20), channel_id=1, source_target_pairs={{0,16},{8,24},{16,0},{24,8},{1,17},{9,25},{17,1},{25,9},{2,18},{10... | collective-permute-start | bytes 786440 | tf_op jit(solution)/shard_map/ppermute | solution.py:22
  12.4 1.5 %collective-permute-start = (bf16[2,128,512]{2,1,0:T(8,128)(2,1)S(1)}, bf16[2,128,512]{2,1,0:T(8,128)(2,1)}, u32[]{:S(2)}, u32[]{:S(2)}) collective-permute-start(bf16[2,128,512]{2,1,0:T(8,128)(2,1)S(1)} %get-tuple-element.18), channel_id=1, source_target_pairs={{0,8},{8,0},{16,24},{24,16},{1,9},{9,1},{17,25},{25,17},{2,10},{10... | collective-permute-start | bytes 786440 | tf_op jit(solution)/shard_map/ppermute | solution.py:22
  13.9 3.7 %shard_map.47 = (bf16[2,128,512]{2,1,0:T(8,128)(2,1)S(1)}, bf16[2,128,512]{2,1,0:T(8,128)(2,1)S(1)}, bf16[2,128,512]{2,1,0:T(8,128)(2,1)S(1)}, bf16[2,128,512]{2,1,0:T(8,128)(2,1)S(1)}) custom-call(s32[4]{0:T(128)S(1)} %copy-done.2, s32[3]{0:T(128)S(1)} %copy-done.3, bf16[2,1,1024,512]{3,2,1,0:T(8,128)(2,1)S(1)} %copy-done.1, ...), custom_call_target="tpu_custom_call" | custom-call | flops 2147483648 | bytes 5242880 | tf_op jit(solution)/shard_map/pallas_call | solution.py:78
  18.3 3.7 %shard_map.48 = (bf16[2,128,512]{2,1,0:T(8,128)(2,1)S(1)}, bf16[2,128,512]{2,1,0:T(8,128)(2,1)S(1)}, bf16[2,128,512]{2,1,0:T(8,128)(2,1)S(1)}, bf16[2,128,512]{2,1,0:T(8,128)(2,1)S(1)}) custom-call(s32[4]{0:T(128)S(1)} %copy-done.2, s32[3]{0:T(128)S(1)} %copy-done.3, bf16[2,1,1024,512]{3,2,1,0:T(8,128)(2,1)S(1)} %copy-done.1, ...), custom_call_target="tpu_custom_call" | custom-call | flops 2147483648 | bytes 5242880 | tf_op jit(solution)/shard_map/pallas_call | solution.py:78
  22.0 2.0 %collective-permute-start.8 = (bf16[2,128,512]{2,1,0:T(8,128)(2,1)S(1)}, bf16[2,128,512]{2,1,0:T(8,128)(2,1)S(1)}, u32[]{:S(2)}, u32[]{:S(2)}) collective-permute-start(bf16[2,128,512]{2,1,0:T(8,128)(2,1)S(1)} %get-tuple-element.26), channel_id=1, source_target_pairs={{0,8},{8,0},{16,24},{24,16},{1,9},{9,1},{17,25},{25,17},{2,10},{10... | collective-permute-start | bytes 786440 | tf_op jit(solution)/shard_map/ppermute | solution.py:22
  23.9 1.6 %collective-permute-start.10 = (bf16[2,128,512]{2,1,0:T(8,128)(2,1)S(1)}, bf16[2,128,512]{2,1,0:T(8,128)(2,1)S(1)}, u32[]{:S(2)}, u32[]{:S(2)}) collective-permute-start(bf16[2,128,512]{2,1,0:T(8,128)(2,1)S(1)} %get-tuple-element.28), channel_id=1, source_target_pairs={{0,16},{8,24},{16,0},{24,8},{1,17},{9,25},{17,1},{25,9},{2,18},{10... | collective-permute-start | bytes 786440 | tf_op jit(solution)/shard_map/ppermute | solution.py:22
  25.5 1.0 add_convert_fusion.4
  27.1 1.0 add_convert_fusion.5
  28.3 1.0 add_convert_fusion.2
  29.4 2.0 %collective-permute-start.7 = (bf16[1,128,512]{2,1,0:T(8,128)(2,1)S(1)}, bf16[1,128,512]{2,1,0:T(8,128)(2,1)S(1)}, u32[]{:S(2)}, u32[]{:S(2)}) collective-permute-start(bf16[1,128,512]{2,1,0:T(8,128)(2,1)S(1)} %slice.113), channel_id=1, source_target_pairs={{0,8},{8,0},{16,24},{24,16},{1,9},{9,1},{17,25},{25,17},{2,10},{10... | collective-permute-start | bytes 393224 | tf_op jit(solution)/shard_map/ppermute | solution.py:22
  31.3 1.0 add_convert_fusion.3
  33.0 1.2 collective-permute-start.5
  35.8 1.4 %collective-permute-start.11 = (bf16[1,128,512]{2,1,0:T(8,128)(2,1)S(1)}, bf16[1,128,512]{2,1,0:T(8,128)(2,1)S(1)}, u32[]{:S(2)}, u32[]{:S(2)}) collective-permute-start(bf16[1,128,512]{2,1,0:T(8,128)(2,1)S(1)} %slice.117), channel_id=1, source_target_pairs={{0,8},{8,0},{16,24},{24,16},{1,9},{9,1},{17,25},{25,17},{2,10},{10... | collective-permute-start | bytes 393224 | tf_op jit(solution)/shard_map/ppermute | solution.py:22
  37.3 1.6 %collective-permute-start.24 = (bf16[2,128,512]{2,1,0:T(8,128)(2,1)S(1)}, bf16[2,128,512]{2,1,0:T(8,128)(2,1)S(1)}, u32[]{:S(2)}, u32[]{:S(2)}) collective-permute-start(bf16[2,128,512]{2,1,0:T(8,128)(2,1)S(1)} %pad_maximum_fusion.2), channel_id=1, source_target_pairs={{0,2},{1,3},{2,4},{3,5},{4,6},{5,7},{6,0},{7,1},{8,10},{9,11},{10,... | collective-permute-start | bytes 786440 | tf_op jit(solution)/shard_map/ppermute | solution.py:17
  39.0 1.6 %collective-permute-start.18 = (bf16[2,128,512]{2,1,0:T(8,128)(2,1)S(1)}, bf16[2,128,512]{2,1,0:T(8,128)(2,1)S(1)}, u32[]{:S(2)}, u32[]{:S(2)}) collective-permute-start(bf16[2,128,512]{2,1,0:T(8,128)(2,1)S(1)} %pad_maximum_fusion.3), channel_id=1, source_target_pairs={{0,2},{1,3},{2,4},{3,5},{4,6},{5,7},{6,0},{7,1},{8,10},{9,11},{10,... | collective-permute-start | bytes 786440 | tf_op jit(solution)/shard_map/ppermute | solution.py:17
  40.8 1.6 %collective-permute-start.12 = (bf16[2,128,512]{2,1,0:T(8,128)(2,1)S(1)}, bf16[2,128,512]{2,1,0:T(8,128)(2,1)S(1)}, u32[]{:S(2)}, u32[]{:S(2)}) collective-permute-start(bf16[2,128,512]{2,1,0:T(8,128)(2,1)S(1)} %pad_maximum_fusion.4), channel_id=1, source_target_pairs={{0,2},{1,3},{2,4},{3,5},{4,6},{5,7},{6,0},{7,1},{8,10},{9,11},{10,... | collective-permute-start | bytes 786440 | tf_op jit(solution)/shard_map/ppermute | solution.py:17
  42.4 5.9 %collective-permute-done.24.refs_2_ = bf16[2,128,512]{2,1,0:T(8,128)(2,1)S(1)} collective-permute-done((bf16[2,128,512]{2,1,0:T(8,128)(2,1)S(1)}, bf16[2,128,512]{2,1,0:T(8,128)(2,1)S(1)}, u32[]{:S(2)}, u32[]{:S(2)}) %collective-permute-start.24) | collective-permute-done | bytes 262176 | tf_op jit(solution)/shard_map/ppermute | solution.py:17
  48.4 4.5 %collective-permute-done.18.refs_2_ = bf16[2,128,512]{2,1,0:T(8,128)(2,1)S(1)} collective-permute-done((bf16[2,128,512]{2,1,0:T(8,128)(2,1)S(1)}, bf16[2,128,512]{2,1,0:T(8,128)(2,1)S(1)}, u32[]{:S(2)}, u32[]{:S(2)}) %collective-permute-start.18) | collective-permute-done | bytes 262176 | tf_op jit(solution)/shard_map/ppermute | solution.py:17
  52.9 2.8 %collective-permute-done.12.refs_2_ = bf16[2,128,512]{2,1,0:T(8,128)(2,1)S(1)} collective-permute-done((bf16[2,128,512]{2,1,0:T(8,128)(2,1)S(1)}, bf16[2,128,512]{2,1,0:T(8,128)(2,1)S(1)}, u32[]{:S(2)}, u32[]{:S(2)}) %collective-permute-start.12) | collective-permute-done | bytes 262176 | tf_op jit(solution)/shard_map/ppermute | solution.py:17
  56.5 1.0 collective-permute-start.51
  58.0 5.0 %collective-permute-done.49.refs_3_ = bf16[2,128,512]{2,1,0:T(8,128)(2,1)S(1)} collective-permute-done((bf16[2,128,512]{2,1,0:T(8,128)(2,1)S(1)}, bf16[2,128,512]{2,1,0:T(8,128)(2,1)S(1)}, u32[]{:S(2)}, u32[]{:S(2)}) %collective-permute-start.49) | collective-permute-done | bytes 262176 | tf_op jit(solution)/shard_map/ppermute | solution.py:22
  63.0 0.9 collective-permute-start.42
  64.0 6.8 %collective-permute-done.40.refs_3_ = bf16[2,128,512]{2,1,0:T(8,128)(2,1)S(1)} collective-permute-done((bf16[2,128,512]{2,1,0:T(8,128)(2,1)S(1)}, bf16[2,128,512]{2,1,0:T(8,128)(2,1)S(1)}, u32[]{:S(2)}, u32[]{:S(2)}) %collective-permute-start.40) | collective-permute-done | bytes 262176 | tf_op jit(solution)/shard_map/ppermute | solution.py:22
  70.9 7.7 %collective-permute-done.31.refs_3_ = bf16[2,128,512]{2,1,0:T(8,128)(2,1)S(1)} collective-permute-done((bf16[2,128,512]{2,1,0:T(8,128)(2,1)S(1)}, bf16[2,128,512]{2,1,0:T(8,128)(2,1)S(1)}, u32[]{:S(2)}, u32[]{:S(2)}) %collective-permute-start.31) | collective-permute-done | bytes 262176 | tf_op jit(solution)/shard_map/ppermute | solution.py:22
  78.7 1.4 %collective-permute-start.55 = (bf16[128,512]{1,0:T(8,128)(2,1)S(1)}, bf16[128,512]{1,0:T(8,128)(2,1)S(1)}, u32[]{:S(2)}, u32[]{:S(2)}) collective-permute-start(bf16[128,512]{1,0:T(8,128)(2,1)S(1)} %slice_bitcast_fusion), channel_id=1, source_target_pairs={{0,8},{8,0},{16,24},{24,16},{1,9},{9,1},{17,25},{25,17},{2,10},{10... | collective-permute-start | bytes 393224 | tf_op jit(solution)/shard_map/ppermute | solution.py:22
  80.8 2.8 %collective-permute-done.53.refs_5_ = bf16[128,512]{1,0:T(8,128)(2,1)S(1)} collective-permute-done((bf16[128,512]{1,0:T(8,128)(2,1)S(1)}, bf16[128,512]{1,0:T(8,128)(2,1)S(1)}, u32[]{:S(2)}, u32[]{:S(2)}) %collective-permute-start.53) | collective-permute-done | bytes 131104 | tf_op jit(solution)/shard_map/ppermute | solution.py:22
  83.7 2.0 %collective-permute-start.27 = (bf16[2,128,512]{2,1,0:T(8,128)(2,1)S(1)}, bf16[2,128,512]{2,1,0:T(8,128)(2,1)S(1)}, u32[]{:S(2)}, u32[]{:S(2)}) collective-permute-start(bf16[2,128,512]{2,1,0:T(8,128)(2,1)S(1)} %collective-permute-done.25.refs_2_), channel_id=1, source_target_pairs={{0,16},{8,24},{16,0},{24,8},{1,17},{9,25},{17,1},{25,9},{2,18},{10... | collective-permute-start | bytes 786440 | tf_op jit(solution)/shard_map/ppermute | solution.py:22
  85.7 1.7 %shard_map.49.refs_7_ = bf16[3,3,3,2,1,128,512]{6,5,4,3,2,1,0:T(8,128)(2,1)} custom-call(bf16[384,512]{1,0:T(8,128)(2,1)S(1)} %bitcast.41, bf16[384,512]{1,0:T(8,128)(2,1)S(1)} %bitcast.32, bf16[2,128,512]{2,1,0:T(8,128)(2,1)S(1)} %collective-permute-done.24.refs_2_, bf16[2,128,512]{2,1,0:T(8,128)(2,1)S(1)} %collective-permute-done.49.refs_3_, ...), custom_call_target="tpu_custom_call" | custom-call | flops 805306368 | bytes 2621440 | tf_op jit(solution)/shard_map/pallas_call | solution.py:171
  87.9 4.5 %collective-permute-done.27.refs_4_ = bf16[2,128,512]{2,1,0:T(8,128)(2,1)S(1)} collective-permute-done((bf16[2,128,512]{2,1,0:T(8,128)(2,1)S(1)}, bf16[2,128,512]{2,1,0:T(8,128)(2,1)S(1)}, u32[]{:S(2)}, u32[]{:S(2)}) %collective-permute-start.27) | collective-permute-done | bytes 262176 | tf_op jit(solution)/shard_map/ppermute | solution.py:22
  92.6 1.8 %collective-permute-start.44 = (bf16[128,512]{1,0:T(8,128)(2,1)S(1)}, bf16[128,512]{1,0:T(8,128)(2,1)S(1)}, u32[]{:S(2)}, u32[]{:S(2)}) collective-permute-start(bf16[128,512]{1,0:T(8,128)(2,1)S(1)} %slice_bitcast_fusion.3), channel_id=1, source_target_pairs={{0,16},{8,24},{16,0},{24,8},{1,17},{9,25},{17,1},{25,9},{2,18},{10... | collective-permute-start | bytes 393224 | tf_op jit(solution)/shard_map/ppermute | solution.py:22
  94.8 1.7 %collective-permute-done.20.refs_3_ = bf16[2,128,512]{2,1,0:T(8,128)(2,1)S(1)} collective-permute-done((bf16[2,128,512]{2,1,0:T(8,128)(2,1)S(1)}, bf16[2,128,512]{2,1,0:T(8,128)(2,1)S(1)}, u32[]{:S(2)}, u32[]{:S(2)}) %collective-permute-start.20) | collective-permute-done | bytes 262176 | tf_op jit(solution)/shard_map/ppermute | solution.py:22
  96.8 7.5 %collective-permute-done.44.refs_5_ = bf16[128,512]{1,0:T(8,128)(2,1)S(1)} collective-permute-done((bf16[128,512]{1,0:T(8,128)(2,1)S(1)}, bf16[128,512]{1,0:T(8,128)(2,1)S(1)}, u32[]{:S(2)}, u32[]{:S(2)}) %collective-permute-start.44) | collective-permute-done | bytes 131104 | tf_op jit(solution)/shard_map/ppermute | solution.py:22
  104.6 2.5 %collective-permute-done.35.refs_5_ = bf16[128,512]{1,0:T(8,128)(2,1)S(1)} collective-permute-done((bf16[128,512]{1,0:T(8,128)(2,1)S(1)}, bf16[128,512]{1,0:T(8,128)(2,1)S(1)}, u32[]{:S(2)}, u32[]{:S(2)}) %collective-permute-start.35) | collective-permute-done | bytes 131104 | tf_op jit(solution)/shard_map/ppermute | solution.py:22
  107.7 1.6 %collective-permute-done.37.refs_6_ = bf16[128,512]{1,0:T(8,128)(2,1)S(1)} collective-permute-done((bf16[128,512]{1,0:T(8,128)(2,1)S(1)}, bf16[128,512]{1,0:T(8,128)(2,1)S(1)}, u32[]{:S(2)}, u32[]{:S(2)}) %collective-permute-start.37) | collective-permute-done | bytes 131104 | tf_op jit(solution)/shard_map/ppermute | solution.py:22
  110.3 1.1 collective-permute-done.45.refs_5_
  112.7 1.7 %shard_map.50.refs_7_ = bf16[3,3,3,2,1,128,512]{6,5,4,3,2,1,0:T(8,128)(2,1)} custom-call(bf16[384,512]{1,0:T(8,128)(2,1)S(1)} %bitcast.42, bf16[384,512]{1,0:T(8,128)(2,1)S(1)} %bitcast.33, bf16[2,128,512]{2,1,0:T(8,128)(2,1)S(1)} %collective-permute-done.48.refs_2_, ...), custom_call_target="tpu_custom_call", output_to_operand_aliasing={{}: (7, {})} | custom-call | flops 805306368 | bytes 2621440 | tf_op jit(solution)/shard_map/pallas_call | solution.py:171
  114.8 1.7 %shard_map.51.refs_7_ = bf16[3,3,3,2,1,128,512]{6,5,4,3,2,1,0:T(8,128)(2,1)} custom-call(bf16[384,512]{1,0:T(8,128)(2,1)S(1)} %bitcast.43, bf16[384,512]{1,0:T(8,128)(2,1)S(1)} %bitcast.34, bf16[2,128,512]{2,1,0:T(8,128)(2,1)S(1)} %collective-permute-done.18.refs_2_, ...), custom_call_target="tpu_custom_call", output_to_operand_aliasing={{}: (7, {})} | custom-call | flops 805306368 | bytes 2621440 | tf_op jit(solution)/shard_map/pallas_call | solution.py:171
  116.9 1.7 %shard_map.52.refs_7_ = bf16[3,3,3,2,1,128,512]{6,5,4,3,2,1,0:T(8,128)(2,1)} custom-call(bf16[384,512]{1,0:T(8,128)(2,1)S(1)} %bitcast.44, bf16[384,512]{1,0:T(8,128)(2,1)S(1)} %bitcast.35, bf16[2,128,512]{2,1,0:T(8,128)(2,1)S(1)} %collective-permute-done.39.refs_2_, ...), custom_call_target="tpu_custom_call", output_to_operand_aliasing={{}: (7, {})} | custom-call | flops 805306368 | bytes 2621440 | tf_op jit(solution)/shard_map/pallas_call | solution.py:171
  119.7 1.7 %shard_map.53.refs_7_ = bf16[3,3,3,2,1,128,512]{6,5,4,3,2,1,0:T(8,128)(2,1)} custom-call(bf16[384,512]{1,0:T(8,128)(2,1)S(1)} %bitcast.45, bf16[384,512]{1,0:T(8,128)(2,1)S(1)} %bitcast.36, bf16[2,128,512]{2,1,0:T(8,128)(2,1)S(1)} %collective-permute-done.12.refs_2_, ...), custom_call_target="tpu_custom_call", output_to_operand_aliasing={{}: (7, {})} | custom-call | flops 805306368 | bytes 2621440 | tf_op jit(solution)/shard_map/pallas_call | solution.py:171
  121.5 1.8 %collective-permute-start.22 = (bf16[128,512]{1,0:T(8,128)(2,1)S(1)}, bf16[128,512]{1,0:T(8,128)(2,1)S(1)}, u32[]{:S(2)}, u32[]{:S(2)}) collective-permute-start(bf16[128,512]{1,0:T(8,128)(2,1)S(1)} %slice_bitcast_fusion.9), channel_id=1, source_target_pairs={{0,16},{8,24},{16,0},{24,8},{1,17},{9,25},{17,1},{25,9},{2,18},{10... | collective-permute-start | bytes 393224 | tf_op jit(solution)/shard_map/ppermute | solution.py:22
  123.3 1.3 collective-permute-start.23
  124.9 1.7 %shard_map.54.refs_7_ = bf16[3,3,3,2,1,128,512]{6,5,4,3,2,1,0:T(8,128)(2,1)} custom-call(bf16[384,512]{1,0:T(8,128)(2,1)S(1)} %bitcast.46, bf16[384,512]{1,0:T(8,128)(2,1)S(1)} %bitcast.37, bf16[2,128,512]{2,1,0:T(8,128)(2,1)S(1)} %collective-permute-done.30.refs_2_, ...), custom_call_target="tpu_custom_call", output_to_operand_aliasing={{}: (7, {})} | custom-call | flops 805306368 | bytes 2621440 | tf_op jit(solution)/shard_map/pallas_call | solution.py:171
  127.4 1.7 %shard_map.55.refs_7_ = bf16[3,3,3,2,1,128,512]{6,5,4,3,2,1,0:T(8,128)(2,1)} custom-call(bf16[384,512]{1,0:T(8,128)(2,1)S(1)} %bitcast.47, bf16[384,512]{1,0:T(8,128)(2,1)S(1)} %bitcast.38, bf16[2,128,512]{2,1,0:T(8,128)(2,1)S(1)} %collective-permute-done.25.refs_2_, ...), custom_call_target="tpu_custom_call", output_to_operand_aliasing={{}: (7, {})} | custom-call | flops 805306368 | bytes 2621440 | tf_op jit(solution)/shard_map/pallas_call | solution.py:171
  129.2 1.7 %shard_map.56.refs_7_ = bf16[3,3,3,2,1,128,512]{6,5,4,3,2,1,0:T(8,128)(2,1)} custom-call(bf16[384,512]{1,0:T(8,128)(2,1)S(1)} %bitcast.48, bf16[384,512]{1,0:T(8,128)(2,1)S(1)} %bitcast.39, bf16[2,128,512]{2,1,0:T(8,128)(2,1)S(1)} %collective-permute-done.19.refs_2_, ...), custom_call_target="tpu_custom_call", output_to_operand_aliasing={{}: (7, {})} | custom-call | flops 805306368 | bytes 2621440 | tf_op jit(solution)/shard_map/pallas_call | solution.py:171
  131.7 1.7 %shard_map.57 = bf16[3,3,3,2,1,128,512]{6,5,4,3,2,1,0:T(8,128)(2,1)} custom-call(bf16[384,512]{1,0:T(8,128)(2,1)S(1)} %bitcast.49, bf16[384,512]{1,0:T(8,128)(2,1)S(1)} %bitcast.40, bf16[2,128,512]{2,1,0:T(8,128)(2,1)S(1)} %collective-permute-done.13.refs_2_, ...), custom_call_target="tpu_custom_call", output_to_operand_aliasing={{}: (7, {})} | custom-call | flops 805306368 | bytes 2621440 | tf_op jit(solution)/shard_map/pallas_call | solution.py:171
  (126 shorter events, 15.5 us)
Async XLA Ops:
  9.4 14.6 %collective-permute-start.2 = (bf16[2,128,512]{2,1,0:T(8,128)(2,1)S(1)}, bf16[2,128,512]{2,1,0:T(8,128)(2,1)}, u32[]{:S(2)}, u32[]{:S(2)}) collective-permute-start(bf16[2,128,512]{2,1,0:T(8,128)(2,1)S(1)} %get-tuple-element.20), channel_id=1, source_target_pairs={{0,16},{8,24},{16,0},{24,8},{1,17},{9,25},{17,1},{25,9},{2,18},{10... | collective-permute-start | bytes 786440 | tf_op jit(solution)/shard_map/ppermute | solution.py:22
  12.4 14.1 %collective-permute-start = (bf16[2,128,512]{2,1,0:T(8,128)(2,1)S(1)}, bf16[2,128,512]{2,1,0:T(8,128)(2,1)}, u32[]{:S(2)}, u32[]{:S(2)}) collective-permute-start(bf16[2,128,512]{2,1,0:T(8,128)(2,1)S(1)} %get-tuple-element.18), channel_id=1, source_target_pairs={{0,8},{8,0},{16,24},{24,16},{1,9},{9,1},{17,25},{25,17},{2,10},{10... | collective-permute-start | bytes 786440 | tf_op jit(solution)/shard_map/ppermute | solution.py:22
  17.6 10.5 %collective-permute-start.6 = (bf16[2,128,512]{2,1,0:T(8,128)(2,1)S(1)}, bf16[2,128,512]{2,1,0:T(8,128)(2,1)}, u32[]{:S(2)}, u32[]{:S(2)}) collective-permute-start(bf16[2,128,512]{2,1,0:T(8,128)(2,1)S(1)} %get-tuple-element.24), channel_id=1, source_target_pairs={{0,16},{8,24},{16,0},{24,8},{1,17},{9,25},{17,1},{25,9},{2,18},{10... | collective-permute-start | bytes 786440 | tf_op jit(solution)/shard_map/ppermute | solution.py:22
  18.2 11.2 %collective-permute-start.4 = (bf16[2,128,512]{2,1,0:T(8,128)(2,1)S(1)}, bf16[2,128,512]{2,1,0:T(8,128)(2,1)}, u32[]{:S(2)}, u32[]{:S(2)}) collective-permute-start(bf16[2,128,512]{2,1,0:T(8,128)(2,1)S(1)} %get-tuple-element.22), channel_id=1, source_target_pairs={{0,8},{8,0},{16,24},{24,16},{1,9},{9,1},{17,25},{25,17},{2,10},{10... | collective-permute-start | bytes 786440 | tf_op jit(solution)/shard_map/ppermute | solution.py:22
  22.0 11.0 %collective-permute-start.8 = (bf16[2,128,512]{2,1,0:T(8,128)(2,1)S(1)}, bf16[2,128,512]{2,1,0:T(8,128)(2,1)S(1)}, u32[]{:S(2)}, u32[]{:S(2)}) collective-permute-start(bf16[2,128,512]{2,1,0:T(8,128)(2,1)S(1)} %get-tuple-element.26), channel_id=1, source_target_pairs={{0,8},{8,0},{16,24},{24,16},{1,9},{9,1},{17,25},{25,17},{2,10},{10... | collective-permute-start | bytes 786440 | tf_op jit(solution)/shard_map/ppermute | solution.py:22
  23.9 10.3 %collective-permute-start.10 = (bf16[2,128,512]{2,1,0:T(8,128)(2,1)S(1)}, bf16[2,128,512]{2,1,0:T(8,128)(2,1)S(1)}, u32[]{:S(2)}, u32[]{:S(2)}) collective-permute-start(bf16[2,128,512]{2,1,0:T(8,128)(2,1)S(1)} %get-tuple-element.28), channel_id=1, source_target_pairs={{0,16},{8,24},{16,0},{24,8},{1,17},{9,25},{17,1},{25,9},{2,18},{10... | collective-permute-start | bytes 786440 | tf_op jit(solution)/shard_map/ppermute | solution.py:22
  26.5 9.2 %collective-permute-start.3 = (bf16[1,128,512]{2,1,0:T(8,128)(2,1)S(1)}, bf16[1,128,512]{2,1,0:T(8,128)(2,1)S(1)}, u32[]{:S(2)}, u32[]{:S(2)}) collective-permute-start(bf16[1,128,512]{2,1,0:T(8,128)(2,1)S(1)} %slice.109), channel_id=1, source_target_pairs={{0,8},{8,0},{16,24},{24,16},{1,9},{9,1},{17,25},{25,17},{2,10},{10... | collective-permute-start | bytes 393224 | tf_op jit(solution)/shard_map/ppermute | solution.py:22
  28.1 9.1 %collective-permute-start.1 = (bf16[1,128,512]{2,1,0:T(8,128)(2,1)S(1)}, bf16[1,128,512]{2,1,0:T(8,128)(2,1)S(1)}, u32[]{:S(2)}, u32[]{:S(2)}) collective-permute-start(bf16[1,128,512]{2,1,0:T(8,128)(2,1)S(1)} %slice.107), channel_id=1, source_target_pairs={{0,16},{8,24},{16,0},{24,8},{1,17},{9,25},{17,1},{25,9},{2,18},{10... | collective-permute-start | bytes 393224 | tf_op jit(solution)/shard_map/ppermute | solution.py:22
  29.4 9.5 %collective-permute-start.7 = (bf16[1,128,512]{2,1,0:T(8,128)(2,1)S(1)}, bf16[1,128,512]{2,1,0:T(8,128)(2,1)S(1)}, u32[]{:S(2)}, u32[]{:S(2)}) collective-permute-start(bf16[1,128,512]{2,1,0:T(8,128)(2,1)S(1)} %slice.113), channel_id=1, source_target_pairs={{0,8},{8,0},{16,24},{24,16},{1,9},{9,1},{17,25},{25,17},{2,10},{10... | collective-permute-start | bytes 393224 | tf_op jit(solution)/shard_map/ppermute | solution.py:22
  33.0 6.0 %collective-permute-start.5 = (bf16[1,128,512]{2,1,0:T(8,128)(2,1)S(1)}, bf16[1,128,512]{2,1,0:T(8,128)(2,1)S(1)}, u32[]{:S(2)}, u32[]{:S(2)}) collective-permute-start(bf16[1,128,512]{2,1,0:T(8,128)(2,1)S(1)} %slice.111), channel_id=1, source_target_pairs={{0,16},{8,24},{16,0},{24,8},{1,17},{9,25},{17,1},{25,9},{2,18},{10... | collective-permute-start | bytes 393224 | tf_op jit(solution)/shard_map/ppermute | solution.py:22
  34.3 6.4 %collective-permute-start.9 = (bf16[1,128,512]{2,1,0:T(8,128)(2,1)S(1)}, bf16[1,128,512]{2,1,0:T(8,128)(2,1)S(1)}, u32[]{:S(2)}, u32[]{:S(2)}) collective-permute-start(bf16[1,128,512]{2,1,0:T(8,128)(2,1)S(1)} %slice.115), channel_id=1, source_target_pairs={{0,16},{8,24},{16,0},{24,8},{1,17},{9,25},{17,1},{25,9},{2,18},{10... | collective-permute-start | bytes 393224 | tf_op jit(solution)/shard_map/ppermute | solution.py:22
  35.8 5.0 %collective-permute-start.11 = (bf16[1,128,512]{2,1,0:T(8,128)(2,1)S(1)}, bf16[1,128,512]{2,1,0:T(8,128)(2,1)S(1)}, u32[]{:S(2)}, u32[]{:S(2)}) collective-permute-start(bf16[1,128,512]{2,1,0:T(8,128)(2,1)S(1)} %slice.117), channel_id=1, source_target_pairs={{0,8},{8,0},{16,24},{24,16},{1,9},{9,1},{17,25},{25,17},{2,10},{10... | collective-permute-start | bytes 393224 | tf_op jit(solution)/shard_map/ppermute | solution.py:22
  37.3 11.0 %collective-permute-start.24 = (bf16[2,128,512]{2,1,0:T(8,128)(2,1)S(1)}, bf16[2,128,512]{2,1,0:T(8,128)(2,1)S(1)}, u32[]{:S(2)}, u32[]{:S(2)}) collective-permute-start(bf16[2,128,512]{2,1,0:T(8,128)(2,1)S(1)} %pad_maximum_fusion.2), channel_id=1, source_target_pairs={{0,2},{1,3},{2,4},{3,5},{4,6},{5,7},{6,0},{7,1},{8,10},{9,11},{10,... | collective-permute-start | bytes 786440 | tf_op jit(solution)/shard_map/ppermute | solution.py:17
  39.0 13.8 %collective-permute-start.18 = (bf16[2,128,512]{2,1,0:T(8,128)(2,1)S(1)}, bf16[2,128,512]{2,1,0:T(8,128)(2,1)S(1)}, u32[]{:S(2)}, u32[]{:S(2)}) collective-permute-start(bf16[2,128,512]{2,1,0:T(8,128)(2,1)S(1)} %pad_maximum_fusion.3), channel_id=1, source_target_pairs={{0,2},{1,3},{2,4},{3,5},{4,6},{5,7},{6,0},{7,1},{8,10},{9,11},{10,... | collective-permute-start | bytes 786440 | tf_op jit(solution)/shard_map/ppermute | solution.py:17
  40.8 14.9 %collective-permute-start.12 = (bf16[2,128,512]{2,1,0:T(8,128)(2,1)S(1)}, bf16[2,128,512]{2,1,0:T(8,128)(2,1)S(1)}, u32[]{:S(2)}, u32[]{:S(2)}) collective-permute-start(bf16[2,128,512]{2,1,0:T(8,128)(2,1)S(1)} %pad_maximum_fusion.4), channel_id=1, source_target_pairs={{0,2},{1,3},{2,4},{3,5},{4,6},{5,7},{6,0},{7,1},{8,10},{9,11},{10,... | collective-permute-start | bytes 786440 | tf_op jit(solution)/shard_map/ppermute | solution.py:17
  56.0 7.0 %collective-permute-start.49 = (bf16[2,128,512]{2,1,0:T(8,128)(2,1)S(1)}, bf16[2,128,512]{2,1,0:T(8,128)(2,1)S(1)}, u32[]{:S(2)}, u32[]{:S(2)}) collective-permute-start(bf16[2,128,512]{2,1,0:T(8,128)(2,1)S(1)} %collective-permute-done.24.refs_2_), channel_id=1, source_target_pairs={{0,8},{8,0},{16,24},{24,16},{1,9},{9,1},{17,25},{25,17},{2,10},{10... | collective-permute-start | bytes 786440 | tf_op jit(solution)/shard_map/ppermute | solution.py:22
  56.5 6.5 %collective-permute-start.51 = (bf16[2,128,512]{2,1,0:T(8,128)(2,1)S(1)}, bf16[2,128,512]{2,1,0:T(8,128)(2,1)S(1)}, u32[]{:S(2)}, u32[]{:S(2)}) collective-permute-start(bf16[2,128,512]{2,1,0:T(8,128)(2,1)S(1)} %collective-permute-done.24.refs_2_), channel_id=1, source_target_pairs={{0,16},{8,24},{16,0},{24,8},{1,17},{9,25},{17,1},{25,9},{2,18},{10... | collective-permute-start | bytes 786440 | tf_op jit(solution)/shard_map/ppermute | solution.py:22
  57.6 22.4 %collective-permute-start.25 = (bf16[2,128,512]{2,1,0:T(8,128)(2,1)S(1)}, bf16[2,128,512]{2,1,0:T(8,128)(2,1)S(1)}, u32[]{:S(2)}, u32[]{:S(2)}) collective-permute-start(bf16[2,128,512]{2,1,0:T(8,128)(2,1)S(1)} %get-tuple-element.35), channel_id=1, source_target_pairs={{0,1},{1,2},{2,3},{3,4},{4,5},{5,6},{6,7},{7,0},{8,9},{9,10},{10,1... | collective-permute-start | bytes 786440 | tf_op jit(solution)/shard_map/ppermute | solution.py:17
  57.7 29.8 %collective-permute-start.19 = (bf16[2,128,512]{2,1,0:T(8,128)(2,1)S(1)}, bf16[2,128,512]{2,1,0:T(8,128)(2,1)S(1)}, u32[]{:S(2)}, u32[]{:S(2)}) collective-permute-start(bf16[2,128,512]{2,1,0:T(8,128)(2,1)S(1)} %get-tuple-element.37), channel_id=1, source_target_pairs={{0,1},{1,2},{2,3},{3,4},{4,5},{5,6},{6,7},{7,0},{8,9},{9,10},{10,1... | collective-permute-start | bytes 786440 | tf_op jit(solution)/shard_map/ppermute | solution.py:17
  57.8 36.7 %collective-permute-start.13 = (bf16[2,128,512]{2,1,0:T(8,128)(2,1)S(1)}, bf16[2,128,512]{2,1,0:T(8,128)(2,1)S(1)}, u32[]{:S(2)}, u32[]{:S(2)}) collective-permute-start(bf16[2,128,512]{2,1,0:T(8,128)(2,1)S(1)} %get-tuple-element.39), channel_id=1, source_target_pairs={{0,1},{1,2},{2,3},{3,4},{4,5},{5,6},{6,7},{7,0},{8,9},{9,10},{10,1... | collective-permute-start | bytes 786440 | tf_op jit(solution)/shard_map/ppermute | solution.py:17
  63.0 7.8 %collective-permute-start.40 = (bf16[2,128,512]{2,1,0:T(8,128)(2,1)S(1)}, bf16[2,128,512]{2,1,0:T(8,128)(2,1)S(1)}, u32[]{:S(2)}, u32[]{:S(2)}) collective-permute-start(bf16[2,128,512]{2,1,0:T(8,128)(2,1)S(1)} %collective-permute-done.18.refs_2_), channel_id=1, source_target_pairs={{0,8},{8,0},{16,24},{24,16},{1,9},{9,1},{17,25},{25,17},{2,10},{10... | collective-permute-start | bytes 786440 | tf_op jit(solution)/shard_map/ppermute | solution.py:22
  63.0 7.8 %collective-permute-start.42 = (bf16[2,128,512]{2,1,0:T(8,128)(2,1)S(1)}, bf16[2,128,512]{2,1,0:T(8,128)(2,1)S(1)}, u32[]{:S(2)}, u32[]{:S(2)}) collective-permute-start(bf16[2,128,512]{2,1,0:T(8,128)(2,1)S(1)} %collective-permute-done.18.refs_2_), channel_id=1, source_target_pairs={{0,16},{8,24},{16,0},{24,8},{1,17},{9,25},{17,1},{25,9},{2,18},{10... | collective-permute-start | bytes 786440 | tf_op jit(solution)/shard_map/ppermute | solution.py:22
  70.8 7.8 %collective-permute-start.31 = (bf16[2,128,512]{2,1,0:T(8,128)(2,1)S(1)}, bf16[2,128,512]{2,1,0:T(8,128)(2,1)S(1)}, u32[]{:S(2)}, u32[]{:S(2)}) collective-permute-start(bf16[2,128,512]{2,1,0:T(8,128)(2,1)S(1)} %collective-permute-done.12.refs_2_), channel_id=1, source_target_pairs={{0,8},{8,0},{16,24},{24,16},{1,9},{9,1},{17,25},{25,17},{2,10},{10... | collective-permute-start | bytes 786440 | tf_op jit(solution)/shard_map/ppermute | solution.py:22
  70.8 7.8 %collective-permute-start.33 = (bf16[2,128,512]{2,1,0:T(8,128)(2,1)S(1)}, bf16[2,128,512]{2,1,0:T(8,128)(2,1)S(1)}, u32[]{:S(2)}, u32[]{:S(2)}) collective-permute-start(bf16[2,128,512]{2,1,0:T(8,128)(2,1)S(1)} %collective-permute-done.12.refs_2_), channel_id=1, source_target_pairs={{0,16},{8,24},{16,0},{24,8},{1,17},{9,25},{17,1},{25,9},{2,18},{10... | collective-permute-start | bytes 786440 | tf_op jit(solution)/shard_map/ppermute | solution.py:22
  78.6 5.0 %collective-permute-start.53 = (bf16[128,512]{1,0:T(8,128)(2,1)S(1)}, bf16[128,512]{1,0:T(8,128)(2,1)S(1)}, u32[]{:S(2)}, u32[]{:S(2)}) collective-permute-start(bf16[128,512]{1,0:T(8,128)(2,1)S(1)} %slice_bitcast_fusion.1), channel_id=1, source_target_pairs={{0,16},{8,24},{16,0},{24,8},{1,17},{9,25},{17,1},{25,9},{2,18},{10... | collective-permute-start | bytes 393224 | tf_op jit(solution)/shard_map/ppermute | solution.py:22
  78.7 5.0 %collective-permute-start.55 = (bf16[128,512]{1,0:T(8,128)(2,1)S(1)}, bf16[128,512]{1,0:T(8,128)(2,1)S(1)}, u32[]{:S(2)}, u32[]{:S(2)}) collective-permute-start(bf16[128,512]{1,0:T(8,128)(2,1)S(1)} %slice_bitcast_fusion), channel_id=1, source_target_pairs={{0,8},{8,0},{16,24},{24,16},{1,9},{9,1},{17,25},{25,17},{2,10},{10... | collective-permute-start | bytes 393224 | tf_op jit(solution)/shard_map/ppermute | solution.py:22
  80.1 7.5 %collective-permute-start.26 = (bf16[2,128,512]{2,1,0:T(8,128)(2,1)S(1)}, bf16[2,128,512]{2,1,0:T(8,128)(2,1)S(1)}, u32[]{:S(2)}, u32[]{:S(2)}) collective-permute-start(bf16[2,128,512]{2,1,0:T(8,128)(2,1)S(1)} %collective-permute-done.25.refs_2_), channel_id=1, source_target_pairs={{0,8},{8,0},{16,24},{24,16},{1,9},{9,1},{17,25},{25,17},{2,10},{10... | collective-permute-start | bytes 786440 | tf_op jit(solution)/shard_map/ppermute | solution.py:22
  83.6 9.0 %collective-permute-start.48 = (bf16[2,128,512]{2,1,0:T(8,128)(2,1)S(1)}, bf16[2,128,512]{2,1,0:T(8,128)(2,1)S(1)}, u32[]{:S(2)}, u32[]{:S(2)}) collective-permute-start(bf16[2,128,512]{2,1,0:T(8,128)(2,1)S(1)} %collective-permute-done.24.refs_2_), channel_id=1, source_target_pairs={{0,1},{1,0},{2,3},{3,2},{4,5},{5,4},{6,7},{7,6},{8,9},{9,8},{10,11... | collective-permute-start | bytes 786440 | tf_op jit(solution)/shard_map/ppermute | solution.py:22
  83.7 8.6 %collective-permute-start.27 = (bf16[2,128,512]{2,1,0:T(8,128)(2,1)S(1)}, bf16[2,128,512]{2,1,0:T(8,128)(2,1)S(1)}, u32[]{:S(2)}, u32[]{:S(2)}) collective-permute-start(bf16[2,128,512]{2,1,0:T(8,128)(2,1)S(1)} %collective-permute-done.25.refs_2_), channel_id=1, source_target_pairs={{0,16},{8,24},{16,0},{24,8},{1,17},{9,25},{17,1},{25,9},{2,18},{10... | collective-permute-start | bytes 786440 | tf_op jit(solution)/shard_map/ppermute | solution.py:22
  87.5 7.0 %collective-permute-start.39 = (bf16[2,128,512]{2,1,0:T(8,128)(2,1)S(1)}, bf16[2,128,512]{2,1,0:T(8,128)(2,1)S(1)}, u32[]{:S(2)}, u32[]{:S(2)}) collective-permute-start(bf16[2,128,512]{2,1,0:T(8,128)(2,1)S(1)} %collective-permute-done.18.refs_2_), channel_id=1, source_target_pairs={{0,1},{1,0},{2,3},{3,2},{4,5},{5,4},{6,7},{7,6},{8,9},{9,8},{10,11... | collective-permute-start | bytes 786440 | tf_op jit(solution)/shard_map/ppermute | solution.py:22
  87.6 8.9 %collective-permute-start.20 = (bf16[2,128,512]{2,1,0:T(8,128)(2,1)S(1)}, bf16[2,128,512]{2,1,0:T(8,128)(2,1)S(1)}, u32[]{:S(2)}, u32[]{:S(2)}) collective-permute-start(bf16[2,128,512]{2,1,0:T(8,128)(2,1)S(1)} %collective-permute-done.19.refs_2_), channel_id=1, source_target_pairs={{0,8},{8,0},{16,24},{24,16},{1,9},{9,1},{17,25},{25,17},{2,10},{10... | collective-permute-start | bytes 786440 | tf_op jit(solution)/shard_map/ppermute | solution.py:22
  92.3 14.8 %collective-permute-start.21 = (bf16[2,128,512]{2,1,0:T(8,128)(2,1)S(1)}, bf16[2,128,512]{2,1,0:T(8,128)(2,1)S(1)}, u32[]{:S(2)}, u32[]{:S(2)}) collective-permute-start(bf16[2,128,512]{2,1,0:T(8,128)(2,1)S(1)} %collective-permute-done.19.refs_2_), channel_id=1, source_target_pairs={{0,16},{8,24},{16,0},{24,8},{1,17},{9,25},{17,1},{25,9},{2,18},{10... | collective-permute-start | bytes 786440 | tf_op jit(solution)/shard_map/ppermute | solution.py:22
  92.6 11.7 %collective-permute-start.44 = (bf16[128,512]{1,0:T(8,128)(2,1)S(1)}, bf16[128,512]{1,0:T(8,128)(2,1)S(1)}, u32[]{:S(2)}, u32[]{:S(2)}) collective-permute-start(bf16[128,512]{1,0:T(8,128)(2,1)S(1)} %slice_bitcast_fusion.3), channel_id=1, source_target_pairs={{0,16},{8,24},{16,0},{24,8},{1,17},{9,25},{17,1},{25,9},{2,18},{10... | collective-permute-start | bytes 393224 | tf_op jit(solution)/shard_map/ppermute | solution.py:22
  94.5 9.9 %collective-permute-start.46 = (bf16[128,512]{1,0:T(8,128)(2,1)S(1)}, bf16[128,512]{1,0:T(8,128)(2,1)S(1)}, u32[]{:S(2)}, u32[]{:S(2)}) collective-permute-start(bf16[128,512]{1,0:T(8,128)(2,1)S(1)} %slice_bitcast_fusion.2), channel_id=1, source_target_pairs={{0,8},{8,0},{16,24},{24,16},{1,9},{9,1},{17,25},{25,17},{2,10},{10... | collective-permute-start | bytes 393224 | tf_op jit(solution)/shard_map/ppermute | solution.py:22
  94.5 12.7 %collective-permute-start.35 = (bf16[128,512]{1,0:T(8,128)(2,1)S(1)}, bf16[128,512]{1,0:T(8,128)(2,1)S(1)}, u32[]{:S(2)}, u32[]{:S(2)}) collective-permute-start(bf16[128,512]{1,0:T(8,128)(2,1)S(1)} %slice_bitcast_fusion.5), channel_id=1, source_target_pairs={{0,16},{8,24},{16,0},{24,8},{1,17},{9,25},{17,1},{25,9},{2,18},{10... | collective-permute-start | bytes 393224 | tf_op jit(solution)/shard_map/ppermute | solution.py:22
  96.5 13.4 %collective-permute-start.14 = (bf16[2,128,512]{2,1,0:T(8,128)(2,1)S(1)}, bf16[2,128,512]{2,1,0:T(8,128)(2,1)S(1)}, u32[]{:S(2)}, u32[]{:S(2)}) collective-permute-start(bf16[2,128,512]{2,1,0:T(8,128)(2,1)S(1)} %collective-permute-done.13.refs_2_), channel_id=1, source_target_pairs={{0,8},{8,0},{16,24},{24,16},{1,9},{9,1},{17,25},{25,17},{2,10},{10... | collective-permute-start | bytes 786440 | tf_op jit(solution)/shard_map/ppermute | solution.py:22
  104.3 5.0 %collective-permute-start.37 = (bf16[128,512]{1,0:T(8,128)(2,1)S(1)}, bf16[128,512]{1,0:T(8,128)(2,1)S(1)}, u32[]{:S(2)}, u32[]{:S(2)}) collective-permute-start(bf16[128,512]{1,0:T(8,128)(2,1)S(1)} %slice_bitcast_fusion.4), channel_id=1, source_target_pairs={{0,8},{8,0},{16,24},{24,16},{1,9},{9,1},{17,25},{25,17},{2,10},{10... | collective-permute-start | bytes 393224 | tf_op jit(solution)/shard_map/ppermute | solution.py:22
  104.3 7.6 %collective-permute-start.15 = (bf16[2,128,512]{2,1,0:T(8,128)(2,1)S(1)}, bf16[2,128,512]{2,1,0:T(8,128)(2,1)S(1)}, u32[]{:S(2)}, u32[]{:S(2)}) collective-permute-start(bf16[2,128,512]{2,1,0:T(8,128)(2,1)S(1)} %collective-permute-done.13.refs_2_), channel_id=1, source_target_pairs={{0,16},{8,24},{16,0},{24,8},{1,17},{9,25},{17,1},{25,9},{2,18},{10... | collective-permute-start | bytes 786440 | tf_op jit(solution)/shard_map/ppermute | solution.py:22
  111.4 7.2 %collective-permute-start.30 = (bf16[2,128,512]{2,1,0:T(8,128)(2,1)S(1)}, bf16[2,128,512]{2,1,0:T(8,128)(2,1)S(1)}, u32[]{:S(2)}, u32[]{:S(2)}) collective-permute-start(bf16[2,128,512]{2,1,0:T(8,128)(2,1)S(1)} %collective-permute-done.12.refs_2_), channel_id=1, source_target_pairs={{0,1},{1,0},{2,3},{3,2},{4,5},{5,4},{6,7},{7,6},{8,9},{9,8},{10,11... | collective-permute-start | bytes 786440 | tf_op jit(solution)/shard_map/ppermute | solution.py:22
  112.1 11.2 %collective-permute-start.32 = (bf16[2,128,512]{2,1,0:T(8,128)(2,1)S(1)}, bf16[2,128,512]{2,1,0:T(8,128)(2,1)S(1)}, u32[]{:S(2)}, u32[]{:S(2)}) collective-permute-start(bf16[2,128,512]{2,1,0:T(8,128)(2,1)S(1)} %collective-permute-done.31.refs_3_), channel_id=1, source_target_pairs={{0,1},{1,0},{2,3},{3,2},{4,5},{5,4},{6,7},{7,6},{8,9},{9,8},{10,11... | collective-permute-start | bytes 786440 | tf_op jit(solution)/shard_map/ppermute | solution.py:22
  112.5 12.1 %collective-permute-start.34 = (bf16[2,128,512]{2,1,0:T(8,128)(2,1)S(1)}, bf16[2,128,512]{2,1,0:T(8,128)(2,1)S(1)}, u32[]{:S(2)}, u32[]{:S(2)}) collective-permute-start(bf16[2,128,512]{2,1,0:T(8,128)(2,1)S(1)} %collective-permute-done.33.refs_4_), channel_id=1, source_target_pairs={{0,1},{1,0},{2,3},{3,2},{4,5},{5,4},{6,7},{7,6},{8,9},{9,8},{10,11... | collective-permute-start | bytes 786440 | tf_op jit(solution)/shard_map/ppermute | solution.py:22
  116.6 4.8 %collective-permute-start.38 = (bf16[128,512]{1,0:T(8,128)(2,1)S(1)}, bf16[128,512]{1,0:T(8,128)(2,1)S(1)}, u32[]{:S(2)}, u32[]{:S(2)}) collective-permute-start(bf16[128,512]{1,0:T(8,128)(2,1)S(1)} %collective-permute-done.37.refs_6_), channel_id=1, source_target_pairs={{0,1},{1,0},{2,3},{3,2},{4,5},{5,4},{6,7},{7,6},{8,9},{9,8},{10,11... | collective-permute-start | bytes 393224 | tf_op jit(solution)/shard_map/ppermute | solution.py:22
  118.6 8.0 %collective-permute-start.28 = (bf16[128,512]{1,0:T(8,128)(2,1)S(1)}, bf16[128,512]{1,0:T(8,128)(2,1)S(1)}, u32[]{:S(2)}, u32[]{:S(2)}) collective-permute-start(bf16[128,512]{1,0:T(8,128)(2,1)S(1)} %slice_bitcast_fusion.7), channel_id=1, source_target_pairs={{0,16},{8,24},{16,0},{24,8},{1,17},{9,25},{17,1},{25,9},{2,18},{10... | collective-permute-start | bytes 393224 | tf_op jit(solution)/shard_map/ppermute | solution.py:22
  119.0 8.4 %collective-permute-start.29 = (bf16[128,512]{1,0:T(8,128)(2,1)S(1)}, bf16[128,512]{1,0:T(8,128)(2,1)S(1)}, u32[]{:S(2)}, u32[]{:S(2)}) collective-permute-start(bf16[128,512]{1,0:T(8,128)(2,1)S(1)} %slice_bitcast_fusion.6), channel_id=1, source_target_pairs={{0,8},{8,0},{16,24},{24,16},{1,9},{9,1},{17,25},{25,17},{2,10},{10... | collective-permute-start | bytes 393224 | tf_op jit(solution)/shard_map/ppermute | solution.py:22
  121.5 7.7 %collective-permute-start.22 = (bf16[128,512]{1,0:T(8,128)(2,1)S(1)}, bf16[128,512]{1,0:T(8,128)(2,1)S(1)}, u32[]{:S(2)}, u32[]{:S(2)}) collective-permute-start(bf16[128,512]{1,0:T(8,128)(2,1)S(1)} %slice_bitcast_fusion.9), channel_id=1, source_target_pairs={{0,16},{8,24},{16,0},{24,8},{1,17},{9,25},{17,1},{25,9},{2,18},{10... | collective-permute-start | bytes 393224 | tf_op jit(solution)/shard_map/ppermute | solution.py:22
  123.3 5.9 %collective-permute-start.23 = (bf16[128,512]{1,0:T(8,128)(2,1)S(1)}, bf16[128,512]{1,0:T(8,128)(2,1)S(1)}, u32[]{:S(2)}, u32[]{:S(2)}) collective-permute-start(bf16[128,512]{1,0:T(8,128)(2,1)S(1)} %slice_bitcast_fusion.8), channel_id=1, source_target_pairs={{0,8},{8,0},{16,24},{24,16},{1,9},{9,1},{17,25},{25,17},{2,10},{10... | collective-permute-start | bytes 393224 | tf_op jit(solution)/shard_map/ppermute | solution.py:22
  124.6 6.4 %collective-permute-start.16 = (bf16[128,512]{1,0:T(8,128)(2,1)S(1)}, bf16[128,512]{1,0:T(8,128)(2,1)S(1)}, u32[]{:S(2)}, u32[]{:S(2)}) collective-permute-start(bf16[128,512]{1,0:T(8,128)(2,1)S(1)} %slice_bitcast_fusion.11), channel_id=1, source_target_pairs={{0,16},{8,24},{16,0},{24,8},{1,17},{9,25},{17,1},{25,9},{2,18},{10... | collective-permute-start | bytes 393224 | tf_op jit(solution)/shard_map/ppermute | solution.py:22
  126.6 5.0 %collective-permute-start.17 = (bf16[128,512]{1,0:T(8,128)(2,1)S(1)}, bf16[128,512]{1,0:T(8,128)(2,1)S(1)}, u32[]{:S(2)}, u32[]{:S(2)}) collective-permute-start(bf16[128,512]{1,0:T(8,128)(2,1)S(1)} %slice_bitcast_fusion.10), channel_id=1, source_target_pairs={{0,8},{8,0},{16,24},{24,16},{1,9},{9,1},{17,25},{25,17},{2,10},{10... | collective-permute-start | bytes 393224 | tf_op jit(solution)/shard_map/ppermute | solution.py:22
  (13 other events, 31.9 us)
where the time goes:
time: 134 us
  waiting for transfers between devices  56.5 us (42%)
  starting transfers between devices  38.8 us (29%)
  Pallas kernels  26.7 us (20%)
  local copies, waits for them, and re-layouts  6.09 us (5%)
  other arithmetic  4.78 us (4%)
    ppermute x51, waiting for transfers between devices, exchanged(): lax.ppermute(value, axis, [(source, source ^ bit) for source in range(cou...  43.3 us
    ppermute x51, starting transfers between devices, exchanged(): lax.ppermute(value, axis, [(source, source ^ bit) for source in range(cou...  33.6 us
    pallas_call x9, Pallas kernels, sandwich(): pl.pallas_call(functools.partial(sandwich_kernel, 0.5 * order ** (-0.5),...  15.7 us
    ppermute x6, waiting for transfers between devices, shifted(): return lax.ppermute(value, 'ta', pairs)  13.2 us
    pallas_call x3, Pallas kernels, products(): pl.pallas_call(functools.partial(product_kernel, sections, source), in_sp...  11 us
    unnamed x8, local copies, waits for them, and re-layouts  5.68 us
    ppermute x6, starting transfers between devices, shifted(): return lax.ppermute(value, 'ta', pairs)  5.22 us
    convert_element_type x12, other arithmetic, reduced(): real, imag = (real.astype(jnp.bfloat16), imag.astype(jnp.bfloat16))  4.39 us
  transfers between devices with their start and end apart: 57, of which 17 were waited for; matrix products, arithmetic and copies ran while one was open for 4% of the time, Pallas kernels for 16%

commit v1 on v0

v1 whole, which is shorter than its diff:
```python
import functools

import jax
import jax.numpy as jnp
from jax import lax
from jax.experimental import pallas as pl
from jax.experimental.pallas import tpu as pltpu
from jax.sharding import PartitionSpec as P

STOPS = 3
dot = functools.partial(jnp.dot, preferred_element_type=jnp.float32)


def shifted(value, steps):
    count = lax.axis_size("ta")
    pairs = [(source, (source + steps) % count) for source in range(count)]
    return lax.ppermute(value, "ta", pairs)


def exchanged(value, axis, bit):
    count = lax.axis_size(axis)
    return lax.ppermute(value, axis, [(source, source ^ bit) for source in range(count)])


def reversed_bits(value, width):
    return sum(((value >> place) & 1) << (width - 1 - place) for place in range(width))


def over_rows(left, right):
    return lax.dot_general(
        left, right, (((0,), (0,)), ((), ())), preferred_element_type=jnp.float32
    )


def product_kernel(sections, source, sources, *refs):
    refs = list(refs)
    first, last = source == 0, source == sources - 1
    if first:
        live_hbm, times_hbm, sink_hbm, prop_hbm = refs[:4]
        refs = refs[4:]
    else:
        times_hbm, sink, prop, prop_hbm = refs[:4]
        refs = refs[4:]
    keep_real, send_real, keep_imag, send_imag = refs[:4]
    refs = refs[4:]
    if first:
        sink = refs.pop(0)
    following = None if last else refs.pop(0)
    real, imag, times, sems, index_sems = refs[:5]
    refs = refs[5:]
    index_copies = [pltpu.make_async_copy(times_hbm, times, index_sems.at[0])]
    copies = []
    if first:
        live_rows, raw, prop = refs
        index_copies.append(pltpu.make_async_copy(live_hbm, live_rows, index_sems.at[1]))
        for part in range(2):
            copies.append(pltpu.make_async_copy(sink_hbm.at[part, 0], raw.at[part], sems.at[part]))
            copies.append(
                pltpu.make_async_copy(prop_hbm.at[0, part, 0], prop.at[part], sems.at[2 + part])
            )
    if not last:
        for part in range(2):
            copies.append(
                pltpu.make_async_copy(
                    prop_hbm.at[source + 1, part, 0], following.at[part], sems.at[4 + part]
                )
            )
    for copy in index_copies + copies:
        copy.start()
    section = lax.axis_index("sec")
    depth, order = sink.shape[1:]
    for copy in index_copies:
        copy.wait()
    sign = jnp.where(lax.axis_index("ta") < times[source], -1.0, 1.0).astype(jnp.float32)
    if first:
        live = lax.broadcasted_iota(jnp.int32, (depth, order), 0) < live_rows[section]
        for part in range(2):
            copies.pop(0).wait()
            sink[part] = jnp.where(live, raw[part], jnp.zeros((depth, order), jnp.bfloat16))
            copies.pop(0).wait()
            if part == 0:
                start = over_rows(sink[0], prop[0])
        real[...] = ((start + over_rows(sink[1], prop[1])) * sign).astype(jnp.bfloat16)
    else:
        real[...] = (
            (over_rows(sink[0], prop[0]) + over_rows(sink[1], prop[1])) * sign
        ).astype(jnp.bfloat16)
    imag[...] = (
        (over_rows(sink[0], prop[1]) - over_rows(sink[1], prop[0])) * sign
    ).astype(jnp.bfloat16)
    half = sections // 2
    width = sections.bit_length() - 1
    rows = order // sections
    for q in range(sections):
        window = pl.ds(pl.multiple_of((section ^ q) * rows, rows), rows)
        slot = reversed_bits(q, width)
        (keep_real if slot < half else send_real)[slot % half] = real[window, :]
        (keep_imag if q < half else send_imag)[q % half] = imag[window, :]
    for copy in copies:
        copy.wait()


def hbm(value):
    return pltpu.with_memory_space_constraint(value, pltpu.HBM)


def products(live_rows, source_times, sink_vectors, propagators, sections):
    _, _, depth, order = sink_vectors.shape
    sources, columns = propagators.shape[0], propagators.shape[4]
    bf16 = jnp.bfloat16
    in_hbm, in_vmem = pl.BlockSpec(memory_space=pltpu.HBM), pl.BlockSpec(memory_space=pltpu.VMEM)
    half = pltpu.VMEM((sections // 2, order // sections, columns), bf16)
    held = pltpu.VMEM((2, depth, order), bf16)
    fetched = pltpu.VMEM((2, depth, columns), bf16)
    halves, sink, prop = [], None, None
    for source in range(sources):
        first, last = source == 0, source == sources - 1
        if first:
            operands = [hbm(live_rows), hbm(source_times), hbm(sink_vectors), hbm(propagators)]
            in_specs = [in_hbm] * 4
        else:
            operands = [hbm(source_times), sink, prop, hbm(propagators)]
            in_specs = [in_hbm, in_vmem, in_vmem, in_hbm]
        outs = [half] * 4 + [held] * first + [fetched] * (not last)
        scratch = [
            pltpu.VMEM((order, columns), bf16),
            pltpu.VMEM((order, columns), bf16),
            pltpu.SMEM(source_times.shape, jnp.int32),
            pltpu.SemaphoreType.DMA((6,)),
            pltpu.SemaphoreType.DMA((2,)),
        ]
        if first:
            scratch += [pltpu.SMEM(live_rows.shape, jnp.int32), held, fetched]
        results = pl.pallas_call(
            functools.partial(product_kernel, sections, source, sources),
            in_specs=in_specs,
            out_specs=[in_vmem] * len(outs),
            out_shape=outs,
            scratch_shapes=scratch,
            compiler_params=pltpu.CompilerParams(vmem_limit_bytes=24 << 20),
            cost_estimate=pl.CostEstimate(
                flops=8 * order * depth * columns,
                bytes_accessed=4 * depth * columns,
                transcendentals=0,
            ),
        )(*operands)
        halves.append(results[:4])
        if first:
            sink = results[4]
        prop = results[-1]
    return halves


def reduced(keep_real, send_real, keep_imag, send_imag, width):
    for step in range(width):
        got_real = exchanged(send_real, "sec", 1 << step)
        got_imag = exchanged(send_imag, "sec", 1 << (width - 1 - step))
        real = keep_real.astype(jnp.float32) + got_real.astype(jnp.float32)
        imag = keep_imag.astype(jnp.float32) + got_imag.astype(jnp.float32)
        real, imag = real.astype(jnp.bfloat16), imag.astype(jnp.bfloat16)
        half = real.shape[0] // 2
        if half:
            keep_real, send_real = real[:half], real[half:]
            keep_imag, send_imag = imag[:half], imag[half:]
    return jnp.concatenate((real, imag), 0)


def gathered(own, width):
    count = own.shape[0]
    whole = {0: own}
    places = [[((own, (s, 0)), (own, (s, 1)))] for s in range(count)]
    for q in range(1, 1 << width):
        high = 1 << (q.bit_length() - 1)
        low = q & -q
        if high == low:
            whole[q] = exchanged(own, "sec", high)
        for s in range(count):
            if high == low:
                places[s].append(((whole[q], (s, 0)), (whole[q], (s, 1))))
                continue
            (first, at_first), (second, at_second) = places[s][q ^ high][0], places[s][q ^ low][1]
            places[s].append(
                (
                    (exchanged(first[at_first], "sec", high), ()),
                    (exchanged(second[at_second], "sec", low), ()),
                )
            )
    return places


def sandwich_kernel(scale, lookup, source, kind, aliased, passed_on, *refs):
    left_real, left_imag = refs[0], refs[1]
    names = 1 + max(name for pair in lookup for name, _ in pair)
    blocks = refs[2 : 2 + names]
    rest = list(refs[2 + names + aliased :])
    out = rest.pop(0)
    real = [blocks[name][at if at else ...] for (name, at), _ in lookup]
    imag = [blocks[name][at if at else ...] for _, (name, at) in lookup]
    if passed_on:
        together = rest.pop(0)
        for q, pair in enumerate(zip(real, imag)):
            for part in range(2):
                together[q, part] = pair[part]
    tile, sems = rest
    right_real, right_imag = jnp.concatenate(real, 0), jnp.concatenate(imag, 0)
    one, two = left_real[...], left_imag[...]
    parity = lax.axis_index("ta") % 2
    stop = (2 * parity, 1, 2 - 2 * parity)[kind]
    shape = tile.shape[1:]
    copies = []
    for part in range(2):
        if part == 0:
            value = dot(one, right_real) - dot(two, right_imag)
        else:
            value = dot(one, right_imag) + dot(two, right_real)
        tile[part] = (value * scale).astype(jnp.bfloat16).reshape(shape)
        copies.append(
            pltpu.make_async_copy(tile.at[part], out.at[stop, :, source, part, 0], sems.at[part])
        )
        copies[-1].start()
    for copy in copies:
        copy.wait()


def sandwich(buffer, kind, source, left_real, left_imag, places, shape, passed_on=False):
    arrays, lookup = [], []
    for pair in places:
        entry = []
        for array, at in pair:
            known = [i for i, other in enumerate(arrays) if other is array]
            if not known:
                arrays.append(array)
                known = [len(arrays) - 1]
            entry.append((known[0], at))
        lookup.append(tuple(entry))
    order, columns = left_real.shape[1], shape[6]
    operands = [left_real, left_imag, *arrays]
    in_vmem, in_hbm = pl.BlockSpec(memory_space=pltpu.VMEM), pl.BlockSpec(memory_space=pltpu.HBM)
    in_specs = [in_vmem] * len(operands)
    aliases = {}
    if buffer is not None:
        aliases = {len(operands): 0}
        in_specs.append(in_hbm)
        operands.append(hbm(buffer))
    outs = [pltpu.HBM(shape, jnp.bfloat16)]
    if passed_on:
        outs.append(pltpu.VMEM((len(places), 2, shape[5], columns), jnp.bfloat16))
    return pl.pallas_call(
        functools.partial(
            sandwich_kernel, 0.5 * order ** (-0.5), tuple(lookup), source, kind,
            len(aliases), passed_on,
        ),
        in_specs=in_specs,
        out_specs=[in_hbm, in_vmem][: len(outs)],
        out_shape=outs,
        scratch_shapes=[
            pltpu.VMEM((2, shape[1]) + tuple(shape[5:]), jnp.bfloat16),
            pltpu.SemaphoreType.DMA((2,)),
        ],
        input_output_aliases=aliases,
        compiler_params=pltpu.CompilerParams(vmem_limit_bytes=12 << 20),
        cost_estimate=pl.CostEstimate(
            flops=8 * left_real.shape[0] * order * columns,
            bytes_accessed=4 * order * columns + 8 * left_real.size,
            transcendentals=0,
        ),
    )(*operands)


def body(sink_vectors, propagators, live_rows, source_times):
    sections = lax.axis_size("sec")
    width = sections.bit_length() - 1
    section = lax.axis_index("sec")
    first_core = lax.axis_index("ta") % 2 == 0
    sources = propagators.shape[0]
    order = sink_vectors.shape[3]
    rows = order // sections

    halves = products(live_rows, source_times, sink_vectors, propagators, sections)
    own = [reduced(*halves[s], width) for s in range(sources)]
    second = [shifted(own[s], 2) for s in range(sources)]
    mine, theirs = jnp.stack(own), jnp.stack(second)
    other = shifted(jnp.where(first_core, mine, theirs), 1)

    left = jnp.swapaxes(mine, 0, 1)
    left = jnp.concatenate(
        [
            lax.dynamic_slice_in_dim(left, (section ^ q) * rows, rows, axis=3)
            for q in range(sections)
        ],
        3,
    ).reshape(2, sources * rows, order)
    left_real, left_imag = left[0], left[1]

    shape = (STOPS, sources, sources, 2, 1, rows, order)
    result = None
    for s in range(sources):
        (places,) = gathered(second[s][None], width)
        result, together = sandwich(result, 1, s, left_real, left_imag, places, shape, True)
        together = exchanged(together, "ta", 1)
        places = [tuple((together, (q, part)) for part in range(2)) for q in range(sections)]
        (result,) = sandwich(result, 0, s, left_real, left_imag, places, shape)
    for s, places in enumerate(gathered(other, width)):
        (result,) = sandwich(result, 2, s, left_real, left_imag, places, shape)
    return result


def solution(mesh):
    return jax.shard_map(
        body,
        mesh=mesh,
        in_specs=(P(None, "ta", "sec", None), P(None, None, "ta", "sec", None), P(), P()),
        out_specs=P(None, None, None, None, "ta", "sec", None),
        check_vma=False,
    )
```

time: 134 us -> 135 us (level)
  starting transfers between devices: 38.8 us -> 49.5 us
  local copies, waits for them, and re-layouts: 6.09 us -> 0.4 us
  other arithmetic: 4.78 us -> 0.98 us
    ppermute x51 -> x35, starting transfers between devices: 33.6 us -> 44.1 us  [exchanged(): lax.ppermute(value, axis, [(source, source ^ bit) for source in range(cou...]
    ppermute x51 -> x35, waiting for transfers between devices: 43.3 us -> 49.1 us  [exchanged(): lax.ppermute(value, axis, [(source, source ^ bit) for source in range(cou...]
    unnamed x8 -> x0, local copies, waits for them, and re-layouts: 5.68 us -> none
    ppermute x6 -> x4, waiting for transfers between devices: 13.2 us -> 7.63 us  [shifted(): return lax.ppermute(value, 'ta', pairs)]
    convert_element_type x12, other arithmetic: 4.39 us -> 0.59 us  [reduced(): real, imag = (real.astype(jnp.bfloat16), imag.astype(jnp.bfloat16))]
    ppermute x6 -> x4, starting transfers between devices: 5.22 us -> 5.35 us  [shifted(): return lax.ppermute(value, 'ta', pairs)]
  transfers between devices with their start and end apart: 57 -> 39, of which waited for: 17 -> 19; matrix products, arithmetic and copies ran while one was open for 4% -> 1% of each run, Pallas kernels for 16% -> 9%
where the time goes in v1:
time: 135 us
  waiting for transfers between devices  56.8 us (42%)
  starting transfers between devices  49.5 us (37%)
  Pallas kernels  26.9 us (20%)
    ppermute x35, waiting for transfers between devices, exchanged(): lax.ppermute(value, axis, [(source, source ^ bit) for source in range(cou...  49.1 us
    ppermute x35, starting transfers between devices, exchanged(): lax.ppermute(value, axis, [(source, source ^ bit) for source in range(cou...  44.1 us
    pallas_call x9, Pallas kernels, sandwich(): pl.pallas_call(functools.partial(sandwich_kernel, 0.5 * order ** (-0.5),...  15.7 us
    pallas_call x3, Pallas kernels, products(): pl.pallas_call(functools.partial(product_kernel, sections, source, source...  11.1 us
    ppermute x4, waiting for transfers between devices, shifted(): return lax.ppermute(value, 'ta', pairs)  7.63 us
    ppermute x4, starting transfers between devices, shifted(): return lax.ppermute(value, 'ta', pairs)  5.35 us
  transfers between devices with their start and end apart: 39, of which 19 were waited for; matrix products, arithmetic and copies ran while one was open for 1% of the time, Pallas kernels for 9%

profile of v1, /device:TPU:0, one launch (start us, length us, event | category | flops | bytes accessed | tf_op | source)
XLA Modules:
  0.0 135.1 jit_solution(678428636367945330)
XLA Ops:
  0.0 4.7 %shard_map.46 = (bf16[2,128,512]{2,1,0:T(8,128)(2,1)S(1)}, bf16[2,128,512]{2,1,0:T(8,128)(2,1)S(1)}, bf16[2,128,512]{2,1,0:T(8,128)(2,1)S(1)}, bf16[2,128,512]{2...) custom-call(s32[4]{0:T(128)} %refs_0_.3, s32[3]{0:T(128)} %refs_0_.5, ...), custom_call_target="tpu_custom_call" | custom-call | flops 2147483648 | bytes 2097152 | tf_op jit(solution)/shard_map/pallas_call | solution.py:134
  4.7 3.3 %shard_map.47 = (bf16[2,128,512]{2,1,0:T(8,128)(2,1)S(1)}, bf16[2,128,512]{2,1,0:T(8,128)(2,1)S(1)}, bf16[2,128,512]{2,1,0:T(8,128)(2,1)S(1)}, bf16[2,128,512]{2,1,0:T(8,128)(2,1)S(1)}, bf16[2,1024,512]{2,1,0:T(8,128)(2,1)S(1)}) custom-call(s32[3]{0:T(128)} %refs_0_.5, bf16[2,1024,512]{2,1,0:T(8,128)(2,1)S(1)} %get-tuple-element.30.refs_1_, ...), custom_call_target="tpu_custom_call" | custom-call | flops 2147483648 | bytes 2097152 | tf_op jit(solution)/shard_map/pallas_call | solution.py:134
  8.0 3.2 %shard_map.48 = (bf16[2,128,512]{2,1,0:T(8,128)(2,1)S(1)}, bf16[2,128,512]{2,1,0:T(8,128)(2,1)S(1)}, bf16[2,128,512]{2,1,0:T(8,128)(2,1)S(1)}, bf16[2,128,512]{2,1,0:T(8,128)(2,1)S(1)}) custom-call(s32[3]{0:T(128)} %refs_0_.5, bf16[2,1024,512]{2,1,0:T(8,128)(2,1)S(1)} %get-tuple-element.30.refs_1_, bf16[2,1024,512]{2,1,0:T(8,128)(2,1)S(1)} %get-tuple-element.36.refs_2_, ...), custom_call_target="tpu_custom_call" | custom-call | flops 2147483648 | bytes 2097152 | tf_op jit(solution)/shard_map/pallas_call | solution.py:134
  11.2 3.0 %collective-permute-start.8 = (bf16[2,128,512]{2,1,0:T(8,128)(2,1)S(1)}, bf16[2,128,512]{2,1,0:T(8,128)(2,1)S(1)}, u32[]{:S(2)}, u32[]{:S(2)}) collective-permute-start(bf16[2,128,512]{2,1,0:T(8,128)(2,1)S(1)} %get-tuple-element.38), channel_id=1, source_target_pairs={{0,8},{8,0},{16,24},{24,16},{1,9},{9,1},{17,25},{25,17},{2,10},{10... | collective-permute-start | bytes 786440 | tf_op jit(solution)/shard_map/ppermute | solution.py:22
  14.2 1.6 %collective-permute-start.10 = (bf16[2,128,512]{2,1,0:T(8,128)(2,1)S(1)}, bf16[2,128,512]{2,1,0:T(8,128)(2,1)S(1)}, u32[]{:S(2)}, u32[]{:S(2)}) collective-permute-start(bf16[2,128,512]{2,1,0:T(8,128)(2,1)S(1)} %get-tuple-element.40), channel_id=1, source_target_pairs={{0,16},{8,24},{16,0},{24,8},{1,17},{9,25},{17,1},{25,9},{2,18},{10... | collective-permute-start | bytes 786440 | tf_op jit(solution)/shard_map/ppermute | solution.py:22
  16.3 1.9 %collective-permute-start = (bf16[2,128,512]{2,1,0:T(8,128)(2,1)S(1)}, bf16[2,128,512]{2,1,0:T(8,128)(2,1)S(1)}, u32[]{:S(2)}, u32[]{:S(2)}) collective-permute-start(bf16[2,128,512]{2,1,0:T(8,128)(2,1)S(1)} %get-tuple-element.27), channel_id=1, source_target_pairs={{0,8},{8,0},{16,24},{24,16},{1,9},{9,1},{17,25},{25,17},{2,10},{10... | collective-permute-start | bytes 786440 | tf_op jit(solution)/shard_map/ppermute | solution.py:22
  18.3 3.1 %collective-permute-done.8 = bf16[2,128,512]{2,1,0:T(8,128)(2,1)S(1)} collective-permute-done((bf16[2,128,512]{2,1,0:T(8,128)(2,1)S(1)}, bf16[2,128,512]{2,1,0:T(8,128)(2,1)S(1)}, u32[]{:S(2)}, u32[]{:S(2)}) %collective-permute-start.8) | collective-permute-done | bytes 262176 | tf_op jit(solution)/shard_map/ppermute | solution.py:22
  21.4 2.1 %collective-permute-start.2 = (bf16[2,128,512]{2,1,0:T(8,128)(2,1)S(1)}, bf16[2,128,512]{2,1,0:T(8,128)(2,1)S(1)}, u32[]{:S(2)}, u32[]{:S(2)}) collective-permute-start(bf16[2,128,512]{2,1,0:T(8,128)(2,1)S(1)} %get-tuple-element.29), channel_id=1, source_target_pairs={{0,16},{8,24},{16,0},{24,8},{1,17},{9,25},{17,1},{25,9},{2,18},{10... | collective-permute-start | bytes 786440 | tf_op jit(solution)/shard_map/ppermute | solution.py:22
  23.5 1.5 %collective-permute-start.9 = (bf16[1,128,512]{2,1,0:T(8,128)(2,1)S(1)}, bf16[1,128,512]{2,1,0:T(8,128)(2,1)S(1)}, u32[]{:S(2)}, u32[]{:S(2)}) collective-permute-start(bf16[1,128,512]{2,1,0:T(8,128)(2,1)S(1)} %slice.115), channel_id=1, source_target_pairs={{0,16},{8,24},{16,0},{24,8},{1,17},{9,25},{17,1},{25,9},{2,18},{10... | collective-permute-start | bytes 393224 | tf_op jit(solution)/shard_map/ppermute | solution.py:22
  25.1 1.9 %collective-permute-done.4 = bf16[2,128,512]{2,1,0:T(8,128)(2,1)S(1)} collective-permute-done((bf16[2,128,512]{2,1,0:T(8,128)(2,1)S(1)}, bf16[2,128,512]{2,1,0:T(8,128)(2,1)S(1)}, u32[]{:S(2)}, u32[]{:S(2)}) %collective-permute-start.4) | collective-permute-done | bytes 262176 | tf_op jit(solution)/shard_map/ppermute | solution.py:22
  27.0 2.0 %collective-permute-start.11 = (bf16[1,128,512]{2,1,0:T(8,128)(2,1)S(1)}, bf16[1,128,512]{2,1,0:T(8,128)(2,1)S(1)}, u32[]{:S(2)}, u32[]{:S(2)}) collective-permute-start(bf16[1,128,512]{2,1,0:T(8,128)(2,1)S(1)} %slice.117), channel_id=1, source_target_pairs={{0,8},{8,0},{16,24},{24,16},{1,9},{9,1},{17,25},{25,17},{2,10},{10... | collective-permute-start | bytes 393224 | tf_op jit(solution)/shard_map/ppermute | solution.py:22
  29.1 1.7 %collective-permute-start.5 = (bf16[1,128,512]{2,1,0:T(8,128)(2,1)S(1)}, bf16[1,128,512]{2,1,0:T(8,128)(2,1)S(1)}, u32[]{:S(2)}, u32[]{:S(2)}) collective-permute-start(bf16[1,128,512]{2,1,0:T(8,128)(2,1)S(1)} %slice.111), channel_id=1, source_target_pairs={{0,16},{8,24},{16,0},{24,8},{1,17},{9,25},{17,1},{25,9},{2,18},{10... | collective-permute-start | bytes 393224 | tf_op jit(solution)/shard_map/ppermute | solution.py:22
  30.9 1.7 %collective-permute-done = bf16[2,128,512]{2,1,0:T(8,128)(2,1)S(1)} collective-permute-done((bf16[2,128,512]{2,1,0:T(8,128)(2,1)S(1)}, bf16[2,128,512]{2,1,0:T(8,128)(2,1)S(1)}, u32[]{:S(2)}, u32[]{:S(2)}) %collective-permute-start) | collective-permute-done | bytes 262176 | tf_op jit(solution)/shard_map/ppermute | solution.py:22
  32.6 2.0 %collective-permute-start.7 = (bf16[1,128,512]{2,1,0:T(8,128)(2,1)S(1)}, bf16[1,128,512]{2,1,0:T(8,128)(2,1)S(1)}, u32[]{:S(2)}, u32[]{:S(2)}) collective-permute-start(bf16[1,128,512]{2,1,0:T(8,128)(2,1)S(1)} %slice.113), channel_id=1, source_target_pairs={{0,8},{8,0},{16,24},{24,16},{1,9},{9,1},{17,25},{25,17},{2,10},{10... | collective-permute-start | bytes 393224 | tf_op jit(solution)/shard_map/ppermute | solution.py:22
  34.7 1.7 %collective-permute-start.1 = (bf16[1,128,512]{2,1,0:T(8,128)(2,1)S(1)}, bf16[1,128,512]{2,1,0:T(8,128)(2,1)S(1)}, u32[]{:S(2)}, u32[]{:S(2)}) collective-permute-start(bf16[1,128,512]{2,1,0:T(8,128)(2,1)S(1)} %slice.107), channel_id=1, source_target_pairs={{0,16},{8,24},{16,0},{24,8},{1,17},{9,25},{17,1},{25,9},{2,18},{10... | collective-permute-start | bytes 393224 | tf_op jit(solution)/shard_map/ppermute | solution.py:22
  37.6 2.1 %collective-permute-start.14 = (bf16[2,128,512]{2,1,0:T(8,128)(2,1)S(1)}, bf16[2,128,512]{2,1,0:T(8,128)(2,1)S(1)}, u32[]{:S(2)}, u32[]{:S(2)}) collective-permute-start(bf16[2,128,512]{2,1,0:T(8,128)(2,1)S(1)} %get-tuple-element.65), channel_id=1, source_target_pairs={{0,2},{1,3},{2,4},{3,5},{4,6},{5,7},{6,0},{7,1},{8,10},{9,11},{10,... | collective-permute-start | bytes 786440 | tf_op jit(solution)/shard_map/ppermute | solution.py:17
  39.7 1.9 %collective-permute-done.1 = bf16[1,128,512]{2,1,0:T(8,128)(2,1)S(1)} collective-permute-done((bf16[1,128,512]{2,1,0:T(8,128)(2,1)S(1)}, bf16[1,128,512]{2,1,0:T(8,128)(2,1)S(1)}, u32[]{:S(2)}, u32[]{:S(2)}) %collective-permute-start.1) | collective-permute-done | bytes 131104 | tf_op jit(solution)/shard_map/ppermute | solution.py:22
  42.5 1.6 %collective-permute-start.12 = (bf16[2,128,512]{2,1,0:T(8,128)(2,1)S(1)}, bf16[2,128,512]{2,1,0:T(8,128)(2,1)S(1)}, u32[]{:S(2)}, u32[]{:S(2)}) collective-permute-start(bf16[2,128,512]{2,1,0:T(8,128)(2,1)S(1)} %get-tuple-element.61), channel_id=1, source_target_pairs={{0,2},{1,3},{2,4},{3,5},{4,6},{5,7},{6,0},{7,1},{8,10},{9,11},{10,... | collective-permute-start | bytes 786440 | tf_op jit(solution)/shard_map/ppermute | solution.py:17
  44.2 1.6 %collective-permute-start.13 = (bf16[2,128,512]{2,1,0:T(8,128)(2,1)S(1)}, bf16[2,128,512]{2,1,0:T(8,128)(2,1)S(1)}, u32[]{:S(2)}, u32[]{:S(2)}) collective-permute-start(bf16[2,128,512]{2,1,0:T(8,128)(2,1)S(1)} %get-tuple-element.63), channel_id=1, source_target_pairs={{0,2},{1,3},{2,4},{3,5},{4,6},{5,7},{6,0},{7,1},{8,10},{9,11},{10,... | collective-permute-start | bytes 786440 | tf_op jit(solution)/shard_map/ppermute | solution.py:17
  45.9 7.6 %collective-permute-done.12 = bf16[2,128,512]{2,1,0:T(8,128)(2,1)S(1)} collective-permute-done((bf16[2,128,512]{2,1,0:T(8,128)(2,1)S(1)}, bf16[2,128,512]{2,1,0:T(8,128)(2,1)S(1)}, u32[]{:S(2)}, u32[]{:S(2)}) %collective-permute-start.12) | collective-permute-done | bytes 262176 | tf_op jit(solution)/shard_map/ppermute | solution.py:17
  53.5 2.2 %collective-permute-start.32 = (bf16[1,2,128,512]{3,2,1,0:T(8,128)(2,1)S(1)}, bf16[1,2,128,512]{3,2,1,0:T(8,128)(2,1)S(1)}, u32[]{:S(2)}, u32[]{:S(2)}) collective-permute-start(bf16[1,2,128,512]{3,2,1,0:T(8,128)(2,1)S(1)} %bitcast.69), channel_id=1, source_target_pairs={{0,8},{8,0},{16,24},{24,16},{1,9},{9,1},{17,25},{25,17},{2,10},{10... | collective-permute-start | bytes 786440 | tf_op jit(solution)/shard_map/ppermute | solution.py:22
  55.7 1.8 %collective-permute-start.33 = (bf16[1,2,128,512]{3,2,1,0:T(8,128)(2,1)S(1)}, bf16[1,2,128,512]{3,2,1,0:T(8,128)(2,1)S(1)}, u32[]{:S(2)}, u32[]{:S(2)}) collective-permute-start(bf16[1,2,128,512]{3,2,1,0:T(8,128)(2,1)S(1)} %bitcast.70), channel_id=1, source_target_pairs={{0,16},{8,24},{16,0},{24,8},{1,17},{9,25},{17,1},{25,9},{2,18},{10... | collective-permute-start | bytes 786440 | tf_op jit(solution)/shard_map/ppermute | solution.py:22
  57.9 2.4 %collective-permute-done.32.refs_3_ = bf16[1,2,128,512]{3,2,1,0:T(8,128)(2,1)S(1)} collective-permute-done((bf16[1,2,128,512]{3,2,1,0:T(8,128)(2,1)S(1)}, bf16[1,2,128,512]{3,2,1,0:T(8,128)(2,1)S(1)}, u32[]{:S(2)}, u32[]{:S(2)}) %collective-permute-start.32) | collective-permute-done | bytes 262176 | tf_op jit(solution)/shard_map/ppermute | solution.py:22
  60.3 2.6 %collective-permute-start.34 = (bf16[128,512]{1,0:T(8,128)(2,1)S(1)}, bf16[128,512]{1,0:T(8,128)(2,1)S(1)}, u32[]{:S(2)}, u32[]{:S(2)}) collective-permute-start(bf16[128,512]{1,0:T(8,128)(2,1)S(1)} %slice_bitcast_fusion.1), channel_id=1, source_target_pairs={{0,16},{8,24},{16,0},{24,8},{1,17},{9,25},{17,1},{25,9},{2,18},{10... | collective-permute-start | bytes 393224 | tf_op jit(solution)/shard_map/ppermute | solution.py:22
  63.1 2.3 %collective-permute-start.35 = (bf16[128,512]{1,0:T(8,128)(2,1)S(1)}, bf16[128,512]{1,0:T(8,128)(2,1)S(1)}, u32[]{:S(2)}, u32[]{:S(2)}) collective-permute-start(bf16[128,512]{1,0:T(8,128)(2,1)S(1)} %slice_bitcast_fusion), channel_id=1, source_target_pairs={{0,8},{8,0},{16,24},{24,16},{1,9},{9,1},{17,25},{25,17},{2,10},{10... | collective-permute-start | bytes 393224 | tf_op jit(solution)/shard_map/ppermute | solution.py:22
  65.9 2.5 %collective-permute-done.35.refs_6_ = bf16[128,512]{1,0:T(8,128)(2,1)S(1)} collective-permute-done((bf16[128,512]{1,0:T(8,128)(2,1)S(1)}, bf16[128,512]{1,0:T(8,128)(2,1)S(1)}, u32[]{:S(2)}, u32[]{:S(2)}) %collective-permute-start.35) | collective-permute-done | bytes 131104 | tf_op jit(solution)/shard_map/ppermute | solution.py:22
  68.4 1.8 %shard_map.49 = (bf16[3,3,3,2,1,128,512]{6,5,4,3,2,1,0:T(8,128)(2,1)}, bf16[4,2,128,512]{3,2,1,0:T(8,128)(2,1)S(1)}) custom-call(bf16[384,512]{1,0:T(8,128)(2,1)S(1)} %bitcast.52, bf16[384,512]{1,0:T(8,128)(2,1)S(1)} %bitcast.43, bf16[1,2,128,512]{3,2,1,0:T(8,128)(2,1)S(1)} %bitcast.72, bf16[1,2,128,512]{3,2,1,0:T(8,128)(2,1)S(1)} %collective-permute-done.32.refs_3_, ...), custom_call_target="tpu_custom_call" | custom-call | flops 805306368 | bytes 2621440 | tf_op jit(solution)/shard_map/pallas_call | solution.py:248
  70.2 2.1 %collective-permute-start.28 = (bf16[1,2,128,512]{3,2,1,0:T(8,128)(2,1)S(1)}, bf16[1,2,128,512]{3,2,1,0:T(8,128)(2,1)S(1)}, u32[]{:S(2)}, u32[]{:S(2)}) collective-permute-start(bf16[1,2,128,512]{3,2,1,0:T(8,128)(2,1)S(1)} %bitcast.66), channel_id=1, source_target_pairs={{0,8},{8,0},{16,24},{24,16},{1,9},{9,1},{17,25},{25,17},{2,10},{10... | collective-permute-start | bytes 786440 | tf_op jit(solution)/shard_map/ppermute | solution.py:22
  72.3 6.9 %collective-permute-done.28.refs_3_ = bf16[1,2,128,512]{3,2,1,0:T(8,128)(2,1)S(1)} collective-permute-done((bf16[1,2,128,512]{3,2,1,0:T(8,128)(2,1)S(1)}, bf16[1,2,128,512]{3,2,1,0:T(8,128)(2,1)S(1)}, u32[]{:S(2)}, u32[]{:S(2)}) %collective-permute-start.28) | collective-permute-done | bytes 262176 | tf_op jit(solution)/shard_map/ppermute | solution.py:22
  79.2 1.3 collective-permute-start.30
  81.1 1.7 %shard_map.50.refs_7_ = bf16[3,3,3,2,1,128,512]{6,5,4,3,2,1,0:T(8,128)(2,1)} custom-call(bf16[384,512]{1,0:T(8,128)(2,1)S(1)} %bitcast.53, bf16[384,512]{1,0:T(8,128)(2,1)S(1)} %bitcast.44, bf16[4,2,128,512]{3,2,1,0:T(8,128)(2,1)S(1)} %collective-permute-done.36.refs_2_, ...), custom_call_target="tpu_custom_call", output_to_operand_aliasing={{}: (3, {})} | custom-call | flops 805306368 | bytes 2621440 | tf_op jit(solution)/shard_map/pallas_call | solution.py:248
  82.9 1.6 %collective-permute-done.30.refs_5_ = bf16[128,512]{1,0:T(8,128)(2,1)S(1)} collective-permute-done((bf16[128,512]{1,0:T(8,128)(2,1)S(1)}, bf16[128,512]{1,0:T(8,128)(2,1)S(1)}, u32[]{:S(2)}, u32[]{:S(2)}) %collective-permute-start.30) | collective-permute-done | bytes 131104 | tf_op jit(solution)/shard_map/ppermute | solution.py:22
  84.5 1.2 collective-permute-done.31.refs_6_
  85.7 1.8 %shard_map.51 = (bf16[3,3,3,2,1,128,512]{6,5,4,3,2,1,0:T(8,128)(2,1)}, bf16[4,2,128,512]{3,2,1,0:T(8,128)(2,1)S(1)}) custom-call(bf16[384,512]{1,0:T(8,128)(2,1)S(1)} %bitcast.54, bf16[384,512]{1,0:T(8,128)(2,1)S(1)} %bitcast.45, bf16[1,2,128,512]{3,2,1,0:T(8,128)(2,1)S(1)} %bitcast.68, ...), custom_call_target="tpu_custom_call", output_to_operand_aliasing={{0}: (7, {})} | custom-call | flops 805306368 | bytes 2621440 | tf_op jit(solution)/shard_map/pallas_call | solution.py:248
  88.0 2.0 %collective-permute-start.25 = (bf16[1,2,128,512]{3,2,1,0:T(8,128)(2,1)S(1)}, bf16[1,2,128,512]{3,2,1,0:T(8,128)(2,1)S(1)}, u32[]{:S(2)}, u32[]{:S(2)}) collective-permute-start(bf16[1,2,128,512]{3,2,1,0:T(8,128)(2,1)S(1)} %bitcast.63), channel_id=1, source_target_pairs={{0,16},{8,24},{16,0},{24,8},{1,17},{9,25},{17,1},{25,9},{2,18},{10... | collective-permute-start | bytes 786440 | tf_op jit(solution)/shard_map/ppermute | solution.py:22
  90.0 6.3 %collective-permute-done.24.refs_3_ = bf16[1,2,128,512]{3,2,1,0:T(8,128)(2,1)S(1)} collective-permute-done((bf16[1,2,128,512]{3,2,1,0:T(8,128)(2,1)S(1)}, bf16[1,2,128,512]{3,2,1,0:T(8,128)(2,1)S(1)}, u32[]{:S(2)}, u32[]{:S(2)}) %collective-permute-start.24) | collective-permute-done | bytes 262176 | tf_op jit(solution)/shard_map/ppermute | solution.py:22
  97.0 1.7 %collective-permute-start.16 = (bf16[3,2,128,512]{3,2,1,0:T(8,128)(2,1)S(1)}, bf16[3,2,128,512]{3,2,1,0:T(8,128)(2,1)S(1)}, u32[]{:S(2)}, u32[]{:S(2)}) collective-permute-start(bf16[3,2,128,512]{3,2,1,0:T(8,128)(2,1)S(1)} %collective-permute-done.15.refs_2_), channel_id=1, source_target_pairs={{0,8},{8,0},{16,24},{24,16},{1,9},{9,1},{17,25},{25,17},{2,10},{10... | collective-permute-start | bytes 2359304 | tf_op jit(solution)/shard_map/ppermute | solution.py:22
  99.1 1.4 %collective-permute-start.17 = (bf16[3,2,128,512]{3,2,1,0:T(8,128)(2,1)S(1)}, bf16[3,2,128,512]{3,2,1,0:T(8,128)(2,1)S(1)}, u32[]{:S(2)}, u32[]{:S(2)}) collective-permute-start(bf16[3,2,128,512]{3,2,1,0:T(8,128)(2,1)S(1)} %collective-permute-done.15.refs_2_), channel_id=1, source_target_pairs={{0,16},{8,24},{16,0},{24,8},{1,17},{9,25},{17,1},{25,9},{2,18},{10... | collective-permute-start | bytes 2359304 | tf_op jit(solution)/shard_map/ppermute | solution.py:22
  100.5 1.7 %shard_map.52.refs_7_ = bf16[3,3,3,2,1,128,512]{6,5,4,3,2,1,0:T(8,128)(2,1)} custom-call(bf16[384,512]{1,0:T(8,128)(2,1)S(1)} %bitcast.55, bf16[384,512]{1,0:T(8,128)(2,1)S(1)} %bitcast.46, bf16[4,2,128,512]{3,2,1,0:T(8,128)(2,1)S(1)} %collective-permute-done.37.refs_2_, ...), custom_call_target="tpu_custom_call", output_to_operand_aliasing={{}: (3, {})} | custom-call | flops 805306368 | bytes 2621440 | tf_op jit(solution)/shard_map/pallas_call | solution.py:248
  102.2 16.3 %collective-permute-done.27.refs_6_ = bf16[128,512]{1,0:T(8,128)(2,1)S(1)} collective-permute-done((bf16[128,512]{1,0:T(8,128)(2,1)S(1)}, bf16[128,512]{1,0:T(8,128)(2,1)S(1)}, u32[]{:S(2)}, u32[]{:S(2)}) %collective-permute-start.27) | collective-permute-done | bytes 131104 | tf_op jit(solution)/shard_map/ppermute | solution.py:22
  118.5 1.8 %shard_map.53 = (bf16[3,3,3,2,1,128,512]{6,5,4,3,2,1,0:T(8,128)(2,1)}, bf16[4,2,128,512]{3,2,1,0:T(8,128)(2,1)S(1)}) custom-call(bf16[384,512]{1,0:T(8,128)(2,1)S(1)} %bitcast.56, bf16[384,512]{1,0:T(8,128)(2,1)S(1)} %bitcast.47, bf16[1,2,128,512]{3,2,1,0:T(8,128)(2,1)S(1)} %bitcast.64, ...), custom_call_target="tpu_custom_call", output_to_operand_aliasing={{0}: (7, {})} | custom-call | flops 805306368 | bytes 2621440 | tf_op jit(solution)/shard_map/pallas_call | solution.py:248
  120.4 1.4 %collective-permute-start.22 = (bf16[128,512]{1,0:T(8,128)(2,1)S(1)}, bf16[128,512]{1,0:T(8,128)(2,1)S(1)}, u32[]{:S(2)}, u32[]{:S(2)}) collective-permute-start(bf16[128,512]{1,0:T(8,128)(2,1)S(1)} %get-tuple-element.50), channel_id=1, source_target_pairs={{0,16},{8,24},{16,0},{24,8},{1,17},{9,25},{17,1},{25,9},{2,18},{10... | collective-permute-start | bytes 393224 | tf_op jit(solution)/shard_map/ppermute | solution.py:22
  122.7 1.7 %collective-permute-start.20 = (bf16[128,512]{1,0:T(8,128)(2,1)S(1)}, bf16[128,512]{1,0:T(8,128)(2,1)S(1)}, u32[]{:S(2)}, u32[]{:S(2)}) collective-permute-start(bf16[128,512]{1,0:T(8,128)(2,1)S(1)} %get-tuple-element.51), channel_id=1, source_target_pairs={{0,16},{8,24},{16,0},{24,8},{1,17},{9,25},{17,1},{25,9},{2,18},{10... | collective-permute-start | bytes 393224 | tf_op jit(solution)/shard_map/ppermute | solution.py:22
  124.6 1.4 %collective-permute-start.18 = (bf16[128,512]{1,0:T(8,128)(2,1)S(1)}, bf16[128,512]{1,0:T(8,128)(2,1)S(1)}, u32[]{:S(2)}, u32[]{:S(2)}) collective-permute-start(bf16[128,512]{1,0:T(8,128)(2,1)S(1)} %get-tuple-element.52), channel_id=1, source_target_pairs={{0,16},{8,24},{16,0},{24,8},{1,17},{9,25},{17,1},{25,9},{2,18},{10... | collective-permute-start | bytes 393224 | tf_op jit(solution)/shard_map/ppermute | solution.py:22
  126.0 1.7 %shard_map.54.refs_7_ = bf16[3,3,3,2,1,128,512]{6,5,4,3,2,1,0:T(8,128)(2,1)} custom-call(bf16[384,512]{1,0:T(8,128)(2,1)S(1)} %bitcast.57, bf16[384,512]{1,0:T(8,128)(2,1)S(1)} %bitcast.48, bf16[4,2,128,512]{3,2,1,0:T(8,128)(2,1)S(1)} %collective-permute-done.38.refs_2_, ...), custom_call_target="tpu_custom_call", output_to_operand_aliasing={{}: (3, {})} | custom-call | flops 805306368 | bytes 2621440 | tf_op jit(solution)/shard_map/pallas_call | solution.py:248
  128.6 1.7 %shard_map.55.refs_7_ = bf16[3,3,3,2,1,128,512]{6,5,4,3,2,1,0:T(8,128)(2,1)} custom-call(bf16[384,512]{1,0:T(8,128)(2,1)S(1)} %bitcast.58, bf16[384,512]{1,0:T(8,128)(2,1)S(1)} %bitcast.49, bf16[3,2,128,512]{3,2,1,0:T(8,128)(2,1)S(1)} %collective-permute-done.15.refs_2_, ...), custom_call_target="tpu_custom_call", output_to_operand_aliasing={{}: (7, {})} | custom-call | flops 805306368 | bytes 2621440 | tf_op jit(solution)/shard_map/pallas_call | solution.py:248
  131.1 1.7 %shard_map.56.refs_7_ = bf16[3,3,3,2,1,128,512]{6,5,4,3,2,1,0:T(8,128)(2,1)} custom-call(bf16[384,512]{1,0:T(8,128)(2,1)S(1)} %bitcast.59, bf16[384,512]{1,0:T(8,128)(2,1)S(1)} %bitcast.50, bf16[3,2,128,512]{3,2,1,0:T(8,128)(2,1)S(1)} %collective-permute-done.15.refs_2_, ...), custom_call_target="tpu_custom_call", output_to_operand_aliasing={{}: (7, {})} | custom-call | flops 805306368 | bytes 2621440 | tf_op jit(solution)/shard_map/pallas_call | solution.py:248
  133.2 1.7 %shard_map.57 = bf16[3,3,3,2,1,128,512]{6,5,4,3,2,1,0:T(8,128)(2,1)} custom-call(bf16[384,512]{1,0:T(8,128)(2,1)S(1)} %bitcast.60, bf16[384,512]{1,0:T(8,128)(2,1)S(1)} %bitcast.51, bf16[3,2,128,512]{3,2,1,0:T(8,128)(2,1)S(1)} %collective-permute-done.15.refs_2_, ...), custom_call_target="tpu_custom_call", output_to_operand_aliasing={{}: (7, {})} | custom-call | flops 805306368 | bytes 2621440 | tf_op jit(solution)/shard_map/pallas_call | solution.py:248
  (75 shorter events, 9.5 us)
Async XLA Ops:
  11.2 10.2 %collective-permute-start.8 = (bf16[2,128,512]{2,1,0:T(8,128)(2,1)S(1)}, bf16[2,128,512]{2,1,0:T(8,128)(2,1)S(1)}, u32[]{:S(2)}, u32[]{:S(2)}) collective-permute-start(bf16[2,128,512]{2,1,0:T(8,128)(2,1)S(1)} %get-tuple-element.38), channel_id=1, source_target_pairs={{0,8},{8,0},{16,24},{24,16},{1,9},{9,1},{17,25},{25,17},{2,10},{10... | collective-permute-start | bytes 786440 | tf_op jit(solution)/shard_map/ppermute | solution.py:22
  14.2 9.3 %collective-permute-start.10 = (bf16[2,128,512]{2,1,0:T(8,128)(2,1)S(1)}, bf16[2,128,512]{2,1,0:T(8,128)(2,1)S(1)}, u32[]{:S(2)}, u32[]{:S(2)}) collective-permute-start(bf16[2,128,512]{2,1,0:T(8,128)(2,1)S(1)} %get-tuple-element.40), channel_id=1, source_target_pairs={{0,16},{8,24},{16,0},{24,8},{1,17},{9,25},{17,1},{25,9},{2,18},{10... | collective-permute-start | bytes 786440 | tf_op jit(solution)/shard_map/ppermute | solution.py:22
  15.8 11.1 %collective-permute-start.4 = (bf16[2,128,512]{2,1,0:T(8,128)(2,1)S(1)}, bf16[2,128,512]{2,1,0:T(8,128)(2,1)S(1)}, u32[]{:S(2)}, u32[]{:S(2)}) collective-permute-start(bf16[2,128,512]{2,1,0:T(8,128)(2,1)S(1)} %get-tuple-element.33), channel_id=1, source_target_pairs={{0,8},{8,0},{16,24},{24,16},{1,9},{9,1},{17,25},{25,17},{2,10},{10... | collective-permute-start | bytes 786440 | tf_op jit(solution)/shard_map/ppermute | solution.py:22
  16.3 12.8 %collective-permute-start.6 = (bf16[2,128,512]{2,1,0:T(8,128)(2,1)S(1)}, bf16[2,128,512]{2,1,0:T(8,128)(2,1)S(1)}, u32[]{:S(2)}, u32[]{:S(2)}) collective-permute-start(bf16[2,128,512]{2,1,0:T(8,128)(2,1)S(1)} %get-tuple-element.35), channel_id=1, source_target_pairs={{0,16},{8,24},{16,0},{24,8},{1,17},{9,25},{17,1},{25,9},{2,18},{10... | collective-permute-start | bytes 786440 | tf_op jit(solution)/shard_map/ppermute | solution.py:22
  16.3 16.3 %collective-permute-start = (bf16[2,128,512]{2,1,0:T(8,128)(2,1)S(1)}, bf16[2,128,512]{2,1,0:T(8,128)(2,1)S(1)}, u32[]{:S(2)}, u32[]{:S(2)}) collective-permute-start(bf16[2,128,512]{2,1,0:T(8,128)(2,1)S(1)} %get-tuple-element.27), channel_id=1, source_target_pairs={{0,8},{8,0},{16,24},{24,16},{1,9},{9,1},{17,25},{25,17},{2,10},{10... | collective-permute-start | bytes 786440 | tf_op jit(solution)/shard_map/ppermute | solution.py:22
  21.4 13.3 %collective-permute-start.2 = (bf16[2,128,512]{2,1,0:T(8,128)(2,1)S(1)}, bf16[2,128,512]{2,1,0:T(8,128)(2,1)S(1)}, u32[]{:S(2)}, u32[]{:S(2)}) collective-permute-start(bf16[2,128,512]{2,1,0:T(8,128)(2,1)S(1)} %get-tuple-element.29), channel_id=1, source_target_pairs={{0,16},{8,24},{16,0},{24,8},{1,17},{9,25},{17,1},{25,9},{2,18},{10... | collective-permute-start | bytes 786440 | tf_op jit(solution)/shard_map/ppermute | solution.py:22
  23.5 13.9 %collective-permute-start.9 = (bf16[1,128,512]{2,1,0:T(8,128)(2,1)S(1)}, bf16[1,128,512]{2,1,0:T(8,128)(2,1)S(1)}, u32[]{:S(2)}, u32[]{:S(2)}) collective-permute-start(bf16[1,128,512]{2,1,0:T(8,128)(2,1)S(1)} %slice.115), channel_id=1, source_target_pairs={{0,16},{8,24},{16,0},{24,8},{1,17},{9,25},{17,1},{25,9},{2,18},{10... | collective-permute-start | bytes 393224 | tf_op jit(solution)/shard_map/ppermute | solution.py:22
  27.0 10.6 %collective-permute-start.11 = (bf16[1,128,512]{2,1,0:T(8,128)(2,1)S(1)}, bf16[1,128,512]{2,1,0:T(8,128)(2,1)S(1)}, u32[]{:S(2)}, u32[]{:S(2)}) collective-permute-start(bf16[1,128,512]{2,1,0:T(8,128)(2,1)S(1)} %slice.117), channel_id=1, source_target_pairs={{0,8},{8,0},{16,24},{24,16},{1,9},{9,1},{17,25},{25,17},{2,10},{10... | collective-permute-start | bytes 393224 | tf_op jit(solution)/shard_map/ppermute | solution.py:22
  29.1 15.0 %collective-permute-start.5 = (bf16[1,128,512]{2,1,0:T(8,128)(2,1)S(1)}, bf16[1,128,512]{2,1,0:T(8,128)(2,1)S(1)}, u32[]{:S(2)}, u32[]{:S(2)}) collective-permute-start(bf16[1,128,512]{2,1,0:T(8,128)(2,1)S(1)} %slice.111), channel_id=1, source_target_pairs={{0,16},{8,24},{16,0},{24,8},{1,17},{9,25},{17,1},{25,9},{2,18},{10... | collective-permute-start | bytes 393224 | tf_op jit(solution)/shard_map/ppermute | solution.py:22
  32.6 11.6 %collective-permute-start.7 = (bf16[1,128,512]{2,1,0:T(8,128)(2,1)S(1)}, bf16[1,128,512]{2,1,0:T(8,128)(2,1)S(1)}, u32[]{:S(2)}, u32[]{:S(2)}) collective-permute-start(bf16[1,128,512]{2,1,0:T(8,128)(2,1)S(1)} %slice.113), channel_id=1, source_target_pairs={{0,8},{8,0},{16,24},{24,16},{1,9},{9,1},{17,25},{25,17},{2,10},{10... | collective-permute-start | bytes 393224 | tf_op jit(solution)/shard_map/ppermute | solution.py:22
  34.7 6.9 %collective-permute-start.1 = (bf16[1,128,512]{2,1,0:T(8,128)(2,1)S(1)}, bf16[1,128,512]{2,1,0:T(8,128)(2,1)S(1)}, u32[]{:S(2)}, u32[]{:S(2)}) collective-permute-start(bf16[1,128,512]{2,1,0:T(8,128)(2,1)S(1)} %slice.107), channel_id=1, source_target_pairs={{0,16},{8,24},{16,0},{24,8},{1,17},{9,25},{17,1},{25,9},{2,18},{10... | collective-permute-start | bytes 393224 | tf_op jit(solution)/shard_map/ppermute | solution.py:22
  37.4 5.0 %collective-permute-start.3 = (bf16[1,128,512]{2,1,0:T(8,128)(2,1)S(1)}, bf16[1,128,512]{2,1,0:T(8,128)(2,1)S(1)}, u32[]{:S(2)}, u32[]{:S(2)}) collective-permute-start(bf16[1,128,512]{2,1,0:T(8,128)(2,1)S(1)} %slice.109), channel_id=1, source_target_pairs={{0,8},{8,0},{16,24},{24,16},{1,9},{9,1},{17,25},{25,17},{2,10},{10... | collective-permute-start | bytes 393224 | tf_op jit(solution)/shard_map/ppermute | solution.py:22
  37.6 19.8 %collective-permute-start.14 = (bf16[2,128,512]{2,1,0:T(8,128)(2,1)S(1)}, bf16[2,128,512]{2,1,0:T(8,128)(2,1)S(1)}, u32[]{:S(2)}, u32[]{:S(2)}) collective-permute-start(bf16[2,128,512]{2,1,0:T(8,128)(2,1)S(1)} %get-tuple-element.65), channel_id=1, source_target_pairs={{0,2},{1,3},{2,4},{3,5},{4,6},{5,7},{6,0},{7,1},{8,10},{9,11},{10,... | collective-permute-start | bytes 786440 | tf_op jit(solution)/shard_map/ppermute | solution.py:17
  42.5 11.0 %collective-permute-start.12 = (bf16[2,128,512]{2,1,0:T(8,128)(2,1)S(1)}, bf16[2,128,512]{2,1,0:T(8,128)(2,1)S(1)}, u32[]{:S(2)}, u32[]{:S(2)}) collective-permute-start(bf16[2,128,512]{2,1,0:T(8,128)(2,1)S(1)} %get-tuple-element.61), channel_id=1, source_target_pairs={{0,2},{1,3},{2,4},{3,5},{4,6},{5,7},{6,0},{7,1},{8,10},{9,11},{10,... | collective-permute-start | bytes 786440 | tf_op jit(solution)/shard_map/ppermute | solution.py:17
  44.2 13.2 %collective-permute-start.13 = (bf16[2,128,512]{2,1,0:T(8,128)(2,1)S(1)}, bf16[2,128,512]{2,1,0:T(8,128)(2,1)S(1)}, u32[]{:S(2)}, u32[]{:S(2)}) collective-permute-start(bf16[2,128,512]{2,1,0:T(8,128)(2,1)S(1)} %get-tuple-element.63), channel_id=1, source_target_pairs={{0,2},{1,3},{2,4},{3,5},{4,6},{5,7},{6,0},{7,1},{8,10},{9,11},{10,... | collective-permute-start | bytes 786440 | tf_op jit(solution)/shard_map/ppermute | solution.py:17
  53.5 6.8 %collective-permute-start.32 = (bf16[1,2,128,512]{3,2,1,0:T(8,128)(2,1)S(1)}, bf16[1,2,128,512]{3,2,1,0:T(8,128)(2,1)S(1)}, u32[]{:S(2)}, u32[]{:S(2)}) collective-permute-start(bf16[1,2,128,512]{3,2,1,0:T(8,128)(2,1)S(1)} %bitcast.69), channel_id=1, source_target_pairs={{0,8},{8,0},{16,24},{24,16},{1,9},{9,1},{17,25},{25,17},{2,10},{10... | collective-permute-start | bytes 786440 | tf_op jit(solution)/shard_map/ppermute | solution.py:22
  55.7 7.4 %collective-permute-start.33 = (bf16[1,2,128,512]{3,2,1,0:T(8,128)(2,1)S(1)}, bf16[1,2,128,512]{3,2,1,0:T(8,128)(2,1)S(1)}, u32[]{:S(2)}, u32[]{:S(2)}) collective-permute-start(bf16[1,2,128,512]{3,2,1,0:T(8,128)(2,1)S(1)} %bitcast.70), channel_id=1, source_target_pairs={{0,16},{8,24},{16,0},{24,8},{1,17},{9,25},{17,1},{25,9},{2,18},{10... | collective-permute-start | bytes 786440 | tf_op jit(solution)/shard_map/ppermute | solution.py:22
  60.3 5.6 %collective-permute-start.34 = (bf16[128,512]{1,0:T(8,128)(2,1)S(1)}, bf16[128,512]{1,0:T(8,128)(2,1)S(1)}, u32[]{:S(2)}, u32[]{:S(2)}) collective-permute-start(bf16[128,512]{1,0:T(8,128)(2,1)S(1)} %slice_bitcast_fusion.1), channel_id=1, source_target_pairs={{0,16},{8,24},{16,0},{24,8},{1,17},{9,25},{17,1},{25,9},{2,18},{10... | collective-permute-start | bytes 393224 | tf_op jit(solution)/shard_map/ppermute | solution.py:22
  63.1 5.2 %collective-permute-start.35 = (bf16[128,512]{1,0:T(8,128)(2,1)S(1)}, bf16[128,512]{1,0:T(8,128)(2,1)S(1)}, u32[]{:S(2)}, u32[]{:S(2)}) collective-permute-start(bf16[128,512]{1,0:T(8,128)(2,1)S(1)} %slice_bitcast_fusion), channel_id=1, source_target_pairs={{0,8},{8,0},{16,24},{24,16},{1,9},{9,1},{17,25},{25,17},{2,10},{10... | collective-permute-start | bytes 393224 | tf_op jit(solution)/shard_map/ppermute | solution.py:22
  70.1 11.0 %collective-permute-start.36 = (bf16[4,2,128,512]{3,2,1,0:T(8,128)(2,1)S(1)}, bf16[4,2,128,512]{3,2,1,0:T(8,128)(2,1)S(1)}, u32[]{:S(2)}, u32[]{:S(2)}) collective-permute-start(bf16[4,2,128,512]{3,2,1,0:T(8,128)(2,1)S(1)} %get-tuple-element.41), channel_id=1, source_target_pairs={{0,1},{1,0},{2,3},{3,2},{4,5},{5,4},{6,7},{7,6},{8,9},{9,8},{10,11... | collective-permute-start | bytes 3145736 | tf_op jit(solution)/shard_map/ppermute | solution.py:22
  70.2 9.0 %collective-permute-start.28 = (bf16[1,2,128,512]{3,2,1,0:T(8,128)(2,1)S(1)}, bf16[1,2,128,512]{3,2,1,0:T(8,128)(2,1)S(1)}, u32[]{:S(2)}, u32[]{:S(2)}) collective-permute-start(bf16[1,2,128,512]{3,2,1,0:T(8,128)(2,1)S(1)} %bitcast.66), channel_id=1, source_target_pairs={{0,8},{8,0},{16,24},{24,16},{1,9},{9,1},{17,25},{25,17},{2,10},{10... | collective-permute-start | bytes 786440 | tf_op jit(solution)/shard_map/ppermute | solution.py:22
  72.3 8.4 %collective-permute-start.29 = (bf16[1,2,128,512]{3,2,1,0:T(8,128)(2,1)S(1)}, bf16[1,2,128,512]{3,2,1,0:T(8,128)(2,1)S(1)}, u32[]{:S(2)}, u32[]{:S(2)}) collective-permute-start(bf16[1,2,128,512]{3,2,1,0:T(8,128)(2,1)S(1)} %bitcast.67), channel_id=1, source_target_pairs={{0,16},{8,24},{16,0},{24,8},{1,17},{9,25},{17,1},{25,9},{2,18},{10... | collective-permute-start | bytes 786440 | tf_op jit(solution)/shard_map/ppermute | solution.py:22
  79.2 5.3 %collective-permute-start.30 = (bf16[128,512]{1,0:T(8,128)(2,1)S(1)}, bf16[128,512]{1,0:T(8,128)(2,1)S(1)}, u32[]{:S(2)}, u32[]{:S(2)}) collective-permute-start(bf16[128,512]{1,0:T(8,128)(2,1)S(1)} %slice_bitcast_fusion.3), channel_id=1, source_target_pairs={{0,16},{8,24},{16,0},{24,8},{1,17},{9,25},{17,1},{25,9},{2,18},{10... | collective-permute-start | bytes 393224 | tf_op jit(solution)/shard_map/ppermute | solution.py:22
  80.7 5.0 %collective-permute-start.31 = (bf16[128,512]{1,0:T(8,128)(2,1)S(1)}, bf16[128,512]{1,0:T(8,128)(2,1)S(1)}, u32[]{:S(2)}, u32[]{:S(2)}) collective-permute-start(bf16[128,512]{1,0:T(8,128)(2,1)S(1)} %slice_bitcast_fusion.2), channel_id=1, source_target_pairs={{0,8},{8,0},{16,24},{24,16},{1,9},{9,1},{17,25},{25,17},{2,10},{10... | collective-permute-start | bytes 393224 | tf_op jit(solution)/shard_map/ppermute | solution.py:22
  81.1 15.9 %collective-permute-start.15 = (bf16[3,2,128,512]{3,2,1,0:T(8,128)(2,1)S(1)}, bf16[3,2,128,512]{3,2,1,0:T(8,128)(2,1)S(1)}, u32[]{:S(2)}, u32[]{:S(2)}) collective-permute-start(bf16[3,2,128,512]{3,2,1,0:T(8,128)(2,1)S(1)} %get-tuple-element.53), channel_id=1, source_target_pairs={{0,1},{1,2},{2,3},{3,4},{4,5},{5,6},{6,7},{7,0},{8,9},{9,10},{10,1... | collective-permute-start | bytes 2359304 | tf_op jit(solution)/shard_map/ppermute | solution.py:17
  87.5 13.0 %collective-permute-start.37 = (bf16[4,2,128,512]{3,2,1,0:T(8,128)(2,1)S(1)}, bf16[4,2,128,512]{3,2,1,0:T(8,128)(2,1)S(1)}, u32[]{:S(2)}, u32[]{:S(2)}) collective-permute-start(bf16[4,2,128,512]{3,2,1,0:T(8,128)(2,1)S(1)} %get-tuple-element.43), channel_id=1, source_target_pairs={{0,1},{1,0},{2,3},{3,2},{4,5},{5,4},{6,7},{7,6},{8,9},{9,8},{10,11... | collective-permute-start | bytes 3145736 | tf_op jit(solution)/shard_map/ppermute | solution.py:22
  87.5 8.7 %collective-permute-start.24 = (bf16[1,2,128,512]{3,2,1,0:T(8,128)(2,1)S(1)}, bf16[1,2,128,512]{3,2,1,0:T(8,128)(2,1)S(1)}, u32[]{:S(2)}, u32[]{:S(2)}) collective-permute-start(bf16[1,2,128,512]{3,2,1,0:T(8,128)(2,1)S(1)} %bitcast.62), channel_id=1, source_target_pairs={{0,8},{8,0},{16,24},{24,16},{1,9},{9,1},{17,25},{25,17},{2,10},{10... | collective-permute-start | bytes 786440 | tf_op jit(solution)/shard_map/ppermute | solution.py:22
  88.0 10.7 %collective-permute-start.25 = (bf16[1,2,128,512]{3,2,1,0:T(8,128)(2,1)S(1)}, bf16[1,2,128,512]{3,2,1,0:T(8,128)(2,1)S(1)}, u32[]{:S(2)}, u32[]{:S(2)}) collective-permute-start(bf16[1,2,128,512]{3,2,1,0:T(8,128)(2,1)S(1)} %bitcast.63), channel_id=1, source_target_pairs={{0,16},{8,24},{16,0},{24,8},{1,17},{9,25},{17,1},{25,9},{2,18},{10... | collective-permute-start | bytes 786440 | tf_op jit(solution)/shard_map/ppermute | solution.py:22
  96.3 6.0 %collective-permute-start.26 = (bf16[128,512]{1,0:T(8,128)(2,1)S(1)}, bf16[128,512]{1,0:T(8,128)(2,1)S(1)}, u32[]{:S(2)}, u32[]{:S(2)}) collective-permute-start(bf16[128,512]{1,0:T(8,128)(2,1)S(1)} %slice_bitcast_fusion.5), channel_id=1, source_target_pairs={{0,16},{8,24},{16,0},{24,8},{1,17},{9,25},{17,1},{25,9},{2,18},{10... | collective-permute-start | bytes 393224 | tf_op jit(solution)/shard_map/ppermute | solution.py:22
  97.0 23.4 %collective-permute-start.16 = (bf16[3,2,128,512]{3,2,1,0:T(8,128)(2,1)S(1)}, bf16[3,2,128,512]{3,2,1,0:T(8,128)(2,1)S(1)}, u32[]{:S(2)}, u32[]{:S(2)}) collective-permute-start(bf16[3,2,128,512]{3,2,1,0:T(8,128)(2,1)S(1)} %collective-permute-done.15.refs_2_), channel_id=1, source_target_pairs={{0,8},{8,0},{16,24},{24,16},{1,9},{9,1},{17,25},{25,17},{2,10},{10... | collective-permute-start | bytes 2359304 | tf_op jit(solution)/shard_map/ppermute | solution.py:22
  98.7 19.8 %collective-permute-start.27 = (bf16[128,512]{1,0:T(8,128)(2,1)S(1)}, bf16[128,512]{1,0:T(8,128)(2,1)S(1)}, u32[]{:S(2)}, u32[]{:S(2)}) collective-permute-start(bf16[128,512]{1,0:T(8,128)(2,1)S(1)} %slice_bitcast_fusion.4), channel_id=1, source_target_pairs={{0,8},{8,0},{16,24},{24,16},{1,9},{9,1},{17,25},{25,17},{2,10},{10... | collective-permute-start | bytes 393224 | tf_op jit(solution)/shard_map/ppermute | solution.py:22
  99.1 22.8 %collective-permute-start.17 = (bf16[3,2,128,512]{3,2,1,0:T(8,128)(2,1)S(1)}, bf16[3,2,128,512]{3,2,1,0:T(8,128)(2,1)S(1)}, u32[]{:S(2)}, u32[]{:S(2)}) collective-permute-start(bf16[3,2,128,512]{3,2,1,0:T(8,128)(2,1)S(1)} %collective-permute-done.15.refs_2_), channel_id=1, source_target_pairs={{0,16},{8,24},{16,0},{24,8},{1,17},{9,25},{17,1},{25,9},{2,18},{10... | collective-permute-start | bytes 2359304 | tf_op jit(solution)/shard_map/ppermute | solution.py:22
  120.3 4.3 %collective-permute-start.38 = (bf16[4,2,128,512]{3,2,1,0:T(8,128)(2,1)S(1)}, bf16[4,2,128,512]{3,2,1,0:T(8,128)(2,1)S(1)}, u32[]{:S(2)}, u32[]{:S(2)}) collective-permute-start(bf16[4,2,128,512]{3,2,1,0:T(8,128)(2,1)S(1)} %get-tuple-element.45), channel_id=1, source_target_pairs={{0,1},{1,0},{2,3},{3,2},{4,5},{5,4},{6,7},{7,6},{8,9},{9,8},{10,11... | collective-permute-start | bytes 3145736 | tf_op jit(solution)/shard_map/ppermute | solution.py:22
  120.4 7.3 %collective-permute-start.22 = (bf16[128,512]{1,0:T(8,128)(2,1)S(1)}, bf16[128,512]{1,0:T(8,128)(2,1)S(1)}, u32[]{:S(2)}, u32[]{:S(2)}) collective-permute-start(bf16[128,512]{1,0:T(8,128)(2,1)S(1)} %get-tuple-element.50), channel_id=1, source_target_pairs={{0,16},{8,24},{16,0},{24,8},{1,17},{9,25},{17,1},{25,9},{2,18},{10... | collective-permute-start | bytes 393224 | tf_op jit(solution)/shard_map/ppermute | solution.py:22
  121.9 6.7 %collective-permute-start.23 = (bf16[128,512]{1,0:T(8,128)(2,1)S(1)}, bf16[128,512]{1,0:T(8,128)(2,1)S(1)}, u32[]{:S(2)}, u32[]{:S(2)}) collective-permute-start(bf16[128,512]{1,0:T(8,128)(2,1)S(1)} %get-tuple-element.47), channel_id=1, source_target_pairs={{0,8},{8,0},{16,24},{24,16},{1,9},{9,1},{17,25},{25,17},{2,10},{10... | collective-permute-start | bytes 393224 | tf_op jit(solution)/shard_map/ppermute | solution.py:22
  122.7 7.7 %collective-permute-start.20 = (bf16[128,512]{1,0:T(8,128)(2,1)S(1)}, bf16[128,512]{1,0:T(8,128)(2,1)S(1)}, u32[]{:S(2)}, u32[]{:S(2)}) collective-permute-start(bf16[128,512]{1,0:T(8,128)(2,1)S(1)} %get-tuple-element.51), channel_id=1, source_target_pairs={{0,16},{8,24},{16,0},{24,8},{1,17},{9,25},{17,1},{25,9},{2,18},{10... | collective-permute-start | bytes 393224 | tf_op jit(solution)/shard_map/ppermute | solution.py:22
  124.3 6.8 %collective-permute-start.21 = (bf16[128,512]{1,0:T(8,128)(2,1)S(1)}, bf16[128,512]{1,0:T(8,128)(2,1)S(1)}, u32[]{:S(2)}, u32[]{:S(2)}) collective-permute-start(bf16[128,512]{1,0:T(8,128)(2,1)S(1)} %get-tuple-element.48), channel_id=1, source_target_pairs={{0,8},{8,0},{16,24},{24,16},{1,9},{9,1},{17,25},{25,17},{2,10},{10... | collective-permute-start | bytes 393224 | tf_op jit(solution)/shard_map/ppermute | solution.py:22
  124.6 8.2 %collective-permute-start.18 = (bf16[128,512]{1,0:T(8,128)(2,1)S(1)}, bf16[128,512]{1,0:T(8,128)(2,1)S(1)}, u32[]{:S(2)}, u32[]{:S(2)}) collective-permute-start(bf16[128,512]{1,0:T(8,128)(2,1)S(1)} %get-tuple-element.52), channel_id=1, source_target_pairs={{0,16},{8,24},{16,0},{24,8},{1,17},{9,25},{17,1},{25,9},{2,18},{10... | collective-permute-start | bytes 393224 | tf_op jit(solution)/shard_map/ppermute | solution.py:22
  127.8 5.4 %collective-permute-start.19 = (bf16[128,512]{1,0:T(8,128)(2,1)S(1)}, bf16[128,512]{1,0:T(8,128)(2,1)S(1)}, u32[]{:S(2)}, u32[]{:S(2)}) collective-permute-start(bf16[128,512]{1,0:T(8,128)(2,1)S(1)} %get-tuple-element.49), channel_id=1, source_target_pairs={{0,8},{8,0},{16,24},{24,16},{1,9},{9,1},{17,25},{25,17},{2,10},{10... | collective-permute-start | bytes 393224 | tf_op jit(solution)/shard_map/ppermute | solution.py:22

commit v2 on v1

--- a/solution.py
+++ b/solution.py
@@ -65,7 +65,9 @@
                     prop_hbm.at[source + 1, part, 0], following.at[part], sems.at[4 + part]
                 )
             )
-    for copy in index_copies + copies:
+    ahead = copies[-2:] if not last else []
+    copies = copies[: len(copies) - len(ahead)]
+    for copy in copies + index_copies:
         copy.start()
     section = lax.axis_index("sec")
     depth, order = sink.shape[1:]
@@ -79,9 +81,13 @@
             sink[part] = jnp.where(live, raw[part], jnp.zeros((depth, order), jnp.bfloat16))
             copies.pop(0).wait()
             if part == 0:
+                for copy in ahead:
+                    copy.start()
                 start = over_rows(sink[0], prop[0])
         real[...] = ((start + over_rows(sink[1], prop[1])) * sign).astype(jnp.bfloat16)
     else:
+        for copy in ahead:
+            copy.start()
         real[...] = (
             (over_rows(sink[0], prop[0]) + over_rows(sink[1], prop[1])) * sign
         ).astype(jnp.bfloat16)
@@ -96,7 +102,7 @@
         slot = reversed_bits(q, width)
         (keep_real if slot < half else send_real)[slot % half] = real[window, :]
         (keep_imag if q < half else send_imag)[q % half] = imag[window, :]
-    for copy in copies:
+    for copy in ahead:
         copy.wait()
 
 
@@ -137,7 +143,7 @@
             out_specs=[in_vmem] * len(outs),
             out_shape=outs,
             scratch_shapes=scratch,
-            compiler_params=pltpu.CompilerParams(vmem_limit_bytes=24 << 20),
+            compiler_params=pltpu.CompilerParams(vmem_limit_bytes=12 << 20),
             cost_estimate=pl.CostEstimate(
                 flops=8 * order * depth * columns,
                 bytes_accessed=4 * depth * columns,
@@ -151,18 +157,23 @@
     return halves
 
 
+def added(kept, got):
+    return (kept.astype(jnp.float32) + got.astype(jnp.float32)).astype(jnp.bfloat16)
+
+
 def reduced(keep_real, send_real, keep_imag, send_imag, width):
     for step in range(width):
         got_real = exchanged(send_real, "sec", 1 << step)
         got_imag = exchanged(send_imag, "sec", 1 << (width - 1 - step))
-        real = keep_real.astype(jnp.float32) + got_real.astype(jnp.float32)
-        imag = keep_imag.astype(jnp.float32) + got_imag.astype(jnp.float32)
-        real, imag = real.astype(jnp.bfloat16), imag.astype(jnp.bfloat16)
+        if step == width - 1:
+            real = added(keep_real, got_real)
+            imag = added(keep_imag, got_imag)
+            return jnp.concatenate((real, imag), 0)
+        real = added(keep_real, got_real)
+        imag = added(keep_imag, got_imag)
         half = real.shape[0] // 2
-        if half:
-            keep_real, send_real = real[:half], real[half:]
-            keep_imag, send_imag = imag[:half], imag[half:]
-    return jnp.concatenate((real, imag), 0)
+        keep_real, send_real = real[:half], real[half:]
+        keep_imag, send_imag = imag[:half], imag[half:]
 
 
 def gathered(own, width):
@@ -179,11 +190,10 @@
                 places[s].append(((whole[q], (s, 0)), (whole[q], (s, 1))))
                 continue
             (first, at_first), (second, at_second) = places[s][q ^ high][0], places[s][q ^ low][1]
+            real = first[at_first]
+            imag = second[at_second]
             places[s].append(
-                (
-                    (exchanged(first[at_first], "sec", high), ()),
-                    (exchanged(second[at_second], "sec", low), ()),
-                )
+                ((exchanged(real, "sec", high), ()), (exchanged(imag, "sec", low), ()))
             )
     return places
 
@@ -270,23 +280,31 @@
 def body(sink_vectors, propagators, live_rows, source_times):
     sections = lax.axis_size("sec")
     width = sections.bit_length() - 1
-    section = lax.axis_index("sec")
-    first_core = lax.axis_index("ta") % 2 == 0
     sources = propagators.shape[0]
     order = sink_vectors.shape[3]
     rows = order // sections
+    section = lax.axis_index("sec").astype(jnp.uint32)
+    first_core = lax.axis_index("ta").astype(jnp.uint32) & 1 == 0
+    offsets = [(section ^ q) * jnp.uint32(rows) for q in range(sections)]
+    sink_vectors, first_core, offsets = lax.optimization_barrier(
+        (sink_vectors, first_core, offsets)
+    )
 
     halves = products(live_rows, source_times, sink_vectors, propagators, sections)
     own = [reduced(*halves[s], width) for s in range(sources)]
     second = [shifted(own[s], 2) for s in range(sources)]
-    mine, theirs = jnp.stack(own), jnp.stack(second)
-    other = shifted(jnp.where(first_core, mine, theirs), 1)
-
-    left = jnp.swapaxes(mine, 0, 1)
+    groups = ((0,), tuple(range(1, sources)))
+    other = []
+    for group in groups:
+        chosen = jnp.stack([jnp.where(first_core, own[s], second[s]) for s in group])
+        other.append(shifted(chosen, 1))
+
+    left = jnp.stack(own, 1)
+    zero = jnp.uint32(0)
     left = jnp.concatenate(
         [
-            lax.dynamic_slice_in_dim(left, (section ^ q) * rows, rows, axis=3)
-            for q in range(sections)
+            lax.dynamic_slice(left, (zero, zero, zero, offset), (2, sources, rows, rows))
+            for offset in offsets
         ],
         3,
     ).reshape(2, sources * rows, order)
@@ -294,14 +312,30 @@
 
     shape = (STOPS, sources, sources, 2, 1, rows, order)
     result = None
-    for s in range(sources):
+    swapped = {}
+
+    def far(result, s):
         (places,) = gathered(second[s][None], width)
         result, together = sandwich(result, 1, s, left_real, left_imag, places, shape, True)
-        together = exchanged(together, "ta", 1)
-        places = [tuple((together, (q, part)) for part in range(2)) for q in range(sections)]
-        (result,) = sandwich(result, 0, s, left_real, left_imag, places, shape)
-    for s, places in enumerate(gathered(other, width)):
-        (result,) = sandwich(result, 2, s, left_real, left_imag, places, shape)
+        swapped[s] = exchanged(together, "ta", 1)
+        return result
+
+    def near(result, s):
+        places = [
+            tuple((swapped[s], (q, part)) for part in range(2)) for q in range(sections)
+        ]
+        return sandwich(result, 0, s, left_real, left_imag, places, shape)[0]
+
+    for s in range(sources):
+        result = far(result, s)
+        if 0 < s < sources - 1:
+            result = near(result, s - 1)
+            if s == sources - 2:
+                result = near(result, s)
+    result = near(result, sources - 1)
+    for i, group in enumerate(groups):
+        for s, places in zip(group, gathered(other[i], width)):
+            (result,) = sandwich(result, 2, s, left_real, left_imag, places, shape)
     return result
 
 

time: 135 us -> 116 us (0.86)
  waiting for transfers between devices: 56.8 us -> 39.7 us
  starting transfers between devices: 49.5 us -> 47.3 us
    ppermute x35 -> x37, waiting for transfers between devices: 49.1 us -> 32.2 us  [exchanged(): lax.ppermute(value, axis, [(source, source ^ bit) for source in range(cou...]
    ppermute x35 -> x37, starting transfers between devices: 44.1 us -> 42.5 us  [exchanged(): lax.ppermute(value, axis, [(source, source ^ bit) for source in range(cou...]
    ppermute x4 -> x5, starting transfers between devices: 5.35 us -> 4.82 us  [shifted(): return lax.ppermute(value, 'ta', pairs)]
    ppermute x4 -> x5, waiting for transfers between devices: 7.63 us -> 7.51 us  [shifted(): return lax.ppermute(value, 'ta', pairs)]
  transfers between devices with their start and end apart: 39 -> 42, of which waited for: 19 -> 15; matrix products, arithmetic and copies ran while one was open for 1% -> 1% of each run, Pallas kernels for 9% -> 18%
where the time goes in v2:
time: 116 us
  starting transfers between devices  47.3 us (41%)
  waiting for transfers between devices  39.7 us (34%)
  Pallas kernels  26.8 us (23%)
    ppermute x37, starting transfers between devices, exchanged(): lax.ppermute(value, axis, [(source, source ^ bit) for source in range(cou...  42.5 us
    ppermute x37, waiting for transfers between devices, exchanged(): lax.ppermute(value, axis, [(source, source ^ bit) for source in range(cou...  32.2 us
    pallas_call x9, Pallas kernels, sandwich(): pl.pallas_call(functools.partial(sandwich_kernel, 0.5 * order ** (-0.5),...  15.7 us
    pallas_call x3, Pallas kernels, products(): pl.pallas_call(functools.partial(product_kernel, sections, source, source...  11.1 us
    ppermute x5, waiting for transfers between devices, shifted(): return lax.ppermute(value, 'ta', pairs)  7.51 us
    ppermute x5, starting transfers between devices, shifted(): return lax.ppermute(value, 'ta', pairs)  4.82 us
  transfers between devices with their start and end apart: 42, of which 15 were waited for; matrix products, arithmetic and copies ran while one was open for 1% of the time, Pallas kernels for 18%

profile of v2, /device:TPU:0, one launch (start us, length us, event | category | flops | bytes accessed | tf_op | source)
XLA Modules:
  0.0 116.1 jit_solution(9143038432772769109)
XLA Ops:
  0.0 4.7 %shard_map.46 = (bf16[2,128,512]{2,1,0:T(8,128)(2,1)S(1)}, bf16[2,128,512]{2,1,0:T(8,128)(2,1)S(1)}, bf16[2,128,512]{2,1,0:T(8,128)(2,1)S(1)}, bf16[2,128,512]{2...) custom-call(s32[4]{0:T(128)} %refs_0_.3, s32[3]{0:T(128)} %refs_0_.5, ...), custom_call_target="tpu_custom_call" | custom-call | flops 2147483648 | bytes 2097152 | tf_op jit(solution)/shard_map/pallas_call | solution.py:140
  4.7 3.0 %collective-permute-start = (bf16[2,128,512]{2,1,0:T(8,128)(2,1)S(1)}, bf16[2,128,512]{2,1,0:T(8,128)(2,1)S(1)}, u32[]{:S(2)}, u32[]{:S(2)}) collective-permute-start(bf16[2,128,512]{2,1,0:T(8,128)(2,1)S(1)} %get-tuple-element.34), channel_id=1, source_target_pairs={{0,8},{8,0},{16,24},{24,16},{1,9},{9,1},{17,25},{25,17},{2,10},{10... | collective-permute-start | bytes 786440 | tf_op jit(solution)/shard_map/ppermute | solution.py:22
  7.7 1.6 %collective-permute-start.2 = (bf16[2,128,512]{2,1,0:T(8,128)(2,1)S(1)}, bf16[2,128,512]{2,1,0:T(8,128)(2,1)S(1)}, u32[]{:S(2)}, u32[]{:S(2)}) collective-permute-start(bf16[2,128,512]{2,1,0:T(8,128)(2,1)S(1)} %get-tuple-element.36), channel_id=1, source_target_pairs={{0,16},{8,24},{16,0},{24,8},{1,17},{9,25},{17,1},{25,9},{2,18},{10... | collective-permute-start | bytes 786440 | tf_op jit(solution)/shard_map/ppermute | solution.py:22
  9.3 3.3 %shard_map.47 = (bf16[2,128,512]{2,1,0:T(8,128)(2,1)S(1)}, bf16[2,128,512]{2,1,0:T(8,128)(2,1)S(1)}, bf16[2,128,512]{2,1,0:T(8,128)(2,1)S(1)}, bf16[2,128,512]{2,1,0:T(8,128)(2,1)S(1)}, bf16[2,1024,512]{2,1,0:T(8,128)(2,1)S(1)}) custom-call(s32[3]{0:T(128)} %refs_0_.5, bf16[2,1024,512]{2,1,0:T(8,128)(2,1)S(1)} %get-tuple-element.37.refs_1_, ...), custom_call_target="tpu_custom_call" | custom-call | flops 2147483648 | bytes 2097152 | tf_op jit(solution)/shard_map/pallas_call | solution.py:140
  13.2 3.2 %shard_map.48 = (bf16[2,128,512]{2,1,0:T(8,128)(2,1)S(1)}, bf16[2,128,512]{2,1,0:T(8,128)(2,1)S(1)}, bf16[2,128,512]{2,1,0:T(8,128)(2,1)S(1)}, bf16[2,128,512]{2,1,0:T(8,128)(2,1)S(1)}) custom-call(s32[3]{0:T(128)} %refs_0_.5, bf16[2,1024,512]{2,1,0:T(8,128)(2,1)S(1)} %get-tuple-element.37.refs_1_, bf16[2,1024,512]{2,1,0:T(8,128)(2,1)S(1)} %get-tuple-element.43.refs_2_, ...), custom_call_target="tpu_custom_call" | custom-call | flops 2147483648 | bytes 2097152 | tf_op jit(solution)/shard_map/pallas_call | solution.py:140
  16.3 2.0 %collective-permute-start.8 = (bf16[2,128,512]{2,1,0:T(8,128)(2,1)S(1)}, bf16[2,128,512]{2,1,0:T(8,128)(2,1)S(1)}, u32[]{:S(2)}, u32[]{:S(2)}) collective-permute-start(bf16[2,128,512]{2,1,0:T(8,128)(2,1)S(1)} %get-tuple-element.45), channel_id=1, source_target_pairs={{0,8},{8,0},{16,24},{24,16},{1,9},{9,1},{17,25},{25,17},{2,10},{10... | collective-permute-start | bytes 786440 | tf_op jit(solution)/shard_map/ppermute | solution.py:22
  18.3 1.6 %collective-permute-start.10 = (bf16[2,128,512]{2,1,0:T(8,128)(2,1)S(1)}, bf16[2,128,512]{2,1,0:T(8,128)(2,1)S(1)}, u32[]{:S(2)}, u32[]{:S(2)}) collective-permute-start(bf16[2,128,512]{2,1,0:T(8,128)(2,1)S(1)} %get-tuple-element.47), channel_id=1, source_target_pairs={{0,16},{8,24},{16,0},{24,8},{1,17},{9,25},{17,1},{25,9},{2,18},{10... | collective-permute-start | bytes 786440 | tf_op jit(solution)/shard_map/ppermute | solution.py:22
  20.6 1.2 %collective-permute-done.4 = bf16[2,128,512]{2,1,0:T(8,128)(2,1)S(1)} collective-permute-done((bf16[2,128,512]{2,1,0:T(8,128)(2,1)S(1)}, bf16[2,128,512]{2,1,0:T(8,128)(2,1)S(1)}, u32[]{:S(2)}, u32[]{:S(2)}) %collective-permute-start.4) | collective-permute-done | bytes 262176 | tf_op jit(solution)/shard_map/ppermute | solution.py:22
  22.4 1.9 %collective-permute-start.5 = (bf16[1,128,512]{2,1,0:T(8,128)(2,1)S(1)}, bf16[1,128,512]{2,1,0:T(8,128)(2,1)S(1)}, u32[]{:S(2)}, u32[]{:S(2)}) collective-permute-start(bf16[1,128,512]{2,1,0:T(8,128)(2,1)S(1)} %slice.111), channel_id=1, source_target_pairs={{0,16},{8,24},{16,0},{24,8},{1,17},{9,25},{17,1},{25,9},{2,18},{10... | collective-permute-start | bytes 393224 | tf_op jit(solution)/shard_map/ppermute | solution.py:22
  24.3 2.8 %collective-permute-done.8 = bf16[2,128,512]{2,1,0:T(8,128)(2,1)S(1)} collective-permute-done((bf16[2,128,512]{2,1,0:T(8,128)(2,1)S(1)}, bf16[2,128,512]{2,1,0:T(8,128)(2,1)S(1)}, u32[]{:S(2)}, u32[]{:S(2)}) %collective-permute-start.8) | collective-permute-done | bytes 262176 | tf_op jit(solution)/shard_map/ppermute | solution.py:22
  28.0 1.9 %collective-permute-start.9 = (bf16[1,128,512]{2,1,0:T(8,128)(2,1)S(1)}, bf16[1,128,512]{2,1,0:T(8,128)(2,1)S(1)}, u32[]{:S(2)}, u32[]{:S(2)}) collective-permute-start(bf16[1,128,512]{2,1,0:T(8,128)(2,1)S(1)} %slice.115), channel_id=1, source_target_pairs={{0,16},{8,24},{16,0},{24,8},{1,17},{9,25},{17,1},{25,9},{2,18},{10... | collective-permute-start | bytes 393224 | tf_op jit(solution)/shard_map/ppermute | solution.py:22
  30.7 1.5 %collective-permute-start.11 = (bf16[1,128,512]{2,1,0:T(8,128)(2,1)S(1)}, bf16[1,128,512]{2,1,0:T(8,128)(2,1)S(1)}, u32[]{:S(2)}, u32[]{:S(2)}) collective-permute-start(bf16[1,128,512]{2,1,0:T(8,128)(2,1)S(1)} %slice.117), channel_id=1, source_target_pairs={{0,8},{8,0},{16,24},{24,16},{1,9},{9,1},{17,25},{25,17},{2,10},{10... | collective-permute-start | bytes 393224 | tf_op jit(solution)/shard_map/ppermute | solution.py:22
  32.4 1.6 %collective-permute-start.21 = (bf16[2,128,512]{2,1,0:T(8,128)(2,1)S(1)}, bf16[2,128,512]{2,1,0:T(8,128)(2,1)S(1)}, u32[]{:S(2)}, u32[]{:S(2)}) collective-permute-start(bf16[2,128,512]{2,1,0:T(8,128)(2,1)S(1)} %pad_maximum_fusion.3), channel_id=1, source_target_pairs={{0,2},{1,3},{2,4},{3,5},{4,6},{5,7},{6,0},{7,1},{8,10},{9,11},{10,... | collective-permute-start | bytes 786440 | tf_op jit(solution)/shard_map/ppermute | solution.py:17
  34.1 1.6 %collective-permute-start.12 = (bf16[2,128,512]{2,1,0:T(8,128)(2,1)S(1)}, bf16[2,128,512]{2,1,0:T(8,128)(2,1)S(1)}, u32[]{:S(2)}, u32[]{:S(2)}) collective-permute-start(bf16[2,128,512]{2,1,0:T(8,128)(2,1)S(1)} %pad_maximum_fusion.4), channel_id=1, source_target_pairs={{0,2},{1,3},{2,4},{3,5},{4,6},{5,7},{6,0},{7,1},{8,10},{9,11},{10,... | collective-permute-start | bytes 786440 | tf_op jit(solution)/shard_map/ppermute | solution.py:17
  35.8 1.6 %collective-permute-start.13 = (bf16[2,128,512]{2,1,0:T(8,128)(2,1)S(1)}, bf16[2,128,512]{2,1,0:T(8,128)(2,1)S(1)}, u32[]{:S(2)}, u32[]{:S(2)}) collective-permute-start(bf16[2,128,512]{2,1,0:T(8,128)(2,1)S(1)} %pad_maximum_fusion.5), channel_id=1, source_target_pairs={{0,2},{1,3},{2,4},{3,5},{4,6},{5,7},{6,0},{7,1},{8,10},{9,11},{10,... | collective-permute-start | bytes 786440 | tf_op jit(solution)/shard_map/ppermute | solution.py:17
  37.4 6.0 %collective-permute-done.21 = bf16[2,128,512]{2,1,0:T(8,128)(2,1)S(1)} collective-permute-done((bf16[2,128,512]{2,1,0:T(8,128)(2,1)S(1)}, bf16[2,128,512]{2,1,0:T(8,128)(2,1)S(1)}, u32[]{:S(2)}, u32[]{:S(2)}) %collective-permute-start.21) | collective-permute-done | bytes 262176 | tf_op jit(solution)/shard_map/ppermute | solution.py:17
  43.9 1.8 %collective-permute-start.36 = (bf16[1,2,128,512]{3,2,1,0:T(8,128)(2,1)S(1)}, bf16[1,2,128,512]{3,2,1,0:T(8,128)(2,1)S(1)}, u32[]{:S(2)}, u32[]{:S(2)}) collective-permute-start(bf16[1,2,128,512]{3,2,1,0:T(8,128)(2,1)S(1)} %bitcast.66), channel_id=1, source_target_pairs={{0,16},{8,24},{16,0},{24,8},{1,17},{9,25},{17,1},{25,9},{2,18},{10... | collective-permute-start | bytes 786440 | tf_op jit(solution)/shard_map/ppermute | solution.py:22
  45.7 1.5 %collective-permute-done.12 = bf16[2,128,512]{2,1,0:T(8,128)(2,1)S(1)} collective-permute-done((bf16[2,128,512]{2,1,0:T(8,128)(2,1)S(1)}, bf16[2,128,512]{2,1,0:T(8,128)(2,1)S(1)}, u32[]{:S(2)}, u32[]{:S(2)}) %collective-permute-start.12) | collective-permute-done | bytes 262176 | tf_op jit(solution)/shard_map/ppermute | solution.py:17
  47.1 1.7 %collective-permute-start.31 = (bf16[1,2,128,512]{3,2,1,0:T(8,128)(2,1)S(1)}, bf16[1,2,128,512]{3,2,1,0:T(8,128)(2,1)S(1)}, u32[]{:S(2)}, u32[]{:S(2)}) collective-permute-start(bf16[1,2,128,512]{3,2,1,0:T(8,128)(2,1)S(1)} %bitcast.62), channel_id=1, source_target_pairs={{0,8},{8,0},{16,24},{24,16},{1,9},{9,1},{17,25},{25,17},{2,10},{10... | collective-permute-start | bytes 786440 | tf_op jit(solution)/shard_map/ppermute | solution.py:22
  48.9 1.3 %collective-permute-start.32 = (bf16[1,2,128,512]{3,2,1,0:T(8,128)(2,1)S(1)}, bf16[1,2,128,512]{3,2,1,0:T(8,128)(2,1)S(1)}, u32[]{:S(2)}, u32[]{:S(2)}) collective-permute-start(bf16[1,2,128,512]{3,2,1,0:T(8,128)(2,1)S(1)} %bitcast.63), channel_id=1, source_target_pairs={{0,16},{8,24},{16,0},{24,8},{1,17},{9,25},{17,1},{25,9},{2,18},{10... | collective-permute-start | bytes 786440 | tf_op jit(solution)/shard_map/ppermute | solution.py:22
  50.9 1.6 %collective-permute-start.37 = (bf16[128,512]{1,0:T(8,128)(2,1)S(1)}, bf16[128,512]{1,0:T(8,128)(2,1)S(1)}, u32[]{:S(2)}, u32[]{:S(2)}) collective-permute-start(bf16[128,512]{1,0:T(8,128)(2,1)S(1)} %slice_bitcast_fusion.1), channel_id=1, source_target_pairs={{0,16},{8,24},{16,0},{24,8},{1,17},{9,25},{17,1},{25,9},{2,18},{10... | collective-permute-start | bytes 393224 | tf_op jit(solution)/shard_map/ppermute | solution.py:22
  52.5 1.3 %collective-permute-start.38 = (bf16[128,512]{1,0:T(8,128)(2,1)S(1)}, bf16[128,512]{1,0:T(8,128)(2,1)S(1)}, u32[]{:S(2)}, u32[]{:S(2)}) collective-permute-start(bf16[128,512]{1,0:T(8,128)(2,1)S(1)} %slice_bitcast_fusion), channel_id=1, source_target_pairs={{0,8},{8,0},{16,24},{24,16},{1,9},{9,1},{17,25},{25,17},{2,10},{10... | collective-permute-start | bytes 393224 | tf_op jit(solution)/shard_map/ppermute | solution.py:22
  53.8 1.6 %collective-permute-done.31.refs_3_ = bf16[1,2,128,512]{3,2,1,0:T(8,128)(2,1)S(1)} collective-permute-done((bf16[1,2,128,512]{3,2,1,0:T(8,128)(2,1)S(1)}, bf16[1,2,128,512]{3,2,1,0:T(8,128)(2,1)S(1)}, u32[]{:S(2)}, u32[]{:S(2)}) %collective-permute-start.31) | collective-permute-done | bytes 262176 | tf_op jit(solution)/shard_map/ppermute | solution.py:22
  55.4 2.3 %collective-permute-start.33 = (bf16[128,512]{1,0:T(8,128)(2,1)S(1)}, bf16[128,512]{1,0:T(8,128)(2,1)S(1)}, u32[]{:S(2)}, u32[]{:S(2)}) collective-permute-start(bf16[128,512]{1,0:T(8,128)(2,1)S(1)} %slice_bitcast_fusion.3), channel_id=1, source_target_pairs={{0,16},{8,24},{16,0},{24,8},{1,17},{9,25},{17,1},{25,9},{2,18},{10... | collective-permute-start | bytes 393224 | tf_op jit(solution)/shard_map/ppermute | solution.py:22
  57.7 1.5 %collective-permute-start.34 = (bf16[128,512]{1,0:T(8,128)(2,1)S(1)}, bf16[128,512]{1,0:T(8,128)(2,1)S(1)}, u32[]{:S(2)}, u32[]{:S(2)}) collective-permute-start(bf16[128,512]{1,0:T(8,128)(2,1)S(1)} %slice_bitcast_fusion.2), channel_id=1, source_target_pairs={{0,8},{8,0},{16,24},{24,16},{1,9},{9,1},{17,25},{25,17},{2,10},{10... | collective-permute-start | bytes 393224 | tf_op jit(solution)/shard_map/ppermute | solution.py:22
  59.4 1.8 %shard_map.49 = (bf16[3,3,3,2,1,128,512]{6,5,4,3,2,1,0:T(8,128)(2,1)}, bf16[4,2,128,512]{3,2,1,0:T(8,128)(2,1)S(1)}) custom-call(bf16[384,512]{1,0:T(8,128)(2,1)S(1)} %bitcast.50, bf16[384,512]{1,0:T(8,128)(2,1)S(1)} %bitcast.41, bf16[1,2,128,512]{3,2,1,0:T(8,128)(2,1)S(1)} %bitcast.67, bf16[1,2,128,512]{3,2,1,0:T(8,128)(2,1)S(1)} %collective-permute-done.35.refs_3_, ...), custom_call_target="tpu_custom_call" | custom-call | flops 805306368 | bytes 2621440 | tf_op jit(solution)/shard_map/pallas_call | solution.py:258
  61.2 1.5 %collective-permute-done.34.refs_6_ = bf16[128,512]{1,0:T(8,128)(2,1)S(1)} collective-permute-done((bf16[128,512]{1,0:T(8,128)(2,1)S(1)}, bf16[128,512]{1,0:T(8,128)(2,1)S(1)}, u32[]{:S(2)}, u32[]{:S(2)}) %collective-permute-start.34) | collective-permute-done | bytes 131104 | tf_op jit(solution)/shard_map/ppermute | solution.py:22
  62.8 1.8 %shard_map.50 = (bf16[3,3,3,2,1,128,512]{6,5,4,3,2,1,0:T(8,128)(2,1)}, bf16[4,2,128,512]{3,2,1,0:T(8,128)(2,1)S(1)}) custom-call(bf16[384,512]{1,0:T(8,128)(2,1)S(1)} %bitcast.51, bf16[384,512]{1,0:T(8,128)(2,1)S(1)} %bitcast.42, bf16[1,2,128,512]{3,2,1,0:T(8,128)(2,1)S(1)} %bitcast.64, ...), custom_call_target="tpu_custom_call", output_to_operand_aliasing={{0}: (7, {})} | custom-call | flops 805306368 | bytes 2621440 | tf_op jit(solution)/shard_map/pallas_call | solution.py:258
  64.6 1.5 %collective-permute-start.27 = (bf16[1,2,128,512]{3,2,1,0:T(8,128)(2,1)S(1)}, bf16[1,2,128,512]{3,2,1,0:T(8,128)(2,1)S(1)}, u32[]{:S(2)}, u32[]{:S(2)}) collective-permute-start(bf16[1,2,128,512]{3,2,1,0:T(8,128)(2,1)S(1)} %bitcast.59), channel_id=1, source_target_pairs={{0,8},{8,0},{16,24},{24,16},{1,9},{9,1},{17,25},{25,17},{2,10},{10... | collective-permute-start | bytes 786440 | tf_op jit(solution)/shard_map/ppermute | solution.py:22
  67.0 6.3 %collective-permute-done.27.refs_3_ = bf16[1,2,128,512]{3,2,1,0:T(8,128)(2,1)S(1)} collective-permute-done((bf16[1,2,128,512]{3,2,1,0:T(8,128)(2,1)S(1)}, bf16[1,2,128,512]{3,2,1,0:T(8,128)(2,1)S(1)}, u32[]{:S(2)}, u32[]{:S(2)}) %collective-permute-start.27) | collective-permute-done | bytes 262176 | tf_op jit(solution)/shard_map/ppermute | solution.py:22
  73.3 1.2 %collective-permute-done.28.refs_4_ = bf16[1,2,128,512]{3,2,1,0:T(8,128)(2,1)S(1)} collective-permute-done((bf16[1,2,128,512]{3,2,1,0:T(8,128)(2,1)S(1)}, bf16[1,2,128,512]{3,2,1,0:T(8,128)(2,1)S(1)}, u32[]{:S(2)}, u32[]{:S(2)}) %collective-permute-start.28) | collective-permute-done | bytes 262176 | tf_op jit(solution)/shard_map/ppermute | solution.py:22
  75.8 1.7 %collective-permute-start.23 = (bf16[1,2,128,512]{3,2,1,0:T(8,128)(2,1)S(1)}, bf16[1,2,128,512]{3,2,1,0:T(8,128)(2,1)S(1)}, u32[]{:S(2)}, u32[]{:S(2)}) collective-permute-start(bf16[1,2,128,512]{3,2,1,0:T(8,128)(2,1)S(1)} %collective-permute-done.22.refs_2_), channel_id=1, source_target_pairs={{0,8},{8,0},{16,24},{24,16},{1,9},{9,1},{17,25},{25,17},{2,10},{10... | collective-permute-start | bytes 786440 | tf_op jit(solution)/shard_map/ppermute | solution.py:22
  77.4 1.7 %shard_map.51.refs_3_ = bf16[3,3,3,2,1,128,512]{6,5,4,3,2,1,0:T(8,128)(2,1)} custom-call(bf16[384,512]{1,0:T(8,128)(2,1)S(1)} %bitcast.52, bf16[384,512]{1,0:T(8,128)(2,1)S(1)} %bitcast.43, bf16[4,2,128,512]{3,2,1,0:T(8,128)(2,1)S(1)} %collective-permute-done.40.refs_2_, ...), custom_call_target="tpu_custom_call", output_to_operand_aliasing={{}: (3, {})} | custom-call | flops 805306368 | bytes 2621440 | tf_op jit(solution)/shard_map/pallas_call | solution.py:258
  79.2 1.7 %shard_map.52.refs_7_ = bf16[3,3,3,2,1,128,512]{6,5,4,3,2,1,0:T(8,128)(2,1)} custom-call(bf16[384,512]{1,0:T(8,128)(2,1)S(1)} %bitcast.53, bf16[384,512]{1,0:T(8,128)(2,1)S(1)} %bitcast.44, bf16[4,2,128,512]{3,2,1,0:T(8,128)(2,1)S(1)} %collective-permute-done.39.refs_2_, ...), custom_call_target="tpu_custom_call", output_to_operand_aliasing={{}: (3, {})} | custom-call | flops 805306368 | bytes 2621440 | tf_op jit(solution)/shard_map/pallas_call | solution.py:258
  81.8 1.8 %shard_map.53 = (bf16[3,3,3,2,1,128,512]{6,5,4,3,2,1,0:T(8,128)(2,1)}, bf16[4,2,128,512]{3,2,1,0:T(8,128)(2,1)S(1)}) custom-call(bf16[384,512]{1,0:T(8,128)(2,1)S(1)} %bitcast.54, bf16[384,512]{1,0:T(8,128)(2,1)S(1)} %bitcast.45, bf16[1,2,128,512]{3,2,1,0:T(8,128)(2,1)S(1)} %bitcast.61, ...), custom_call_target="tpu_custom_call", output_to_operand_aliasing={{0}: (7, {})} | custom-call | flops 805306368 | bytes 2621440 | tf_op jit(solution)/shard_map/pallas_call | solution.py:258
  83.7 1.5 %collective-permute-start.15 = (bf16[2,2,128,512]{3,2,1,0:T(8,128)(2,1)S(1)}, bf16[2,2,128,512]{3,2,1,0:T(8,128)(2,1)S(1)}, u32[]{:S(2)}, u32[]{:S(2)}) collective-permute-start(bf16[2,2,128,512]{3,2,1,0:T(8,128)(2,1)S(1)} %collective-permute-done.14.refs_2_), channel_id=1, source_target_pairs={{0,8},{8,0},{16,24},{24,16},{1,9},{9,1},{17,25},{25,17},{2,10},{10... | collective-permute-start | bytes 1572872 | tf_op jit(solution)/shard_map/ppermute | solution.py:22
  86.0 1.2 %collective-permute-start.16 = (bf16[2,2,128,512]{3,2,1,0:T(8,128)(2,1)S(1)}, bf16[2,2,128,512]{3,2,1,0:T(8,128)(2,1)S(1)}, u32[]{:S(2)}, u32[]{:S(2)}) collective-permute-start(bf16[2,2,128,512]{3,2,1,0:T(8,128)(2,1)S(1)} %collective-permute-done.14.refs_2_), channel_id=1, source_target_pairs={{0,16},{8,24},{16,0},{24,8},{1,17},{9,25},{17,1},{25,9},{2,18},{10... | collective-permute-start | bytes 1572872 | tf_op jit(solution)/shard_map/ppermute | solution.py:22
  87.2 0.9 collective-permute-start.25
  88.1 6.3 %collective-permute-done.24.refs_4_ = bf16[1,2,128,512]{3,2,1,0:T(8,128)(2,1)S(1)} collective-permute-done((bf16[1,2,128,512]{3,2,1,0:T(8,128)(2,1)S(1)}, bf16[1,2,128,512]{3,2,1,0:T(8,128)(2,1)S(1)}, u32[]{:S(2)}, u32[]{:S(2)}) %collective-permute-start.24) | collective-permute-done | bytes 262176 | tf_op jit(solution)/shard_map/ppermute | solution.py:22
  95.0 3.5 %collective-permute-done.15.refs_3_ = bf16[2,2,128,512]{3,2,1,0:T(8,128)(2,1)S(1)} collective-permute-done((bf16[2,2,128,512]{3,2,1,0:T(8,128)(2,1)S(1)}, bf16[2,2,128,512]{3,2,1,0:T(8,128)(2,1)S(1)}, u32[]{:S(2)}, u32[]{:S(2)}) %collective-permute-start.15) | collective-permute-done | bytes 524320 | tf_op jit(solution)/shard_map/ppermute | solution.py:22
  98.5 1.3 %collective-permute-start.19 = (bf16[128,512]{1,0:T(8,128)(2,1)S(1)}, bf16[128,512]{1,0:T(8,128)(2,1)S(1)}, u32[]{:S(2)}, u32[]{:S(2)}) collective-permute-start(bf16[128,512]{1,0:T(8,128)(2,1)S(1)} %get-tuple-element.67), channel_id=1, source_target_pairs={{0,16},{8,24},{16,0},{24,8},{1,17},{9,25},{17,1},{25,9},{2,18},{10... | collective-permute-start | bytes 393224 | tf_op jit(solution)/shard_map/ppermute | solution.py:22
  99.8 5.8 %collective-permute-done.16.refs_4_ = bf16[2,2,128,512]{3,2,1,0:T(8,128)(2,1)S(1)} collective-permute-done((bf16[2,2,128,512]{3,2,1,0:T(8,128)(2,1)S(1)}, bf16[2,2,128,512]{3,2,1,0:T(8,128)(2,1)S(1)}, u32[]{:S(2)}, u32[]{:S(2)}) %collective-permute-start.16) | collective-permute-done | bytes 524320 | tf_op jit(solution)/shard_map/ppermute | solution.py:22
  106.2 1.2 %collective-permute-start.17 = (bf16[128,512]{1,0:T(8,128)(2,1)S(1)}, bf16[128,512]{1,0:T(8,128)(2,1)S(1)}, u32[]{:S(2)}, u32[]{:S(2)}) collective-permute-start(bf16[128,512]{1,0:T(8,128)(2,1)S(1)} %get-tuple-element.68), channel_id=1, source_target_pairs={{0,16},{8,24},{16,0},{24,8},{1,17},{9,25},{17,1},{25,9},{2,18},{10... | collective-permute-start | bytes 393224 | tf_op jit(solution)/shard_map/ppermute | solution.py:22
  107.4 1.7 %shard_map.54.refs_7_ = bf16[3,3,3,2,1,128,512]{6,5,4,3,2,1,0:T(8,128)(2,1)} custom-call(bf16[384,512]{1,0:T(8,128)(2,1)S(1)} %bitcast.55, bf16[384,512]{1,0:T(8,128)(2,1)S(1)} %bitcast.46, bf16[4,2,128,512]{3,2,1,0:T(8,128)(2,1)S(1)} %collective-permute-done.41.refs_2_, ...), custom_call_target="tpu_custom_call", output_to_operand_aliasing={{}: (3, {})} | custom-call | flops 805306368 | bytes 2621440 | tf_op jit(solution)/shard_map/pallas_call | solution.py:258
  109.2 1.2 %collective-permute-start.18 = (bf16[128,512]{1,0:T(8,128)(2,1)S(1)}, bf16[128,512]{1,0:T(8,128)(2,1)S(1)}, u32[]{:S(2)}, u32[]{:S(2)}) collective-permute-start(bf16[128,512]{1,0:T(8,128)(2,1)S(1)} %get-tuple-element.66), channel_id=1, source_target_pairs={{0,8},{8,0},{16,24},{24,16},{1,9},{9,1},{17,25},{25,17},{2,10},{10... | collective-permute-start | bytes 393224 | tf_op jit(solution)/shard_map/ppermute | solution.py:22
  110.4 1.7 %shard_map.55.refs_7_ = bf16[3,3,3,2,1,128,512]{6,5,4,3,2,1,0:T(8,128)(2,1)} custom-call(bf16[384,512]{1,0:T(8,128)(2,1)S(1)} %bitcast.56, bf16[384,512]{1,0:T(8,128)(2,1)S(1)} %bitcast.47, bf16[1,2,128,512]{3,2,1,0:T(8,128)(2,1)S(1)} %collective-permute-done.22.refs_2_, ...), custom_call_target="tpu_custom_call", output_to_operand_aliasing={{}: (7, {})} | custom-call | flops 805306368 | bytes 2621440 | tf_op jit(solution)/shard_map/pallas_call | solution.py:258
  112.1 1.7 %shard_map.56.refs_7_ = bf16[3,3,3,2,1,128,512]{6,5,4,3,2,1,0:T(8,128)(2,1)} custom-call(bf16[384,512]{1,0:T(8,128)(2,1)S(1)} %bitcast.57, bf16[384,512]{1,0:T(8,128)(2,1)S(1)} %bitcast.48, bf16[2,2,128,512]{3,2,1,0:T(8,128)(2,1)S(1)} %collective-permute-done.14.refs_2_, ...), custom_call_target="tpu_custom_call", output_to_operand_aliasing={{}: (7, {})} | custom-call | flops 805306368 | bytes 2621440 | tf_op jit(solution)/shard_map/pallas_call | solution.py:258
  114.2 1.7 %shard_map.57 = bf16[3,3,3,2,1,128,512]{6,5,4,3,2,1,0:T(8,128)(2,1)} custom-call(bf16[384,512]{1,0:T(8,128)(2,1)S(1)} %bitcast.58, bf16[384,512]{1,0:T(8,128)(2,1)S(1)} %bitcast.49, bf16[2,2,128,512]{3,2,1,0:T(8,128)(2,1)S(1)} %collective-permute-done.14.refs_2_, ...), custom_call_target="tpu_custom_call", output_to_operand_aliasing={{}: (7, {})} | custom-call | flops 805306368 | bytes 2621440 | tf_op jit(solution)/shard_map/pallas_call | solution.py:258
  (87 shorter events, 10.9 us)
Async XLA Ops:
  4.7 13.7 %collective-permute-start = (bf16[2,128,512]{2,1,0:T(8,128)(2,1)S(1)}, bf16[2,128,512]{2,1,0:T(8,128)(2,1)S(1)}, u32[]{:S(2)}, u32[]{:S(2)}) collective-permute-start(bf16[2,128,512]{2,1,0:T(8,128)(2,1)S(1)} %get-tuple-element.34), channel_id=1, source_target_pairs={{0,8},{8,0},{16,24},{24,16},{1,9},{9,1},{17,25},{25,17},{2,10},{10... | collective-permute-start | bytes 786440 | tf_op jit(solution)/shard_map/ppermute | solution.py:22
  7.7 12.3 %collective-permute-start.2 = (bf16[2,128,512]{2,1,0:T(8,128)(2,1)S(1)}, bf16[2,128,512]{2,1,0:T(8,128)(2,1)S(1)}, u32[]{:S(2)}, u32[]{:S(2)}) collective-permute-start(bf16[2,128,512]{2,1,0:T(8,128)(2,1)S(1)} %get-tuple-element.36), channel_id=1, source_target_pairs={{0,16},{8,24},{16,0},{24,8},{1,17},{9,25},{17,1},{25,9},{2,18},{10... | collective-permute-start | bytes 786440 | tf_op jit(solution)/shard_map/ppermute | solution.py:22
  12.5 9.2 %collective-permute-start.4 = (bf16[2,128,512]{2,1,0:T(8,128)(2,1)S(1)}, bf16[2,128,512]{2,1,0:T(8,128)(2,1)S(1)}, u32[]{:S(2)}, u32[]{:S(2)}) collective-permute-start(bf16[2,128,512]{2,1,0:T(8,128)(2,1)S(1)} %get-tuple-element.40), channel_id=1, source_target_pairs={{0,8},{8,0},{16,24},{24,16},{1,9},{9,1},{17,25},{25,17},{2,10},{10... | collective-permute-start | bytes 786440 | tf_op jit(solution)/shard_map/ppermute | solution.py:22
  13.1 9.3 %collective-permute-start.6 = (bf16[2,128,512]{2,1,0:T(8,128)(2,1)S(1)}, bf16[2,128,512]{2,1,0:T(8,128)(2,1)S(1)}, u32[]{:S(2)}, u32[]{:S(2)}) collective-permute-start(bf16[2,128,512]{2,1,0:T(8,128)(2,1)S(1)} %get-tuple-element.42), channel_id=1, source_target_pairs={{0,16},{8,24},{16,0},{24,8},{1,17},{9,25},{17,1},{25,9},{2,18},{10... | collective-permute-start | bytes 786440 | tf_op jit(solution)/shard_map/ppermute | solution.py:22
  16.3 10.8 %collective-permute-start.8 = (bf16[2,128,512]{2,1,0:T(8,128)(2,1)S(1)}, bf16[2,128,512]{2,1,0:T(8,128)(2,1)S(1)}, u32[]{:S(2)}, u32[]{:S(2)}) collective-permute-start(bf16[2,128,512]{2,1,0:T(8,128)(2,1)S(1)} %get-tuple-element.45), channel_id=1, source_target_pairs={{0,8},{8,0},{16,24},{24,16},{1,9},{9,1},{17,25},{25,17},{2,10},{10... | collective-permute-start | bytes 786440 | tf_op jit(solution)/shard_map/ppermute | solution.py:22
  18.3 9.7 %collective-permute-start.10 = (bf16[2,128,512]{2,1,0:T(8,128)(2,1)S(1)}, bf16[2,128,512]{2,1,0:T(8,128)(2,1)S(1)}, u32[]{:S(2)}, u32[]{:S(2)}) collective-permute-start(bf16[2,128,512]{2,1,0:T(8,128)(2,1)S(1)} %get-tuple-element.47), channel_id=1, source_target_pairs={{0,16},{8,24},{16,0},{24,8},{1,17},{9,25},{17,1},{25,9},{2,18},{10... | collective-permute-start | bytes 786440 | tf_op jit(solution)/shard_map/ppermute | solution.py:22
  20.0 10.7 %collective-permute-start.1 = (bf16[1,128,512]{2,1,0:T(8,128)(2,1)S(1)}, bf16[1,128,512]{2,1,0:T(8,128)(2,1)S(1)}, u32[]{:S(2)}, u32[]{:S(2)}) collective-permute-start(bf16[1,128,512]{2,1,0:T(8,128)(2,1)S(1)} %slice.107), channel_id=1, source_target_pairs={{0,16},{8,24},{16,0},{24,8},{1,17},{9,25},{17,1},{25,9},{2,18},{10... | collective-permute-start | bytes 393224 | tf_op jit(solution)/shard_map/ppermute | solution.py:22
  21.8 10.5 %collective-permute-start.3 = (bf16[1,128,512]{2,1,0:T(8,128)(2,1)S(1)}, bf16[1,128,512]{2,1,0:T(8,128)(2,1)S(1)}, u32[]{:S(2)}, u32[]{:S(2)}) collective-permute-start(bf16[1,128,512]{2,1,0:T(8,128)(2,1)S(1)} %slice.109), channel_id=1, source_target_pairs={{0,8},{8,0},{16,24},{24,16},{1,9},{9,1},{17,25},{25,17},{2,10},{10... | collective-permute-start | bytes 393224 | tf_op jit(solution)/shard_map/ppermute | solution.py:22
  22.4 11.6 %collective-permute-start.5 = (bf16[1,128,512]{2,1,0:T(8,128)(2,1)S(1)}, bf16[1,128,512]{2,1,0:T(8,128)(2,1)S(1)}, u32[]{:S(2)}, u32[]{:S(2)}) collective-permute-start(bf16[1,128,512]{2,1,0:T(8,128)(2,1)S(1)} %slice.111), channel_id=1, source_target_pairs={{0,16},{8,24},{16,0},{24,8},{1,17},{9,25},{17,1},{25,9},{2,18},{10... | collective-permute-start | bytes 393224 | tf_op jit(solution)/shard_map/ppermute | solution.py:22
  27.2 6.8 %collective-permute-start.7 = (bf16[1,128,512]{2,1,0:T(8,128)(2,1)S(1)}, bf16[1,128,512]{2,1,0:T(8,128)(2,1)S(1)}, u32[]{:S(2)}, u32[]{:S(2)}) collective-permute-start(bf16[1,128,512]{2,1,0:T(8,128)(2,1)S(1)} %slice.113), channel_id=1, source_target_pairs={{0,8},{8,0},{16,24},{24,16},{1,9},{9,1},{17,25},{25,17},{2,10},{10... | collective-permute-start | bytes 393224 | tf_op jit(solution)/shard_map/ppermute | solution.py:22
  28.0 7.7 %collective-permute-start.9 = (bf16[1,128,512]{2,1,0:T(8,128)(2,1)S(1)}, bf16[1,128,512]{2,1,0:T(8,128)(2,1)S(1)}, u32[]{:S(2)}, u32[]{:S(2)}) collective-permute-start(bf16[1,128,512]{2,1,0:T(8,128)(2,1)S(1)} %slice.115), channel_id=1, source_target_pairs={{0,16},{8,24},{16,0},{24,8},{1,17},{9,25},{17,1},{25,9},{2,18},{10... | collective-permute-start | bytes 393224 | tf_op jit(solution)/shard_map/ppermute | solution.py:22
  30.7 5.0 %collective-permute-start.11 = (bf16[1,128,512]{2,1,0:T(8,128)(2,1)S(1)}, bf16[1,128,512]{2,1,0:T(8,128)(2,1)S(1)}, u32[]{:S(2)}, u32[]{:S(2)}) collective-permute-start(bf16[1,128,512]{2,1,0:T(8,128)(2,1)S(1)} %slice.117), channel_id=1, source_target_pairs={{0,8},{8,0},{16,24},{24,16},{1,9},{9,1},{17,25},{25,17},{2,10},{10... | collective-permute-start | bytes 393224 | tf_op jit(solution)/shard_map/ppermute | solution.py:22
  32.4 11.0 %collective-permute-start.21 = (bf16[2,128,512]{2,1,0:T(8,128)(2,1)S(1)}, bf16[2,128,512]{2,1,0:T(8,128)(2,1)S(1)}, u32[]{:S(2)}, u32[]{:S(2)}) collective-permute-start(bf16[2,128,512]{2,1,0:T(8,128)(2,1)S(1)} %pad_maximum_fusion.3), channel_id=1, source_target_pairs={{0,2},{1,3},{2,4},{3,5},{4,6},{5,7},{6,0},{7,1},{8,10},{9,11},{10,... | collective-permute-start | bytes 786440 | tf_op jit(solution)/shard_map/ppermute | solution.py:17
  34.1 13.1 %collective-permute-start.12 = (bf16[2,128,512]{2,1,0:T(8,128)(2,1)S(1)}, bf16[2,128,512]{2,1,0:T(8,128)(2,1)S(1)}, u32[]{:S(2)}, u32[]{:S(2)}) collective-permute-start(bf16[2,128,512]{2,1,0:T(8,128)(2,1)S(1)} %pad_maximum_fusion.4), channel_id=1, source_target_pairs={{0,2},{1,3},{2,4},{3,5},{4,6},{5,7},{6,0},{7,1},{8,10},{9,11},{10,... | collective-permute-start | bytes 786440 | tf_op jit(solution)/shard_map/ppermute | solution.py:17
  35.8 14.4 %collective-permute-start.13 = (bf16[2,128,512]{2,1,0:T(8,128)(2,1)S(1)}, bf16[2,128,512]{2,1,0:T(8,128)(2,1)S(1)}, u32[]{:S(2)}, u32[]{:S(2)}) collective-permute-start(bf16[2,128,512]{2,1,0:T(8,128)(2,1)S(1)} %pad_maximum_fusion.5), channel_id=1, source_target_pairs={{0,2},{1,3},{2,4},{3,5},{4,6},{5,7},{6,0},{7,1},{8,10},{9,11},{10,... | collective-permute-start | bytes 786440 | tf_op jit(solution)/shard_map/ppermute | solution.py:17
  43.4 7.5 %collective-permute-start.35 = (bf16[1,2,128,512]{3,2,1,0:T(8,128)(2,1)S(1)}, bf16[1,2,128,512]{3,2,1,0:T(8,128)(2,1)S(1)}, u32[]{:S(2)}, u32[]{:S(2)}) collective-permute-start(bf16[1,2,128,512]{3,2,1,0:T(8,128)(2,1)S(1)} %bitcast.65), channel_id=1, source_target_pairs={{0,8},{8,0},{16,24},{24,16},{1,9},{9,1},{17,25},{25,17},{2,10},{10... | collective-permute-start | bytes 786440 | tf_op jit(solution)/shard_map/ppermute | solution.py:22
  43.9 8.6 %collective-permute-start.36 = (bf16[1,2,128,512]{3,2,1,0:T(8,128)(2,1)S(1)}, bf16[1,2,128,512]{3,2,1,0:T(8,128)(2,1)S(1)}, u32[]{:S(2)}, u32[]{:S(2)}) collective-permute-start(bf16[1,2,128,512]{3,2,1,0:T(8,128)(2,1)S(1)} %bitcast.66), channel_id=1, source_target_pairs={{0,16},{8,24},{16,0},{24,8},{1,17},{9,25},{17,1},{25,9},{2,18},{10... | collective-permute-start | bytes 786440 | tf_op jit(solution)/shard_map/ppermute | solution.py:22
  47.1 8.3 %collective-permute-start.31 = (bf16[1,2,128,512]{3,2,1,0:T(8,128)(2,1)S(1)}, bf16[1,2,128,512]{3,2,1,0:T(8,128)(2,1)S(1)}, u32[]{:S(2)}, u32[]{:S(2)}) collective-permute-start(bf16[1,2,128,512]{3,2,1,0:T(8,128)(2,1)S(1)} %bitcast.62), channel_id=1, source_target_pairs={{0,8},{8,0},{16,24},{24,16},{1,9},{9,1},{17,25},{25,17},{2,10},{10... | collective-permute-start | bytes 786440 | tf_op jit(solution)/shard_map/ppermute | solution.py:22
  48.9 8.8 %collective-permute-start.32 = (bf16[1,2,128,512]{3,2,1,0:T(8,128)(2,1)S(1)}, bf16[1,2,128,512]{3,2,1,0:T(8,128)(2,1)S(1)}, u32[]{:S(2)}, u32[]{:S(2)}) collective-permute-start(bf16[1,2,128,512]{3,2,1,0:T(8,128)(2,1)S(1)} %bitcast.63), channel_id=1, source_target_pairs={{0,16},{8,24},{16,0},{24,8},{1,17},{9,25},{17,1},{25,9},{2,18},{10... | collective-permute-start | bytes 786440 | tf_op jit(solution)/shard_map/ppermute | solution.py:22
  50.9 8.4 %collective-permute-start.37 = (bf16[128,512]{1,0:T(8,128)(2,1)S(1)}, bf16[128,512]{1,0:T(8,128)(2,1)S(1)}, u32[]{:S(2)}, u32[]{:S(2)}) collective-permute-start(bf16[128,512]{1,0:T(8,128)(2,1)S(1)} %slice_bitcast_fusion.1), channel_id=1, source_target_pairs={{0,16},{8,24},{16,0},{24,8},{1,17},{9,25},{17,1},{25,9},{2,18},{10... | collective-permute-start | bytes 393224 | tf_op jit(solution)/shard_map/ppermute | solution.py:22
  52.5 6.8 %collective-permute-start.38 = (bf16[128,512]{1,0:T(8,128)(2,1)S(1)}, bf16[128,512]{1,0:T(8,128)(2,1)S(1)}, u32[]{:S(2)}, u32[]{:S(2)}) collective-permute-start(bf16[128,512]{1,0:T(8,128)(2,1)S(1)} %slice_bitcast_fusion), channel_id=1, source_target_pairs={{0,8},{8,0},{16,24},{24,16},{1,9},{9,1},{17,25},{25,17},{2,10},{10... | collective-permute-start | bytes 393224 | tf_op jit(solution)/shard_map/ppermute | solution.py:22
  55.4 5.8 %collective-permute-start.33 = (bf16[128,512]{1,0:T(8,128)(2,1)S(1)}, bf16[128,512]{1,0:T(8,128)(2,1)S(1)}, u32[]{:S(2)}, u32[]{:S(2)}) collective-permute-start(bf16[128,512]{1,0:T(8,128)(2,1)S(1)} %slice_bitcast_fusion.3), channel_id=1, source_target_pairs={{0,16},{8,24},{16,0},{24,8},{1,17},{9,25},{17,1},{25,9},{2,18},{10... | collective-permute-start | bytes 393224 | tf_op jit(solution)/shard_map/ppermute | solution.py:22
  57.7 5.0 %collective-permute-start.34 = (bf16[128,512]{1,0:T(8,128)(2,1)S(1)}, bf16[128,512]{1,0:T(8,128)(2,1)S(1)}, u32[]{:S(2)}, u32[]{:S(2)}) collective-permute-start(bf16[128,512]{1,0:T(8,128)(2,1)S(1)} %slice_bitcast_fusion.2), channel_id=1, source_target_pairs={{0,8},{8,0},{16,24},{24,16},{1,9},{9,1},{17,25},{25,17},{2,10},{10... | collective-permute-start | bytes 393224 | tf_op jit(solution)/shard_map/ppermute | solution.py:22
  61.1 14.6 %collective-permute-start.40 = (bf16[4,2,128,512]{3,2,1,0:T(8,128)(2,1)S(1)}, bf16[4,2,128,512]{3,2,1,0:T(8,128)(2,1)S(1)}, u32[]{:S(2)}, u32[]{:S(2)}) collective-permute-start(bf16[4,2,128,512]{3,2,1,0:T(8,128)(2,1)S(1)} %get-tuple-element.55), channel_id=1, source_target_pairs={{0,1},{1,0},{2,3},{3,2},{4,5},{5,4},{6,7},{7,6},{8,9},{9,8},{10,11... | collective-permute-start | bytes 3145736 | tf_op jit(solution)/shard_map/ppermute | solution.py:22
  64.5 14.7 %collective-permute-start.39 = (bf16[4,2,128,512]{3,2,1,0:T(8,128)(2,1)S(1)}, bf16[4,2,128,512]{3,2,1,0:T(8,128)(2,1)S(1)}, u32[]{:S(2)}, u32[]{:S(2)}) collective-permute-start(bf16[4,2,128,512]{3,2,1,0:T(8,128)(2,1)S(1)} %get-tuple-element.54), channel_id=1, source_target_pairs={{0,1},{1,0},{2,3},{3,2},{4,5},{5,4},{6,7},{7,6},{8,9},{9,8},{10,11... | collective-permute-start | bytes 3145736 | tf_op jit(solution)/shard_map/ppermute | solution.py:22
  64.6 8.7 %collective-permute-start.27 = (bf16[1,2,128,512]{3,2,1,0:T(8,128)(2,1)S(1)}, bf16[1,2,128,512]{3,2,1,0:T(8,128)(2,1)S(1)}, u32[]{:S(2)}, u32[]{:S(2)}) collective-permute-start(bf16[1,2,128,512]{3,2,1,0:T(8,128)(2,1)S(1)} %bitcast.59), channel_id=1, source_target_pairs={{0,8},{8,0},{16,24},{24,16},{1,9},{9,1},{17,25},{25,17},{2,10},{10... | collective-permute-start | bytes 786440 | tf_op jit(solution)/shard_map/ppermute | solution.py:22
  66.1 8.4 %collective-permute-start.28 = (bf16[1,2,128,512]{3,2,1,0:T(8,128)(2,1)S(1)}, bf16[1,2,128,512]{3,2,1,0:T(8,128)(2,1)S(1)}, u32[]{:S(2)}, u32[]{:S(2)}) collective-permute-start(bf16[1,2,128,512]{3,2,1,0:T(8,128)(2,1)S(1)} %bitcast.60), channel_id=1, source_target_pairs={{0,16},{8,24},{16,0},{24,8},{1,17},{9,25},{17,1},{25,9},{2,18},{10... | collective-permute-start | bytes 786440 | tf_op jit(solution)/shard_map/ppermute | solution.py:22
  67.0 8.4 %collective-permute-start.22 = (bf16[1,2,128,512]{3,2,1,0:T(8,128)(2,1)S(1)}, bf16[1,2,128,512]{3,2,1,0:T(8,128)(2,1)S(1)}, u32[]{:S(2)}, u32[]{:S(2)}) collective-permute-start(bf16[1,2,128,512]{3,2,1,0:T(8,128)(2,1)S(1)} %get-tuple-element.69), channel_id=1, source_target_pairs={{0,1},{1,2},{2,3},{3,4},{4,5},{5,6},{6,7},{7,0},{8,9},{9,10},{10,1... | collective-permute-start | bytes 786440 | tf_op jit(solution)/shard_map/ppermute | solution.py:17
  73.3 10.4 %collective-permute-start.14 = (bf16[2,2,128,512]{3,2,1,0:T(8,128)(2,1)S(1)}, bf16[2,2,128,512]{3,2,1,0:T(8,128)(2,1)S(1)}, u32[]{:S(2)}, u32[]{:S(2)}) collective-permute-start(bf16[2,2,128,512]{3,2,1,0:T(8,128)(2,1)S(1)} %pad_maximum_fusion.2), channel_id=1, source_target_pairs={{0,1},{1,2},{2,3},{3,4},{4,5},{5,6},{6,7},{7,0},{8,9},{9,10},{10,1... | collective-permute-start | bytes 1572872 | tf_op jit(solution)/shard_map/ppermute | solution.py:17
  74.5 6.5 %collective-permute-start.29 = (bf16[128,512]{1,0:T(8,128)(2,1)S(1)}, bf16[128,512]{1,0:T(8,128)(2,1)S(1)}, u32[]{:S(2)}, u32[]{:S(2)}) collective-permute-start(bf16[128,512]{1,0:T(8,128)(2,1)S(1)} %slice_bitcast_fusion.5), channel_id=1, source_target_pairs={{0,16},{8,24},{16,0},{24,8},{1,17},{9,25},{17,1},{25,9},{2,18},{10... | collective-permute-start | bytes 393224 | tf_op jit(solution)/shard_map/ppermute | solution.py:22
  75.3 6.4 %collective-permute-start.30 = (bf16[128,512]{1,0:T(8,128)(2,1)S(1)}, bf16[128,512]{1,0:T(8,128)(2,1)S(1)}, u32[]{:S(2)}, u32[]{:S(2)}) collective-permute-start(bf16[128,512]{1,0:T(8,128)(2,1)S(1)} %slice_bitcast_fusion.4), channel_id=1, source_target_pairs={{0,8},{8,0},{16,24},{24,16},{1,9},{9,1},{17,25},{25,17},{2,10},{10... | collective-permute-start | bytes 393224 | tf_op jit(solution)/shard_map/ppermute | solution.py:22
  75.8 11.4 %collective-permute-start.23 = (bf16[1,2,128,512]{3,2,1,0:T(8,128)(2,1)S(1)}, bf16[1,2,128,512]{3,2,1,0:T(8,128)(2,1)S(1)}, u32[]{:S(2)}, u32[]{:S(2)}) collective-permute-start(bf16[1,2,128,512]{3,2,1,0:T(8,128)(2,1)S(1)} %collective-permute-done.22.refs_2_), channel_id=1, source_target_pairs={{0,8},{8,0},{16,24},{24,16},{1,9},{9,1},{17,25},{25,17},{2,10},{10... | collective-permute-start | bytes 786440 | tf_op jit(solution)/shard_map/ppermute | solution.py:22
  83.5 22.7 %collective-permute-start.41 = (bf16[4,2,128,512]{3,2,1,0:T(8,128)(2,1)S(1)}, bf16[4,2,128,512]{3,2,1,0:T(8,128)(2,1)S(1)}, u32[]{:S(2)}, u32[]{:S(2)}) collective-permute-start(bf16[4,2,128,512]{3,2,1,0:T(8,128)(2,1)S(1)} %get-tuple-element.57), channel_id=1, source_target_pairs={{0,1},{1,0},{2,3},{3,2},{4,5},{5,4},{6,7},{7,6},{8,9},{9,8},{10,11... | collective-permute-start | bytes 3145736 | tf_op jit(solution)/shard_map/ppermute | solution.py:22
  83.7 14.8 %collective-permute-start.15 = (bf16[2,2,128,512]{3,2,1,0:T(8,128)(2,1)S(1)}, bf16[2,2,128,512]{3,2,1,0:T(8,128)(2,1)S(1)}, u32[]{:S(2)}, u32[]{:S(2)}) collective-permute-start(bf16[2,2,128,512]{3,2,1,0:T(8,128)(2,1)S(1)} %collective-permute-done.14.refs_2_), channel_id=1, source_target_pairs={{0,8},{8,0},{16,24},{24,16},{1,9},{9,1},{17,25},{25,17},{2,10},{10... | collective-permute-start | bytes 1572872 | tf_op jit(solution)/shard_map/ppermute | solution.py:22
  85.2 9.2 %collective-permute-start.24 = (bf16[1,2,128,512]{3,2,1,0:T(8,128)(2,1)S(1)}, bf16[1,2,128,512]{3,2,1,0:T(8,128)(2,1)S(1)}, u32[]{:S(2)}, u32[]{:S(2)}) collective-permute-start(bf16[1,2,128,512]{3,2,1,0:T(8,128)(2,1)S(1)} %collective-permute-done.22.refs_2_), channel_id=1, source_target_pairs={{0,16},{8,24},{16,0},{24,8},{1,17},{9,25},{17,1},{25,9},{2,18},{10... | collective-permute-start | bytes 786440 | tf_op jit(solution)/shard_map/ppermute | solution.py:22
  86.0 19.6 %collective-permute-start.16 = (bf16[2,2,128,512]{3,2,1,0:T(8,128)(2,1)S(1)}, bf16[2,2,128,512]{3,2,1,0:T(8,128)(2,1)S(1)}, u32[]{:S(2)}, u32[]{:S(2)}) collective-permute-start(bf16[2,2,128,512]{3,2,1,0:T(8,128)(2,1)S(1)} %collective-permute-done.14.refs_2_), channel_id=1, source_target_pairs={{0,16},{8,24},{16,0},{24,8},{1,17},{9,25},{17,1},{25,9},{2,18},{10... | collective-permute-start | bytes 1572872 | tf_op jit(solution)/shard_map/ppermute | solution.py:22
  87.2 22.0 %collective-permute-start.25 = (bf16[128,512]{1,0:T(8,128)(2,1)S(1)}, bf16[128,512]{1,0:T(8,128)(2,1)S(1)}, u32[]{:S(2)}, u32[]{:S(2)}) collective-permute-start(bf16[128,512]{1,0:T(8,128)(2,1)S(1)} %slice_bitcast_fusion.7), channel_id=1, source_target_pairs={{0,16},{8,24},{16,0},{24,8},{1,17},{9,25},{17,1},{25,9},{2,18},{10... | collective-permute-start | bytes 393224 | tf_op jit(solution)/shard_map/ppermute | solution.py:22
  94.4 16.0 %collective-permute-start.26 = (bf16[128,512]{1,0:T(8,128)(2,1)S(1)}, bf16[128,512]{1,0:T(8,128)(2,1)S(1)}, u32[]{:S(2)}, u32[]{:S(2)}) collective-permute-start(bf16[128,512]{1,0:T(8,128)(2,1)S(1)} %slice_bitcast_fusion.6), channel_id=1, source_target_pairs={{0,8},{8,0},{16,24},{24,16},{1,9},{9,1},{17,25},{25,17},{2,10},{10... | collective-permute-start | bytes 393224 | tf_op jit(solution)/shard_map/ppermute | solution.py:22
  98.5 13.6 %collective-permute-start.19 = (bf16[128,512]{1,0:T(8,128)(2,1)S(1)}, bf16[128,512]{1,0:T(8,128)(2,1)S(1)}, u32[]{:S(2)}, u32[]{:S(2)}) collective-permute-start(bf16[128,512]{1,0:T(8,128)(2,1)S(1)} %get-tuple-element.67), channel_id=1, source_target_pairs={{0,16},{8,24},{16,0},{24,8},{1,17},{9,25},{17,1},{25,9},{2,18},{10... | collective-permute-start | bytes 393224 | tf_op jit(solution)/shard_map/ppermute | solution.py:22
  105.6 6.5 %collective-permute-start.20 = (bf16[128,512]{1,0:T(8,128)(2,1)S(1)}, bf16[128,512]{1,0:T(8,128)(2,1)S(1)}, u32[]{:S(2)}, u32[]{:S(2)}) collective-permute-start(bf16[128,512]{1,0:T(8,128)(2,1)S(1)} %get-tuple-element.65), channel_id=1, source_target_pairs={{0,8},{8,0},{16,24},{24,16},{1,9},{9,1},{17,25},{25,17},{2,10},{10... | collective-permute-start | bytes 393224 | tf_op jit(solution)/shard_map/ppermute | solution.py:22
  106.2 7.7 %collective-permute-start.17 = (bf16[128,512]{1,0:T(8,128)(2,1)S(1)}, bf16[128,512]{1,0:T(8,128)(2,1)S(1)}, u32[]{:S(2)}, u32[]{:S(2)}) collective-permute-start(bf16[128,512]{1,0:T(8,128)(2,1)S(1)} %get-tuple-element.68), channel_id=1, source_target_pairs={{0,16},{8,24},{16,0},{24,8},{1,17},{9,25},{17,1},{25,9},{2,18},{10... | collective-permute-start | bytes 393224 | tf_op jit(solution)/shard_map/ppermute | solution.py:22
  109.2 5.0 %collective-permute-start.18 = (bf16[128,512]{1,0:T(8,128)(2,1)S(1)}, bf16[128,512]{1,0:T(8,128)(2,1)S(1)}, u32[]{:S(2)}, u32[]{:S(2)}) collective-permute-start(bf16[128,512]{1,0:T(8,128)(2,1)S(1)} %get-tuple-element.66), channel_id=1, source_target_pairs={{0,8},{8,0},{16,24},{24,16},{1,9},{9,1},{17,25},{25,17},{2,10},{10... | collective-permute-start | bytes 393224 | tf_op jit(solution)/shard_map/ppermute | solution.py:22

commit v3 on v2

v3 whole, which is shorter than its diff:
```python
import functools

import jax
import jax.numpy as jnp
from jax import lax
from jax.experimental import pallas as pl
from jax.experimental.pallas import tpu as pltpu
from jax.sharding import PartitionSpec as P

STOPS = 3
dot = functools.partial(jnp.dot, preferred_element_type=jnp.float32)


def shifted(value, steps, first=0, stride=1):
    count = lax.axis_size("ta")
    pairs = [(source, (source + steps) % count) for source in range(first, count, stride)]
    return lax.ppermute(value, "ta", pairs)


def swapped_cores(value):
    count = lax.axis_size("ta")
    return lax.ppermute(value, "ta", [(time, time ^ 1) for time in range(count)])


def exchanged(value, bit, first=0, stride=1):
    count, times = lax.axis_size("sec"), lax.axis_size("ta")
    flips = (bit, reversed_bits(bit, count.bit_length() - 1))
    pairs = [
        (section * times + time, (section ^ flips[time % 2]) * times + time)
        for section in range(count)
        for time in range(first, times, stride)
    ]
    return lax.ppermute(value, ("sec", "ta"), pairs)


def reversed_bits(value, width):
    return sum(((value >> place) & 1) << (width - 1 - place) for place in range(width))


def over_rows(left, right):
    return lax.dot_general(
        left, right, (((0,), (0,)), ((), ())), preferred_element_type=jnp.float32
    )


def product_kernel(sections, source, sources, *refs):
    refs = list(refs)
    first, last = source == 0, source == sources - 1
    if first:
        live_hbm, times_hbm, sink_hbm, prop_hbm = refs[:4]
        refs = refs[4:]
    else:
        times_hbm, sink, prop, prop_hbm = refs[:4]
        refs = refs[4:]
    keep, send = refs[:2]
    refs = refs[2:]
    if first:
        sink = refs.pop(0)
    following = None if last else refs.pop(0)
    real, imag, times, sems, index_sems = refs[:5]
    refs = refs[5:]
    index_copies = [pltpu.make_async_copy(times_hbm, times, index_sems.at[0])]
    copies = []
    if first:
        live_rows, raw, prop = refs
        index_copies.append(pltpu.make_async_copy(live_hbm, live_rows, index_sems.at[1]))
        for part in range(2):
            copies.append(pltpu.make_async_copy(sink_hbm.at[part, 0], raw.at[part], sems.at[part]))
            copies.append(
                pltpu.make_async_copy(prop_hbm.at[0, part, 0], prop.at[part], sems.at[2 + part])
            )
    if not last:
        for part in range(2):
            copies.append(
                pltpu.make_async_copy(
                    prop_hbm.at[source + 1, part, 0], following.at[part], sems.at[4 + part]
                )
            )
    ahead = copies[-2:] if not last else []
    copies = copies[: len(copies) - len(ahead)]
    for copy in copies + index_copies:
        copy.start()
    section = lax.axis_index("sec")
    depth, order = sink.shape[1:]
    for copy in index_copies:
        copy.wait()
    sign = jnp.where(lax.axis_index("ta") < times[source], -1.0, 1.0).astype(jnp.float32)
    if first:
        live = lax.broadcasted_iota(jnp.int32, (depth, order), 0) < live_rows[section]
        for part in range(2):
            copies.pop(0).wait()
            sink[part] = jnp.where(live, raw[part], jnp.zeros((depth, order), jnp.bfloat16))
            copies.pop(0).wait()
            if part == 0:
                for copy in ahead:
                    copy.start()
                start = over_rows(sink[0], prop[0])
        real[...] = ((start + over_rows(sink[1], prop[1])) * sign).astype(jnp.bfloat16)
    else:
        for copy in ahead:
            copy.start()
        real[...] = (
            (over_rows(sink[0], prop[0]) + over_rows(sink[1], prop[1])) * sign
        ).astype(jnp.bfloat16)
    imag[...] = (
        (over_rows(sink[0], prop[1]) - over_rows(sink[1], prop[0])) * sign
    ).astype(jnp.bfloat16)
    half = sections // 2
    width = sections.bit_length() - 1
    rows = order // sections
    for q in range(sections):
        slot = reversed_bits(q, width)
        flip = jnp.where(lax.axis_index("ta") % 2 == 0, q, slot)
        window = pl.ds(pl.multiple_of((section ^ flip) * rows, rows), rows)
        target = keep if slot < half else send
        target[slot % half, 0] = real[window, :]
        target[slot % half, 1] = imag[window, :]
    for copy in ahead:
        copy.wait()


def hbm(value):
    return pltpu.with_memory_space_constraint(value, pltpu.HBM)


def products(live_rows, source_times, sink_vectors, propagators, sections):
    _, _, depth, order = sink_vectors.shape
    sources, columns = propagators.shape[0], propagators.shape[4]
    bf16 = jnp.bfloat16
    in_hbm, in_vmem = pl.BlockSpec(memory_space=pltpu.HBM), pl.BlockSpec(memory_space=pltpu.VMEM)
    half = pltpu.VMEM((sections // 2, 2, order // sections, columns), bf16)
    held = pltpu.VMEM((2, depth, order), bf16)
    fetched = pltpu.VMEM((2, depth, columns), bf16)
    halves, sink, prop = [], None, None
    for source in range(sources):
        first, last = source == 0, source == sources - 1
        if first:
            operands = [hbm(live_rows), hbm(source_times), hbm(sink_vectors), hbm(propagators)]
            in_specs = [in_hbm] * 4
        else:
            operands = [hbm(source_times), sink, prop, hbm(propagators)]
            in_specs = [in_hbm, in_vmem, in_vmem, in_hbm]
        outs = [half] * 2 + [held] * first + [fetched] * (not last)
        scratch = [
            pltpu.VMEM((order, columns), bf16),
            pltpu.VMEM((order, columns), bf16),
            pltpu.SMEM(source_times.shape, jnp.int32),
            pltpu.SemaphoreType.DMA((6,)),
            pltpu.SemaphoreType.DMA((2,)),
        ]
        if first:
            scratch += [pltpu.SMEM(live_rows.shape, jnp.int32), held, fetched]
        results = pl.pallas_call(
            functools.partial(product_kernel, sections, source, sources),
            in_specs=in_specs,
            out_specs=[in_vmem] * len(outs),
            out_shape=outs,
            scratch_shapes=scratch,
            compiler_params=pltpu.CompilerParams(vmem_limit_bytes=12 << 20),
            cost_estimate=pl.CostEstimate(
                flops=8 * order * depth * columns,
                bytes_accessed=4 * depth * columns,
                transcendentals=0,
            ),
        )(*operands)
        halves.append(results[:2])
        if first:
            sink = results[2]
        prop = results[-1]
    return halves


def added(kept, got):
    return (kept.astype(jnp.float32) + got.astype(jnp.float32)).astype(jnp.bfloat16)


def reduced(keep, send, width):
    for step in range(width):
        got = exchanged(send, 1 << step)
        total = added(keep, got)
        half = total.shape[0] // 2
        keep, send = total[:half], total[half:]
    return total[0]


def gathered(own, width, **among):
    whole = [own]
    for q in range(1, 1 << width):
        high = 1 << (q.bit_length() - 1)
        whole.append(exchanged(whole[q ^ high], high, **among))
    return [
        [tuple((piece, (s, part)) for part in range(2)) for piece in whole]
        for s in range(own.shape[0])
    ]


def sandwich_kernel(scale, jobs, names, aliased, *refs):
    left_real, left_imag = refs[0], refs[1]
    blocks = refs[2 : 2 + names]
    rest = list(refs[2 + names + aliased :])
    out = rest.pop(0)
    tile, sems = rest
    parity = lax.axis_index("ta") % 2
    shape = tile.shape[2:]

    def run(job, lookup):
        real = [blocks[name][at] for (name, at), _ in lookup]
        imag = [blocks[name][at] for _, (name, at) in lookup]
        right_real, right_imag = jnp.concatenate(real, 0), jnp.concatenate(imag, 0)
        one, two = left_real[...], left_imag[...]
        for part in range(2):
            if part == 0:
                value = dot(one, right_real) - dot(two, right_imag)
            else:
                value = dot(one, right_imag) + dot(two, right_real)
            tile[job, part] = (value * scale).astype(jnp.bfloat16).reshape(shape)
            copies[job][part].start()

    copies = []
    for job, (kind, source, _) in enumerate(jobs):
        stop = (2 * parity, 1, 2 - 2 * parity)[kind]
        copies.append(
            [
                pltpu.make_async_copy(
                    tile.at[job, part], out.at[stop, :, source, part, 0], sems.at[job, part]
                )
                for part in range(2)
            ]
        )
    for job, (_, _, lookups) in enumerate(jobs):
        if len(lookups) == 1:
            run(job, lookups[0])
        else:
            for which in range(2):
                pl.when(parity == which)(functools.partial(run, job, lookups[which]))
    for pair in copies:
        for copy in pair:
            copy.wait()


def sandwich(buffer, jobs, left_real, left_imag, shape):
    arrays, described = [], []
    for kind, source, choices in jobs:
        lookups = []
        for places in choices:
            lookup = []
            for pair in places:
                entry = []
                for array, at in pair:
                    known = [i for i, other in enumerate(arrays) if other is array]
                    if not known:
                        arrays.append(array)
                        known = [len(arrays) - 1]
                    entry.append((known[0], at))
                lookup.append(tuple(entry))
            lookups.append(tuple(lookup))
        described.append((kind, source, tuple(lookups)))
    order, columns = left_real.shape[1], shape[6]
    operands = [left_real, left_imag, *arrays]
    in_vmem, in_hbm = pl.BlockSpec(memory_space=pltpu.VMEM), pl.BlockSpec(memory_space=pltpu.HBM)
    in_specs = [in_vmem] * len(operands)
    aliases = {}
    if buffer is not None:
        aliases = {len(operands): 0}
        in_specs.append(in_hbm)
        operands.append(hbm(buffer))
    return pl.pallas_call(
        functools.partial(
            sandwich_kernel, 0.5 * order ** (-0.5), tuple(described), len(arrays), len(aliases)
        ),
        in_specs=in_specs,
        out_specs=in_hbm,
        out_shape=pltpu.HBM(shape, jnp.bfloat16),
        scratch_shapes=[
            pltpu.VMEM((len(jobs), 2, shape[1]) + tuple(shape[5:]), jnp.bfloat16),
            pltpu.SemaphoreType.DMA((len(jobs), 2)),
        ],
        input_output_aliases=aliases,
        compiler_params=pltpu.CompilerParams(vmem_limit_bytes=14 << 20),
        cost_estimate=pl.CostEstimate(
            flops=8 * len(jobs) * left_real.shape[0] * order * columns,
            bytes_accessed=4 * len(jobs) * left_real.size,
            transcendentals=0,
        ),
    )(*operands)


def body(sink_vectors, propagators, live_rows, source_times):
    sections = lax.axis_size("sec")
    width = sections.bit_length() - 1
    sources = propagators.shape[0]
    order = sink_vectors.shape[3]
    rows = order // sections
    section = lax.axis_index("sec").astype(jnp.uint32)
    first_core = lax.axis_index("ta").astype(jnp.uint32) & 1 == 0
    offsets = [
        (section ^ jnp.where(first_core, jnp.uint32(q), jnp.uint32(reversed_bits(q, width))))
        * jnp.uint32(rows)
        for q in range(sections)
    ]
    sink_vectors, first_core, offsets = lax.optimization_barrier(
        (sink_vectors, first_core, offsets)
    )

    halves = products(live_rows, source_times, sink_vectors, propagators, sections)
    own = [reduced(*halves[s], width) for s in range(sources)]
    second = [shifted(own[s], 2) for s in range(sources)]
    forwarded = tuple(range(sources - 1))
    groups = (forwarded, (sources - 1,))
    last = {}
    for group in groups:
        chosen = jnp.stack(
            [own[s] if s in forwarded else jnp.where(first_core, own[s], second[s]) for s in group]
        )
        if group[0] in forwarded:
            chosen = shifted(chosen, 1, stride=2)
            places = gathered(chosen, width, first=1, stride=2)
        else:
            chosen = shifted(chosen, 1)
            places = gathered(chosen, width)
        last.update(zip(group, places))

    left = jnp.stack(own, 1)
    zero = jnp.uint32(0)
    left = jnp.concatenate(
        [
            lax.dynamic_slice(left, (zero, zero, zero, offset), (2, sources, rows, rows))
            for offset in offsets
        ],
        3,
    ).reshape(2, sources * rows, order)
    left_real, left_imag = left[0], left[1]

    shape = (STOPS, sources, sources, 2, 1, rows, order)
    far, swapped, ahead = {}, {}, {}
    for s in range(sources):
        (far[s],) = gathered(second[s][None], width)
        together = jnp.concatenate([pair[0][0] for pair in far[s]], 0)
        swapped[s] = swapped_cores(together)
        if s in forwarded:
            ahead[s] = shifted(together, 1, first=1, stride=2)

    def whole(value):
        return [
            tuple((value, (reversed_bits(q, width), part)) for part in range(2))
            for q in range(sections)
        ]

    def step(result, jobs):
        listed = []
        for kind, s in jobs:
            if kind == 1:
                choices = (far[s],)
            elif kind == 0:
                choices = (whole(swapped[s]),)
            else:
                choices = (whole(ahead[s]), last[s]) if s in forwarded else (last[s],)
            listed.append((kind, s, choices))
        return sandwich(result, listed, left_real, left_imag, shape)

    result = None
    tail = sources - 1
    calls = [[(1, s), (0, s)] for s in range(tail)] + [[(1, tail)], [(0, tail), (2, 0)]]
    calls += [[(2, s)] for s in range(tail, 0, -1)]
    for jobs in calls:
        result = step(result, jobs)
    return result


def solution(mesh):
    return jax.shard_map(
        body,
        mesh=mesh,
        in_specs=(P(None, "ta", "sec", None), P(None, None, "ta", "sec", None), P(), P()),
        out_specs=P(None, None, None, None, "ta", "sec", None),
        check_vma=False,
    )
```

time: 116 us -> 106 us (0.914)
  starting transfers between devices: 47.3 us -> 42.2 us
  Pallas kernels: 26.8 us -> 24.2 us
  waiting for transfers between devices: 39.7 us -> 37.3 us
    ppermute x37 -> x24, starting transfers between devices: 42.5 us -> 33.6 us  [the longest x21 31.6 us: exchanged(): return lax.ppermute(value, ('sec', 'ta'), pairs)]
    ppermute x37 -> x24, waiting for transfers between devices: 32.2 us -> 23.8 us  [the longest x21 23.7 us: exchanged(): return lax.ppermute(value, ('sec', 'ta'), pairs)]
    ppermute x5 -> x7, waiting for transfers between devices: 7.51 us -> 13.5 us  [shifted(): return lax.ppermute(value, 'ta', pairs)]
    ppermute x5 -> x7, starting transfers between devices: 4.82 us -> 8.69 us  [shifted(): return lax.ppermute(value, 'ta', pairs)]
    pallas_call x9 -> x6, Pallas kernels: 15.7 us -> 13.1 us  [sandwich(): pl.pallas_call(functools.partial(sandwich_kernel, 0.5 * order ** (-0.5),...]
  transfers between devices with their start and end apart: 42 -> 31, of which waited for: 15 -> 14; matrix products, arithmetic and copies ran while one was open for 1% -> 2% of each run, Pallas kernels for 18% -> 17%
where the time goes in v3:
time: 106 us
  starting transfers between devices  42.2 us (40%)
  waiting for transfers between devices  37.3 us (35%)
  Pallas kernels  24.2 us (23%)
  other arithmetic  1.28 us (1%)
    ppermute x21, starting transfers between devices, exchanged(): return lax.ppermute(value, ('sec', 'ta'), pairs)  31.6 us
    ppermute x21, waiting for transfers between devices, exchanged(): return lax.ppermute(value, ('sec', 'ta'), pairs)  23.7 us
    ppermute x7, waiting for transfers between devices, shifted(): return lax.ppermute(value, 'ta', pairs)  13.5 us
    pallas_call x6, Pallas kernels, sandwich(): pl.pallas_call(functools.partial(sandwich_kernel, 0.5 * order ** (-0.5),...  13.1 us
    pallas_call x3, Pallas kernels, products(): pl.pallas_call(functools.partial(product_kernel, sections, source, source...  11.1 us
    ppermute x7, starting transfers between devices, shifted(): return lax.ppermute(value, 'ta', pairs)  8.69 us
  transfers between devices with their start and end apart: 31, of which 14 were waited for; matrix products, arithmetic and copies ran while one was open for 2% of the time, Pallas kernels for 17%

profile of v3, /device:TPU:0, one launch (start us, length us, event | category | flops | bytes accessed | tf_op | source)
XLA Modules:
  0.0 106.0 jit_solution(5252524496435967552)
XLA Ops:
  0.0 4.7 %shard_map.46 = (bf16[2,2,128,512]{3,2,1,0:T(8,128)(2,1)S(1)}, bf16[2,2,128,512]{3,2,1,0:T(8,128)(2,1)S(1)}, bf16[2,1024,512]{2,1,0:T(8,128)(2,1)S(1)}, bf16[2,1024,512]{2,1,0:T(8,128)(2,1)S(1)}) custom-call(s32[4]{0:T(128)} %refs_0_.3, s32[3]{0:T(128)} %refs_0_.5, bf16[2,1,1024,512]{3,2,1,0:T(8,128)(2,1)} %refs_2_, bf16[3,2,1,1024,512]{4,3,2,1,0:T(8,128)(2,1)} %refs_3_.5), custom_call_target="tpu_custom_call" | custom-call | flops 2147483648 | bytes 2097152 | tf_op jit(solution)/shard_map/pallas_call | solution.py:153
  4.7 3.0 %collective-permute-start = (bf16[2,2,128,512]{3,2,1,0:T(8,128)(2,1)S(1)}, bf16[2,2,128,512]{3,2,1,0:T(8,128)(2,1)S(1)}, u32[]{:S(2)}, u32[]{:S(2)}) collective-permute-start(bf16[2,2,128,512]{3,2,1,0:T(8,128)(2,1)S(1)} %get-tuple-element.22), channel_id=1, source_target_pairs={{0,8},{1,17},{2,10},{3,19},{4,12},{5,21},{6,14},{7,23},{8,0},{9,25... | collective-permute-start | bytes 1572872 | tf_op jit(solution)/shard_map/ppermute | solution.py:33
  7.7 3.3 %shard_map.47 = (bf16[2,2,128,512]{3,2,1,0:T(8,128)(2,1)S(1)}, bf16[2,2,128,512]{3,2,1,0:T(8,128)(2,1)S(1)}, bf16[2,1024,512]{2,1,0:T(8,128)(2,1)S(1)}) custom-call(s32[3]{0:T(128)} %refs_0_.5, bf16[2,1024,512]{2,1,0:T(8,128)(2,1)S(1)} %get-tuple-element.23.refs_1_, bf16[2,1024,512]{2,1,0:T(8,128)(2,1)S(1)} %get-tuple-element.24.refs_2_, ...), custom_call_target="tpu_custom_call" | custom-call | flops 2147483648 | bytes 2097152 | tf_op jit(solution)/shard_map/pallas_call | solution.py:153
  11.1 3.2 %shard_map.48 = (bf16[2,2,128,512]{3,2,1,0:T(8,128)(2,1)S(1)}, bf16[2,2,128,512]{3,2,1,0:T(8,128)(2,1)S(1)}) custom-call(s32[3]{0:T(128)} %refs_0_.5, bf16[2,1024,512]{2,1,0:T(8,128)(2,1)S(1)} %get-tuple-element.23.refs_1_, bf16[2,1024,512]{2,1,0:T(8,128)(2,1)S(1)} %get-tuple-element.27.refs_2_, bf16[3,2,1,1024,512]{4,3,2,1,0:T(8,128)(2,1)} %refs_3_.5), custom_call_target="tpu_custom_call" | custom-call | flops 2147483648 | bytes 2097152 | tf_op jit(solution)/shard_map/pallas_call | solution.py:153
  14.2 2.1 %collective-permute-start.4 = (bf16[2,2,128,512]{3,2,1,0:T(8,128)(2,1)S(1)}, bf16[2,2,128,512]{3,2,1,0:T(8,128)(2,1)S(1)}, u32[]{:S(2)}, u32[]{:S(2)}) collective-permute-start(bf16[2,2,128,512]{3,2,1,0:T(8,128)(2,1)S(1)} %get-tuple-element.29), channel_id=1, source_target_pairs={{0,8},{1,17},{2,10},{3,19},{4,12},{5,21},{6,14},{7,23},{8,0},{9,25... | collective-permute-start | bytes 1572872 | tf_op jit(solution)/shard_map/ppermute | solution.py:33
  16.5 1.7 %collective-permute-start.1 = (bf16[1,2,128,512]{3,2,1,0:T(8,128)(2,1)S(1)}, bf16[1,2,128,512]{3,2,1,0:T(8,128)(2,1)S(1)}, u32[]{:S(2)}, u32[]{:S(2)}) collective-permute-start(bf16[1,2,128,512]{3,2,1,0:T(8,128)(2,1)S(1)} %slice.35), channel_id=1, source_target_pairs={{0,16},{1,9},{2,18},{3,11},{4,20},{5,13},{6,22},{7,15},{8,24},{9,1... | collective-permute-start | bytes 786440 | tf_op jit(solution)/shard_map/ppermute | solution.py:33
  18.1 4.7 %collective-permute-done.2 = bf16[2,2,128,512]{3,2,1,0:T(8,128)(2,1)S(1)} collective-permute-done((bf16[2,2,128,512]{3,2,1,0:T(8,128)(2,1)S(1)}, bf16[2,2,128,512]{3,2,1,0:T(8,128)(2,1)S(1)}, u32[]{:S(2)}, u32[]{:S(2)}) %collective-permute-start.2) | collective-permute-done | bytes 524320 | tf_op jit(solution)/shard_map/ppermute | solution.py:33
  23.0 3.1 %collective-permute-start.3 = (bf16[1,2,128,512]{3,2,1,0:T(8,128)(2,1)S(1)}, bf16[1,2,128,512]{3,2,1,0:T(8,128)(2,1)S(1)}, u32[]{:S(2)}, u32[]{:S(2)}) collective-permute-start(bf16[1,2,128,512]{3,2,1,0:T(8,128)(2,1)S(1)} %slice.37), channel_id=1, source_target_pairs={{0,16},{1,9},{2,18},{3,11},{4,20},{5,13},{6,22},{7,15},{8,24},{9,1... | collective-permute-start | bytes 786440 | tf_op jit(solution)/shard_map/ppermute | solution.py:33
  26.2 1.6 %collective-permute-start.24 = (bf16[2,128,512]{2,1,0:T(8,128)(2,1)S(1)}, bf16[2,128,512]{2,1,0:T(8,128)(2,1)S(1)}, u32[]{:S(2)}, u32[]{:S(2)}) collective-permute-start(bf16[2,128,512]{2,1,0:T(8,128)(2,1)S(1)} %bitcast.39), channel_id=1, source_target_pairs={{0,2},{1,3},{2,4},{3,5},{4,6},{5,7},{6,0},{7,1},{8,10},{9,11},{10,... | collective-permute-start | bytes 786440 | tf_op jit(solution)/shard_map/ppermute | solution.py:17
  27.8 3.9 %collective-permute-done.4 = bf16[2,2,128,512]{3,2,1,0:T(8,128)(2,1)S(1)} collective-permute-done((bf16[2,2,128,512]{3,2,1,0:T(8,128)(2,1)S(1)}, bf16[2,2,128,512]{3,2,1,0:T(8,128)(2,1)S(1)}, u32[]{:S(2)}, u32[]{:S(2)}) %collective-permute-start.4) | collective-permute-done | bytes 524320 | tf_op jit(solution)/shard_map/ppermute | solution.py:33
  31.9 2.9 %collective-permute-start.5 = (bf16[1,2,128,512]{3,2,1,0:T(8,128)(2,1)S(1)}, bf16[1,2,128,512]{3,2,1,0:T(8,128)(2,1)S(1)}, u32[]{:S(2)}, u32[]{:S(2)}) collective-permute-start(bf16[1,2,128,512]{3,2,1,0:T(8,128)(2,1)S(1)} %slice.39), channel_id=1, source_target_pairs={{0,16},{1,9},{2,18},{3,11},{4,20},{5,13},{6,22},{7,15},{8,24},{9,1... | collective-permute-start | bytes 786440 | tf_op jit(solution)/shard_map/ppermute | solution.py:33
  34.9 1.3 %collective-permute-start.25 = (bf16[1,2,128,512]{3,2,1,0:T(8,128)(2,1)S(1)}, bf16[1,2,128,512]{3,2,1,0:T(8,128)(2,1)S(1)}, u32[]{:S(2)}, u32[]{:S(2)}) collective-permute-start(bf16[1,2,128,512]{3,2,1,0:T(8,128)(2,1)S(1)} %bitcast.35), channel_id=1, source_target_pairs={{0,8},{1,17},{2,10},{3,19},{4,12},{5,21},{6,14},{7,23},{8,0},{9,25... | collective-permute-start | bytes 786440 | tf_op jit(solution)/shard_map/ppermute | solution.py:33
  36.3 1.6 %collective-permute-start.6 = (bf16[2,128,512]{2,1,0:T(8,128)(2,1)S(1)}, bf16[2,128,512]{2,1,0:T(8,128)(2,1)S(1)}, u32[]{:S(2)}, u32[]{:S(2)}) collective-permute-start(bf16[2,128,512]{2,1,0:T(8,128)(2,1)S(1)} %bitcast.41), channel_id=1, source_target_pairs={{0,2},{1,3},{2,4},{3,5},{4,6},{5,7},{6,0},{7,1},{8,10},{9,11},{10,... | collective-permute-start | bytes 786440 | tf_op jit(solution)/shard_map/ppermute | solution.py:17
  37.9 1.4 %collective-permute-done.5 = bf16[1,2,128,512]{3,2,1,0:T(8,128)(2,1)S(1)} collective-permute-done((bf16[1,2,128,512]{3,2,1,0:T(8,128)(2,1)S(1)}, bf16[1,2,128,512]{3,2,1,0:T(8,128)(2,1)S(1)}, u32[]{:S(2)}, u32[]{:S(2)}) %collective-permute-start.5) | collective-permute-done | bytes 262176 | tf_op jit(solution)/shard_map/ppermute | solution.py:33
  39.4 1.6 %collective-permute-start.15 = (bf16[2,128,512]{2,1,0:T(8,128)(2,1)S(1)}, bf16[2,128,512]{2,1,0:T(8,128)(2,1)S(1)}, u32[]{:S(2)}, u32[]{:S(2)}) collective-permute-start(bf16[2,128,512]{2,1,0:T(8,128)(2,1)S(1)} %get-tuple-element.35), channel_id=1, source_target_pairs={{0,2},{1,3},{2,4},{3,5},{4,6},{5,7},{6,0},{7,1},{8,10},{9,11},{10,... | collective-permute-start | bytes 786440 | tf_op jit(solution)/shard_map/ppermute | solution.py:17
  40.9 2.0 %collective-permute-start.26 = (bf16[1,2,128,512]{3,2,1,0:T(8,128)(2,1)S(1)}, bf16[1,2,128,512]{3,2,1,0:T(8,128)(2,1)S(1)}, u32[]{:S(2)}, u32[]{:S(2)}) collective-permute-start(bf16[1,2,128,512]{3,2,1,0:T(8,128)(2,1)S(1)} %bitcast.36), channel_id=1, source_target_pairs={{0,16},{1,9},{2,18},{3,11},{4,20},{5,13},{6,22},{7,15},{8,24},{9,1... | collective-permute-start | bytes 786440 | tf_op jit(solution)/shard_map/ppermute | solution.py:33
  42.9 0.6 collective-permute-done.25.refs_3_
  43.6 1.5 %collective-permute-done.6 = bf16[2,128,512]{2,1,0:T(8,128)(2,1)S(1)} collective-permute-done((bf16[2,128,512]{2,1,0:T(8,128)(2,1)S(1)}, bf16[2,128,512]{2,1,0:T(8,128)(2,1)S(1)}, u32[]{:S(2)}, u32[]{:S(2)}) %collective-permute-start.6) | collective-permute-done | bytes 262176 | tf_op jit(solution)/shard_map/ppermute | solution.py:17
  45.1 1.5 %collective-permute-start.7 = (bf16[1,2,128,512]{3,2,1,0:T(8,128)(2,1)S(1)}, bf16[1,2,128,512]{3,2,1,0:T(8,128)(2,1)S(1)}, u32[]{:S(2)}, u32[]{:S(2)}) collective-permute-start(bf16[1,2,128,512]{3,2,1,0:T(8,128)(2,1)S(1)} %bitcast.31), channel_id=1, source_target_pairs={{0,8},{1,17},{2,10},{3,19},{4,12},{5,21},{6,14},{7,23},{8,0},{9,25... | collective-permute-start | bytes 786440 | tf_op jit(solution)/shard_map/ppermute | solution.py:33
  46.6 1.3 %collective-permute-start.11 = (bf16[2,2,128,512]{3,2,1,0:T(8,128)(2,1)S(1)}, bf16[2,2,128,512]{3,2,1,0:T(8,128)(2,1)S(1)}, u32[]{:S(2)}, u32[]{:S(2)}) collective-permute-start(bf16[2,2,128,512]{3,2,1,0:T(8,128)(2,1)S(1)} %pad_maximum_fusion.5), channel_id=1, source_target_pairs={{0,1},{2,3},{4,5},{6,7},{8,9},{10,11},{12,13},{14,15},{16,17},{18,... | collective-permute-start | bytes 1572872 | tf_op jit(solution)/shard_map/ppermute | solution.py:17
  48.0 1.9 %collective-permute-start.8 = (bf16[1,2,128,512]{3,2,1,0:T(8,128)(2,1)S(1)}, bf16[1,2,128,512]{3,2,1,0:T(8,128)(2,1)S(1)}, u32[]{:S(2)}, u32[]{:S(2)}) collective-permute-start(bf16[1,2,128,512]{3,2,1,0:T(8,128)(2,1)S(1)} %bitcast.32), channel_id=1, source_target_pairs={{0,16},{1,9},{2,18},{3,11},{4,20},{5,13},{6,22},{7,15},{8,24},{9,1... | collective-permute-start | bytes 786440 | tf_op jit(solution)/shard_map/ppermute | solution.py:33
  49.9 1.2 %collective-permute-start.20 = (bf16[1,2,128,512]{3,2,1,0:T(8,128)(2,1)S(1)}, bf16[1,2,128,512]{3,2,1,0:T(8,128)(2,1)S(1)}, u32[]{:S(2)}, u32[]{:S(2)}) collective-permute-start(bf16[1,2,128,512]{3,2,1,0:T(8,128)(2,1)S(1)} %bitcast.27), channel_id=1, source_target_pairs={{0,8},{1,17},{2,10},{3,19},{4,12},{5,21},{6,14},{7,23},{8,0},{9,25... | collective-permute-start | bytes 786440 | tf_op jit(solution)/shard_map/ppermute | solution.py:33
  51.1 0.9 collective-permute-done.27.refs_5_
  52.0 2.2 %collective-permute-start.21 = (bf16[1,2,128,512]{3,2,1,0:T(8,128)(2,1)S(1)}, bf16[1,2,128,512]{3,2,1,0:T(8,128)(2,1)S(1)}, u32[]{:S(2)}, u32[]{:S(2)}) collective-permute-start(bf16[1,2,128,512]{3,2,1,0:T(8,128)(2,1)S(1)} %bitcast.28), channel_id=1, source_target_pairs={{0,16},{1,9},{2,18},{3,11},{4,20},{5,13},{6,22},{7,15},{8,24},{9,1... | collective-permute-start | bytes 786440 | tf_op jit(solution)/shard_map/ppermute | solution.py:33
  54.5 1.2 %collective-permute-done.8.refs_4_ = bf16[1,2,128,512]{3,2,1,0:T(8,128)(2,1)S(1)} collective-permute-done((bf16[1,2,128,512]{3,2,1,0:T(8,128)(2,1)S(1)}, bf16[1,2,128,512]{3,2,1,0:T(8,128)(2,1)S(1)}, u32[]{:S(2)}, u32[]{:S(2)}) %collective-permute-start.8) | collective-permute-done | bytes 262176 | tf_op jit(solution)/shard_map/ppermute | solution.py:33
  55.7 2.3 %collective-permute-done.20.refs_3_ = bf16[1,2,128,512]{3,2,1,0:T(8,128)(2,1)S(1)} collective-permute-done((bf16[1,2,128,512]{3,2,1,0:T(8,128)(2,1)S(1)}, bf16[1,2,128,512]{3,2,1,0:T(8,128)(2,1)S(1)}, u32[]{:S(2)}, u32[]{:S(2)}) %collective-permute-start.20) | collective-permute-done | bytes 262176 | tf_op jit(solution)/shard_map/ppermute | solution.py:33
  58.1 1.7 %collective-permute-start.9 = (bf16[1,2,128,512]{3,2,1,0:T(8,128)(2,1)S(1)}, bf16[1,2,128,512]{3,2,1,0:T(8,128)(2,1)S(1)}, u32[]{:S(2)}, u32[]{:S(2)}) collective-permute-start(bf16[1,2,128,512]{3,2,1,0:T(8,128)(2,1)S(1)} %collective-permute-done.7.refs_3_), channel_id=1, source_target_pairs={{0,16},{1,9},{2,18},{3,11},{4,20},{5,13},{6,22},{7,15},{8,24},{9,1... | collective-permute-start | bytes 786440 | tf_op jit(solution)/shard_map/ppermute | solution.py:33
  59.8 0.7 collective-permute-start.12
  60.9 2.5 %collective-permute-done.16.refs_2_ = bf16[1,2,128,512]{3,2,1,0:T(8,128)(2,1)S(1)} collective-permute-done((bf16[1,2,128,512]{3,2,1,0:T(8,128)(2,1)S(1)}, bf16[1,2,128,512]{3,2,1,0:T(8,128)(2,1)S(1)}, u32[]{:S(2)}, u32[]{:S(2)}) %collective-permute-start.16) | collective-permute-done | bytes 262176 | tf_op jit(solution)/shard_map/ppermute | solution.py:17
  63.3 0.7 collective-permute-start.13
  64.0 1.7 %collective-permute-done.9.refs_5_ = bf16[1,2,128,512]{3,2,1,0:T(8,128)(2,1)S(1)} collective-permute-done((bf16[1,2,128,512]{3,2,1,0:T(8,128)(2,1)S(1)}, bf16[1,2,128,512]{3,2,1,0:T(8,128)(2,1)S(1)}, u32[]{:S(2)}, u32[]{:S(2)}) %collective-permute-start.9) | collective-permute-done | bytes 262176 | tf_op jit(solution)/shard_map/ppermute | solution.py:33
  65.7 2.1 %collective-permute-start.17 = (bf16[1,2,128,512]{3,2,1,0:T(8,128)(2,1)S(1)}, bf16[1,2,128,512]{3,2,1,0:T(8,128)(2,1)S(1)}, u32[]{:S(2)}, u32[]{:S(2)}) collective-permute-start(bf16[1,2,128,512]{3,2,1,0:T(8,128)(2,1)S(1)} %collective-permute-done.16.refs_2_), channel_id=1, source_target_pairs={{0,8},{1,17},{2,10},{3,19},{4,12},{5,21},{6,14},{7,23},{8,0},{9,25... | collective-permute-start | bytes 786440 | tf_op jit(solution)/shard_map/ppermute | solution.py:33
  67.9 3.4 %collective-permute-done.22.refs_5_ = bf16[1,2,128,512]{3,2,1,0:T(8,128)(2,1)S(1)} collective-permute-done((bf16[1,2,128,512]{3,2,1,0:T(8,128)(2,1)S(1)}, bf16[1,2,128,512]{3,2,1,0:T(8,128)(2,1)S(1)}, u32[]{:S(2)}, u32[]{:S(2)}) %collective-permute-start.22) | collective-permute-done | bytes 262176 | tf_op jit(solution)/shard_map/ppermute | solution.py:33
  71.5 3.5 %collective-permute-done.17.refs_3_ = bf16[1,2,128,512]{3,2,1,0:T(8,128)(2,1)S(1)} collective-permute-done((bf16[1,2,128,512]{3,2,1,0:T(8,128)(2,1)S(1)}, bf16[1,2,128,512]{3,2,1,0:T(8,128)(2,1)S(1)}, u32[]{:S(2)}, u32[]{:S(2)}) %collective-permute-start.17) | collective-permute-done | bytes 262176 | tf_op jit(solution)/shard_map/ppermute | solution.py:33
  74.9 1.3 %collective-permute-start.28 = (bf16[4,2,128,512]{3,2,1,0:T(8,128)(2,1)S(1)}, bf16[4,2,128,512]{3,2,1,0:T(8,128)(2,1)S(1)}, u32[]{:S(2)}, u32[]{:S(2)}) collective-permute-start(bf16[4,2,128,512]{3,2,1,0:T(8,128)(2,1)S(1)} %pad_maximum_fusion.2), channel_id=1, source_target_pairs={{1,2},{3,4},{5,6},{7,0},{9,10},{11,12},{13,14},{15,8},{17,18},{19,... | collective-permute-start | bytes 3145736 | tf_op jit(solution)/shard_map/ppermute | solution.py:17
  76.2 1.9 %collective-permute-start.23 = (bf16[4,2,128,512]{3,2,1,0:T(8,128)(2,1)S(1)}, bf16[4,2,128,512]{3,2,1,0:T(8,128)(2,1)S(1)}, u32[]{:S(2)}, u32[]{:S(2)}) collective-permute-start(bf16[4,2,128,512]{3,2,1,0:T(8,128)(2,1)S(1)} %pad_maximum_fusion.1), channel_id=1, source_target_pairs={{0,1},{1,0},{2,3},{3,2},{4,5},{5,4},{6,7},{7,6},{8,9},{9,8},{10,11... | collective-permute-start | bytes 3145736 | tf_op jit(solution)/shard_map/ppermute | solution.py:22
  78.3 1.3 %collective-permute-start.10 = (bf16[4,2,128,512]{3,2,1,0:T(8,128)(2,1)S(1)}, bf16[4,2,128,512]{3,2,1,0:T(8,128)(2,1)S(1)}, u32[]{:S(2)}, u32[]{:S(2)}) collective-permute-start(bf16[4,2,128,512]{3,2,1,0:T(8,128)(2,1)S(1)} %pad_maximum_fusion), channel_id=1, source_target_pairs={{1,2},{3,4},{5,6},{7,0},{9,10},{11,12},{13,14},{15,8},{17,18},{19,... | collective-permute-start | bytes 3145736 | tf_op jit(solution)/shard_map/ppermute | solution.py:17
  79.9 0.9 collective-permute-start.14
  81.0 2.6 %shard_map.49.refs_7_ = bf16[3,3,3,2,1,128,512]{6,5,4,3,2,1,0:T(8,128)(2,1)} custom-call(bf16[384,512]{1,0:T(8,128)(2,1)S(1)} %bitcast.21, bf16[384,512]{1,0:T(8,128)(2,1)S(1)} %bitcast.15, bf16[1,2,128,512]{3,2,1,0:T(8,128)(2,1)S(1)} %bitcast.38, bf16[1,2,128,512]{3,2,1,0:T(8,128)(2,1)S(1)} %collective-permute-done.25.refs_3_, ...), custom_call_target="tpu_custom_call" | custom-call | flops 1610612736 | bytes 1572864 | tf_op jit(solution)/shard_map/pallas_call | solution.py:267
  83.6 0.5 collective-permute-start.18
  84.1 1.6 %collective-permute-start.19 = (bf16[1,2,128,512]{3,2,1,0:T(8,128)(2,1)S(1)}, bf16[1,2,128,512]{3,2,1,0:T(8,128)(2,1)S(1)}, u32[]{:S(2)}, u32[]{:S(2)}) collective-permute-start(bf16[1,2,128,512]{3,2,1,0:T(8,128)(2,1)S(1)} %collective-permute-done.17.refs_3_), channel_id=1, source_target_pairs={{0,16},{1,9},{2,18},{3,11},{4,20},{5,13},{6,22},{7,15},{8,24},{9,1... | collective-permute-start | bytes 786440 | tf_op jit(solution)/shard_map/ppermute | solution.py:33
  85.7 2.6 %shard_map.50.refs_6_ = bf16[3,3,3,2,1,128,512]{6,5,4,3,2,1,0:T(8,128)(2,1)} custom-call(bf16[384,512]{1,0:T(8,128)(2,1)S(1)} %bitcast.22, bf16[384,512]{1,0:T(8,128)(2,1)S(1)} %bitcast.16, bf16[1,2,128,512]{3,2,1,0:T(8,128)(2,1)S(1)} %bitcast.34, bf16[1,2,128,512]{3,2,1,0:T(8,128)(2,1)S(1)} %collective-permute-done.7.refs_3_, ...), custom_call_target="tpu_custom_call", output_to_operand_aliasing={{}: (7, {})} | custom-call | flops 1610612736 | bytes 1572864 | tf_op jit(solution)/shard_map/pallas_call | solution.py:267
  88.3 1.8 %shard_map.51.refs_8_ = bf16[3,3,3,2,1,128,512]{6,5,4,3,2,1,0:T(8,128)(2,1)} custom-call(bf16[384,512]{1,0:T(8,128)(2,1)S(1)} %bitcast.23, bf16[384,512]{1,0:T(8,128)(2,1)S(1)} %bitcast.17, bf16[1,2,128,512]{3,2,1,0:T(8,128)(2,1)S(1)} %bitcast.30, bf16[1,2,128,512]{3,2,1,0:T(8,128)(2,1)S(1)} %collective-permute-done.20.refs_3_, ...), custom_call_target="tpu_custom_call", output_to_operand_aliasing={{}: (6, {})} | custom-call | flops 805306368 | bytes 786432 | tf_op jit(solution)/shard_map/pallas_call | solution.py:267
  90.0 2.8 %collective-permute-done.28.refs_3_ = bf16[4,2,128,512]{3,2,1,0:T(8,128)(2,1)S(1)} collective-permute-done((bf16[4,2,128,512]{3,2,1,0:T(8,128)(2,1)S(1)}, bf16[4,2,128,512]{3,2,1,0:T(8,128)(2,1)S(1)}, u32[]{:S(2)}, u32[]{:S(2)}) %collective-permute-start.28) | collective-permute-done | bytes 1048608 | tf_op jit(solution)/shard_map/ppermute | solution.py:17
  92.8 2.7 %shard_map.52.refs_6_ = bf16[3,3,3,2,1,128,512]{6,5,4,3,2,1,0:T(8,128)(2,1)} custom-call(bf16[384,512]{1,0:T(8,128)(2,1)S(1)} %bitcast.24, bf16[384,512]{1,0:T(8,128)(2,1)S(1)} %bitcast.18, bf16[4,2,128,512]{3,2,1,0:T(8,128)(2,1)S(1)} %collective-permute-done.23.refs_2_, ...), custom_call_target="tpu_custom_call", output_to_operand_aliasing={{}: (8, {})} | custom-call | flops 1610612736 | bytes 1572864 | tf_op jit(solution)/shard_map/pallas_call | solution.py:267
  95.6 1.7 %shard_map.53.refs_7_ = bf16[3,3,3,2,1,128,512]{6,5,4,3,2,1,0:T(8,128)(2,1)} custom-call(bf16[384,512]{1,0:T(8,128)(2,1)S(1)} %bitcast.25, bf16[384,512]{1,0:T(8,128)(2,1)S(1)} %bitcast.19, bf16[1,2,128,512]{3,2,1,0:T(8,128)(2,1)S(1)} %collective-permute-done.16.refs_2_, ...), custom_call_target="tpu_custom_call", output_to_operand_aliasing={{}: (6, {})} | custom-call | flops 805306368 | bytes 786432 | tf_op jit(solution)/shard_map/pallas_call | solution.py:267
  97.4 6.7 %collective-permute-done.10.refs_2_ = bf16[4,2,128,512]{3,2,1,0:T(8,128)(2,1)S(1)} collective-permute-done((bf16[4,2,128,512]{3,2,1,0:T(8,128)(2,1)S(1)}, bf16[4,2,128,512]{3,2,1,0:T(8,128)(2,1)S(1)}, u32[]{:S(2)}, u32[]{:S(2)}) %collective-permute-start.10) | collective-permute-done | bytes 1048608 | tf_op jit(solution)/shard_map/ppermute | solution.py:17
  104.1 1.7 %shard_map.54 = bf16[3,3,3,2,1,128,512]{6,5,4,3,2,1,0:T(8,128)(2,1)} custom-call(bf16[384,512]{1,0:T(8,128)(2,1)S(1)} %bitcast.26, bf16[384,512]{1,0:T(8,128)(2,1)S(1)} %bitcast.20, bf16[4,2,128,512]{3,2,1,0:T(8,128)(2,1)S(1)} %collective-permute-done.10.refs_2_, ...), custom_call_target="tpu_custom_call", output_to_operand_aliasing={{}: (7, {})} | custom-call | flops 805306368 | bytes 786432 | tf_op jit(solution)/shard_map/pallas_call | solution.py:267
  (41 shorter events, 2.4 us)
Async XLA Ops:
  4.7 11.6 %collective-permute-start = (bf16[2,2,128,512]{3,2,1,0:T(8,128)(2,1)S(1)}, bf16[2,2,128,512]{3,2,1,0:T(8,128)(2,1)S(1)}, u32[]{:S(2)}, u32[]{:S(2)}) collective-permute-start(bf16[2,2,128,512]{3,2,1,0:T(8,128)(2,1)S(1)} %get-tuple-element.22), channel_id=1, source_target_pairs={{0,8},{1,17},{2,10},{3,19},{4,12},{5,21},{6,14},{7,23},{8,0},{9,25... | collective-permute-start | bytes 1572872 | tf_op jit(solution)/shard_map/ppermute | solution.py:33
  11.0 11.8 %collective-permute-start.2 = (bf16[2,2,128,512]{3,2,1,0:T(8,128)(2,1)S(1)}, bf16[2,2,128,512]{3,2,1,0:T(8,128)(2,1)S(1)}, u32[]{:S(2)}, u32[]{:S(2)}) collective-permute-start(bf16[2,2,128,512]{3,2,1,0:T(8,128)(2,1)S(1)} %get-tuple-element.26), channel_id=1, source_target_pairs={{0,8},{1,17},{2,10},{3,19},{4,12},{5,21},{6,14},{7,23},{8,0},{9,25... | collective-permute-start | bytes 1572872 | tf_op jit(solution)/shard_map/ppermute | solution.py:33
  14.2 17.5 %collective-permute-start.4 = (bf16[2,2,128,512]{3,2,1,0:T(8,128)(2,1)S(1)}, bf16[2,2,128,512]{3,2,1,0:T(8,128)(2,1)S(1)}, u32[]{:S(2)}, u32[]{:S(2)}) collective-permute-start(bf16[2,2,128,512]{3,2,1,0:T(8,128)(2,1)S(1)} %get-tuple-element.29), channel_id=1, source_target_pairs={{0,8},{1,17},{2,10},{3,19},{4,12},{5,21},{6,14},{7,23},{8,0},{9,25... | collective-permute-start | bytes 1572872 | tf_op jit(solution)/shard_map/ppermute | solution.py:33
  16.5 9.6 %collective-permute-start.1 = (bf16[1,2,128,512]{3,2,1,0:T(8,128)(2,1)S(1)}, bf16[1,2,128,512]{3,2,1,0:T(8,128)(2,1)S(1)}, u32[]{:S(2)}, u32[]{:S(2)}) collective-permute-start(bf16[1,2,128,512]{3,2,1,0:T(8,128)(2,1)S(1)} %slice.35), channel_id=1, source_target_pairs={{0,16},{1,9},{2,18},{3,11},{4,20},{5,13},{6,22},{7,15},{8,24},{9,1... | collective-permute-start | bytes 786440 | tf_op jit(solution)/shard_map/ppermute | solution.py:33
  23.0 13.2 %collective-permute-start.3 = (bf16[1,2,128,512]{3,2,1,0:T(8,128)(2,1)S(1)}, bf16[1,2,128,512]{3,2,1,0:T(8,128)(2,1)S(1)}, u32[]{:S(2)}, u32[]{:S(2)}) collective-permute-start(bf16[1,2,128,512]{3,2,1,0:T(8,128)(2,1)S(1)} %slice.37), channel_id=1, source_target_pairs={{0,16},{1,9},{2,18},{3,11},{4,20},{5,13},{6,22},{7,15},{8,24},{9,1... | collective-permute-start | bytes 786440 | tf_op jit(solution)/shard_map/ppermute | solution.py:33
  26.2 8.7 %collective-permute-start.24 = (bf16[2,128,512]{2,1,0:T(8,128)(2,1)S(1)}, bf16[2,128,512]{2,1,0:T(8,128)(2,1)S(1)}, u32[]{:S(2)}, u32[]{:S(2)}) collective-permute-start(bf16[2,128,512]{2,1,0:T(8,128)(2,1)S(1)} %bitcast.39), channel_id=1, source_target_pairs={{0,2},{1,3},{2,4},{3,5},{4,6},{5,7},{6,0},{7,1},{8,10},{9,11},{10,... | collective-permute-start | bytes 786440 | tf_op jit(solution)/shard_map/ppermute | solution.py:17
  31.9 7.4 %collective-permute-start.5 = (bf16[1,2,128,512]{3,2,1,0:T(8,128)(2,1)S(1)}, bf16[1,2,128,512]{3,2,1,0:T(8,128)(2,1)S(1)}, u32[]{:S(2)}, u32[]{:S(2)}) collective-permute-start(bf16[1,2,128,512]{3,2,1,0:T(8,128)(2,1)S(1)} %slice.39), channel_id=1, source_target_pairs={{0,16},{1,9},{2,18},{3,11},{4,20},{5,13},{6,22},{7,15},{8,24},{9,1... | collective-permute-start | bytes 786440 | tf_op jit(solution)/shard_map/ppermute | solution.py:33
  34.9 8.7 %collective-permute-start.25 = (bf16[1,2,128,512]{3,2,1,0:T(8,128)(2,1)S(1)}, bf16[1,2,128,512]{3,2,1,0:T(8,128)(2,1)S(1)}, u32[]{:S(2)}, u32[]{:S(2)}) collective-permute-start(bf16[1,2,128,512]{3,2,1,0:T(8,128)(2,1)S(1)} %bitcast.35), channel_id=1, source_target_pairs={{0,8},{1,17},{2,10},{3,19},{4,12},{5,21},{6,14},{7,23},{8,0},{9,25... | collective-permute-start | bytes 786440 | tf_op jit(solution)/shard_map/ppermute | solution.py:33
  36.3 8.8 %collective-permute-start.6 = (bf16[2,128,512]{2,1,0:T(8,128)(2,1)S(1)}, bf16[2,128,512]{2,1,0:T(8,128)(2,1)S(1)}, u32[]{:S(2)}, u32[]{:S(2)}) collective-permute-start(bf16[2,128,512]{2,1,0:T(8,128)(2,1)S(1)} %bitcast.41), channel_id=1, source_target_pairs={{0,2},{1,3},{2,4},{3,5},{4,6},{5,7},{6,0},{7,1},{8,10},{9,11},{10,... | collective-permute-start | bytes 786440 | tf_op jit(solution)/shard_map/ppermute | solution.py:17
  39.4 8.6 %collective-permute-start.15 = (bf16[2,128,512]{2,1,0:T(8,128)(2,1)S(1)}, bf16[2,128,512]{2,1,0:T(8,128)(2,1)S(1)}, u32[]{:S(2)}, u32[]{:S(2)}) collective-permute-start(bf16[2,128,512]{2,1,0:T(8,128)(2,1)S(1)} %get-tuple-element.35), channel_id=1, source_target_pairs={{0,2},{1,3},{2,4},{3,5},{4,6},{5,7},{6,0},{7,1},{8,10},{9,11},{10,... | collective-permute-start | bytes 786440 | tf_op jit(solution)/shard_map/ppermute | solution.py:17
  40.9 9.0 %collective-permute-start.26 = (bf16[1,2,128,512]{3,2,1,0:T(8,128)(2,1)S(1)}, bf16[1,2,128,512]{3,2,1,0:T(8,128)(2,1)S(1)}, u32[]{:S(2)}, u32[]{:S(2)}) collective-permute-start(bf16[1,2,128,512]{3,2,1,0:T(8,128)(2,1)S(1)} %bitcast.36), channel_id=1, source_target_pairs={{0,16},{1,9},{2,18},{3,11},{4,20},{5,13},{6,22},{7,15},{8,24},{9,1... | collective-permute-start | bytes 786440 | tf_op jit(solution)/shard_map/ppermute | solution.py:33
  43.5 8.5 %collective-permute-start.27 = (bf16[1,2,128,512]{3,2,1,0:T(8,128)(2,1)S(1)}, bf16[1,2,128,512]{3,2,1,0:T(8,128)(2,1)S(1)}, u32[]{:S(2)}, u32[]{:S(2)}) collective-permute-start(bf16[1,2,128,512]{3,2,1,0:T(8,128)(2,1)S(1)} %collective-permute-done.25.refs_3_), channel_id=1, source_target_pairs={{0,16},{1,9},{2,18},{3,11},{4,20},{5,13},{6,22},{7,15},{8,24},{9,1... | collective-permute-start | bytes 786440 | tf_op jit(solution)/shard_map/ppermute | solution.py:33
  45.1 9.3 %collective-permute-start.7 = (bf16[1,2,128,512]{3,2,1,0:T(8,128)(2,1)S(1)}, bf16[1,2,128,512]{3,2,1,0:T(8,128)(2,1)S(1)}, u32[]{:S(2)}, u32[]{:S(2)}) collective-permute-start(bf16[1,2,128,512]{3,2,1,0:T(8,128)(2,1)S(1)} %bitcast.31), channel_id=1, source_target_pairs={{0,8},{1,17},{2,10},{3,19},{4,12},{5,21},{6,14},{7,23},{8,0},{9,25... | collective-permute-start | bytes 786440 | tf_op jit(solution)/shard_map/ppermute | solution.py:33
  46.6 13.1 %collective-permute-start.11 = (bf16[2,2,128,512]{3,2,1,0:T(8,128)(2,1)S(1)}, bf16[2,2,128,512]{3,2,1,0:T(8,128)(2,1)S(1)}, u32[]{:S(2)}, u32[]{:S(2)}) collective-permute-start(bf16[2,2,128,512]{3,2,1,0:T(8,128)(2,1)S(1)} %pad_maximum_fusion.5), channel_id=1, source_target_pairs={{0,1},{2,3},{4,5},{6,7},{8,9},{10,11},{12,13},{14,15},{16,17},{18,... | collective-permute-start | bytes 1572872 | tf_op jit(solution)/shard_map/ppermute | solution.py:17
  48.0 7.8 %collective-permute-start.8 = (bf16[1,2,128,512]{3,2,1,0:T(8,128)(2,1)S(1)}, bf16[1,2,128,512]{3,2,1,0:T(8,128)(2,1)S(1)}, u32[]{:S(2)}, u32[]{:S(2)}) collective-permute-start(bf16[1,2,128,512]{3,2,1,0:T(8,128)(2,1)S(1)} %bitcast.32), channel_id=1, source_target_pairs={{0,16},{1,9},{2,18},{3,11},{4,20},{5,13},{6,22},{7,15},{8,24},{9,1... | collective-permute-start | bytes 786440 | tf_op jit(solution)/shard_map/ppermute | solution.py:33
  49.9 8.2 %collective-permute-start.20 = (bf16[1,2,128,512]{3,2,1,0:T(8,128)(2,1)S(1)}, bf16[1,2,128,512]{3,2,1,0:T(8,128)(2,1)S(1)}, u32[]{:S(2)}, u32[]{:S(2)}) collective-permute-start(bf16[1,2,128,512]{3,2,1,0:T(8,128)(2,1)S(1)} %bitcast.27), channel_id=1, source_target_pairs={{0,8},{1,17},{2,10},{3,19},{4,12},{5,21},{6,14},{7,23},{8,0},{9,25... | collective-permute-start | bytes 786440 | tf_op jit(solution)/shard_map/ppermute | solution.py:33
  52.0 8.5 %collective-permute-start.21 = (bf16[1,2,128,512]{3,2,1,0:T(8,128)(2,1)S(1)}, bf16[1,2,128,512]{3,2,1,0:T(8,128)(2,1)S(1)}, u32[]{:S(2)}, u32[]{:S(2)}) collective-permute-start(bf16[1,2,128,512]{3,2,1,0:T(8,128)(2,1)S(1)} %bitcast.28), channel_id=1, source_target_pairs={{0,16},{1,9},{2,18},{3,11},{4,20},{5,13},{6,22},{7,15},{8,24},{9,1... | collective-permute-start | bytes 786440 | tf_op jit(solution)/shard_map/ppermute | solution.py:33
  54.4 25.5 %collective-permute-start.30 = (bf16[4,2,128,512]{3,2,1,0:T(8,128)(2,1)S(1)}, bf16[4,2,128,512]{3,2,1,0:T(8,128)(2,1)S(1)}, u32[]{:S(2)}, u32[]{:S(2)}) collective-permute-start(bf16[4,2,128,512]{3,2,1,0:T(8,128)(2,1)S(1)} %pad_maximum_fusion.2), channel_id=1, source_target_pairs={{0,1},{1,0},{2,3},{3,2},{4,5},{5,4},{6,7},{7,6},{8,9},{9,8},{10,11... | collective-permute-start | bytes 3145736 | tf_op jit(solution)/shard_map/ppermute | solution.py:22
  55.7 7.6 %collective-permute-start.16 = (bf16[1,2,128,512]{3,2,1,0:T(8,128)(2,1)S(1)}, bf16[1,2,128,512]{3,2,1,0:T(8,128)(2,1)S(1)}, u32[]{:S(2)}, u32[]{:S(2)}) collective-permute-start(bf16[1,2,128,512]{3,2,1,0:T(8,128)(2,1)S(1)} %select_bitcast_fusion), channel_id=1, source_target_pairs={{0,1},{1,2},{2,3},{3,4},{4,5},{5,6},{6,7},{7,0},{8,9},{9,10},{10,1... | collective-permute-start | bytes 786440 | tf_op jit(solution)/shard_map/ppermute | solution.py:17
  58.1 7.6 %collective-permute-start.9 = (bf16[1,2,128,512]{3,2,1,0:T(8,128)(2,1)S(1)}, bf16[1,2,128,512]{3,2,1,0:T(8,128)(2,1)S(1)}, u32[]{:S(2)}, u32[]{:S(2)}) collective-permute-start(bf16[1,2,128,512]{3,2,1,0:T(8,128)(2,1)S(1)} %collective-permute-done.7.refs_3_), channel_id=1, source_target_pairs={{0,16},{1,9},{2,18},{3,11},{4,20},{5,13},{6,22},{7,15},{8,24},{9,1... | collective-permute-start | bytes 786440 | tf_op jit(solution)/shard_map/ppermute | solution.py:33
  59.8 16.5 %collective-permute-start.12 = (bf16[2,2,128,512]{3,2,1,0:T(8,128)(2,1)S(1)}, bf16[2,2,128,512]{3,2,1,0:T(8,128)(2,1)S(1)}, u32[]{:S(2)}, u32[]{:S(2)}) collective-permute-start(bf16[2,2,128,512]{3,2,1,0:T(8,128)(2,1)S(1)} %collective-permute-done.11.refs_4_.refs_3_), channel_id=1, source_target_pairs={{1,17},{3,19},{5,21},{7,23},{9,25},{11,27},{13,29},{15,31},{17,1},... | collective-permute-start | bytes 1572872 | tf_op jit(solution)/shard_map/ppermute | solution.py:33
  60.5 10.8 %collective-permute-start.22 = (bf16[1,2,128,512]{3,2,1,0:T(8,128)(2,1)S(1)}, bf16[1,2,128,512]{3,2,1,0:T(8,128)(2,1)S(1)}, u32[]{:S(2)}, u32[]{:S(2)}) collective-permute-start(bf16[1,2,128,512]{3,2,1,0:T(8,128)(2,1)S(1)} %collective-permute-done.20.refs_3_), channel_id=1, source_target_pairs={{0,16},{1,9},{2,18},{3,11},{4,20},{5,13},{6,22},{7,15},{8,24},{9,1... | collective-permute-start | bytes 786440 | tf_op jit(solution)/shard_map/ppermute | solution.py:33
  63.3 14.9 %collective-permute-start.13 = (bf16[2,2,128,512]{3,2,1,0:T(8,128)(2,1)S(1)}, bf16[2,2,128,512]{3,2,1,0:T(8,128)(2,1)S(1)}, u32[]{:S(2)}, u32[]{:S(2)}) collective-permute-start(bf16[2,2,128,512]{3,2,1,0:T(8,128)(2,1)S(1)} %collective-permute-done.11.refs_4_.refs_3_), channel_id=1, source_target_pairs={{1,9},{3,11},{5,13},{7,15},{9,1},{11,3},{13,5},{15,7},{17,25},{19,... | collective-permute-start | bytes 1572872 | tf_op jit(solution)/shard_map/ppermute | solution.py:33
  65.7 9.2 %collective-permute-start.17 = (bf16[1,2,128,512]{3,2,1,0:T(8,128)(2,1)S(1)}, bf16[1,2,128,512]{3,2,1,0:T(8,128)(2,1)S(1)}, u32[]{:S(2)}, u32[]{:S(2)}) collective-permute-start(bf16[1,2,128,512]{3,2,1,0:T(8,128)(2,1)S(1)} %collective-permute-done.16.refs_2_), channel_id=1, source_target_pairs={{0,8},{1,17},{2,10},{3,19},{4,12},{5,21},{6,14},{7,23},{8,0},{9,25... | collective-permute-start | bytes 786440 | tf_op jit(solution)/shard_map/ppermute | solution.py:33
  71.3 12.8 %collective-permute-start.29 = (bf16[4,2,128,512]{3,2,1,0:T(8,128)(2,1)S(1)}, bf16[4,2,128,512]{3,2,1,0:T(8,128)(2,1)S(1)}, u32[]{:S(2)}, u32[]{:S(2)}) collective-permute-start(bf16[4,2,128,512]{3,2,1,0:T(8,128)(2,1)S(1)} %pad_maximum_fusion), channel_id=1, source_target_pairs={{0,1},{1,0},{2,3},{3,2},{4,5},{5,4},{6,7},{7,6},{8,9},{9,8},{10,11... | collective-permute-start | bytes 3145736 | tf_op jit(solution)/shard_map/ppermute | solution.py:22
  74.9 17.9 %collective-permute-start.28 = (bf16[4,2,128,512]{3,2,1,0:T(8,128)(2,1)S(1)}, bf16[4,2,128,512]{3,2,1,0:T(8,128)(2,1)S(1)}, u32[]{:S(2)}, u32[]{:S(2)}) collective-permute-start(bf16[4,2,128,512]{3,2,1,0:T(8,128)(2,1)S(1)} %pad_maximum_fusion.2), channel_id=1, source_target_pairs={{1,2},{3,4},{5,6},{7,0},{9,10},{11,12},{13,14},{15,8},{17,18},{19,... | collective-permute-start | bytes 3145736 | tf_op jit(solution)/shard_map/ppermute | solution.py:17
  76.2 16.6 %collective-permute-start.23 = (bf16[4,2,128,512]{3,2,1,0:T(8,128)(2,1)S(1)}, bf16[4,2,128,512]{3,2,1,0:T(8,128)(2,1)S(1)}, u32[]{:S(2)}, u32[]{:S(2)}) collective-permute-start(bf16[4,2,128,512]{3,2,1,0:T(8,128)(2,1)S(1)} %pad_maximum_fusion.1), channel_id=1, source_target_pairs={{0,1},{1,0},{2,3},{3,2},{4,5},{5,4},{6,7},{7,6},{8,9},{9,8},{10,11... | collective-permute-start | bytes 3145736 | tf_op jit(solution)/shard_map/ppermute | solution.py:22
  78.3 25.8 %collective-permute-start.10 = (bf16[4,2,128,512]{3,2,1,0:T(8,128)(2,1)S(1)}, bf16[4,2,128,512]{3,2,1,0:T(8,128)(2,1)S(1)}, u32[]{:S(2)}, u32[]{:S(2)}) collective-permute-start(bf16[4,2,128,512]{3,2,1,0:T(8,128)(2,1)S(1)} %pad_maximum_fusion), channel_id=1, source_target_pairs={{1,2},{3,4},{5,6},{7,0},{9,10},{11,12},{13,14},{15,8},{17,18},{19,... | collective-permute-start | bytes 3145736 | tf_op jit(solution)/shard_map/ppermute | solution.py:17
  79.9 3.7 %collective-permute-start.14 = (bf16[2,2,128,512]{3,2,1,0:T(8,128)(2,1)S(1)}, bf16[2,2,128,512]{3,2,1,0:T(8,128)(2,1)S(1)}, u32[]{:S(2)}, u32[]{:S(2)}) collective-permute-start(bf16[2,2,128,512]{3,2,1,0:T(8,128)(2,1)S(1)} %collective-permute-done.12.refs_5_.refs_4_), channel_id=1, source_target_pairs={{1,9},{3,11},{5,13},{7,15},{9,1},{11,3},{13,5},{15,7},{17,25},{19,... | collective-permute-start | bytes 1572872 | tf_op jit(solution)/shard_map/ppermute | solution.py:33
  83.6 12.0 %collective-permute-start.18 = (bf16[1,2,128,512]{3,2,1,0:T(8,128)(2,1)S(1)}, bf16[1,2,128,512]{3,2,1,0:T(8,128)(2,1)S(1)}, u32[]{:S(2)}, u32[]{:S(2)}) collective-permute-start(bf16[1,2,128,512]{3,2,1,0:T(8,128)(2,1)S(1)} %collective-permute-done.16.refs_2_), channel_id=1, source_target_pairs={{0,16},{1,9},{2,18},{3,11},{4,20},{5,13},{6,22},{7,15},{8,24},{9,1... | collective-permute-start | bytes 786440 | tf_op jit(solution)/shard_map/ppermute | solution.py:33
  84.1 11.5 %collective-permute-start.19 = (bf16[1,2,128,512]{3,2,1,0:T(8,128)(2,1)S(1)}, bf16[1,2,128,512]{3,2,1,0:T(8,128)(2,1)S(1)}, u32[]{:S(2)}, u32[]{:S(2)}) collective-permute-start(bf16[1,2,128,512]{3,2,1,0:T(8,128)(2,1)S(1)} %collective-permute-done.17.refs_3_), channel_id=1, source_target_pairs={{0,16},{1,9},{2,18},{3,11},{4,20},{5,13},{6,22},{7,15},{8,24},{9,1... | collective-permute-start | bytes 786440 | tf_op jit(solution)/shard_map/ppermute | solution.py:33

commit v4 on v3

--- a/solution.py
+++ b/solution.py
@@ -305,8 +305,8 @@
     halves = products(live_rows, source_times, sink_vectors, propagators, sections)
     own = [reduced(*halves[s], width) for s in range(sources)]
     second = [shifted(own[s], 2) for s in range(sources)]
-    forwarded = tuple(range(sources - 1))
-    groups = (forwarded, (sources - 1,))
+    forwarded = (0,)
+    groups = (forwarded, tuple(range(1, sources)))
     last = {}
     for group in groups:
         chosen = jnp.stack(
@@ -360,8 +360,9 @@
 
     result = None
     tail = sources - 1
-    calls = [[(1, s), (0, s)] for s in range(tail)] + [[(1, tail)], [(0, tail), (2, 0)]]
-    calls += [[(2, s)] for s in range(tail, 0, -1)]
+    middle = [(kind, s) for s in range(1, tail) for kind in (1, 0)]
+    calls = [[(1, 0), (0, 0)], middle + [(1, tail)], [(0, tail), (2, 0)]]
+    calls += [[(2, s) for s in range(1, sources)]]
     for jobs in calls:
         result = step(result, jobs)
     return result

time: 106 us -> 107 us (level); the launches traced: 106 us -> 105 us
  waiting for transfers between devices: 37.3 us -> 45.9 us
  starting transfers between devices: 42.2 us -> 34.8 us
  Pallas kernels: 24.2 us -> 22.4 us
    ppermute x21, waiting for transfers between devices: 23.7 us -> 38.1 us  [exchanged(): return lax.ppermute(value, ('sec', 'ta'), pairs)]
    ppermute x21, starting transfers between devices: 31.6 us -> 25.7 us  [exchanged(): return lax.ppermute(value, ('sec', 'ta'), pairs)]
    ppermute x7 -> x6, waiting for transfers between devices: 13.5 us -> 7.78 us  [shifted(): return lax.ppermute(value, 'ta', pairs)]
    pallas_call x6 -> x4, Pallas kernels: 13.1 us -> 11.3 us  [sandwich(): pl.pallas_call(functools.partial(sandwich_kernel, 0.5 * order ** (-0.5),...]
    ppermute x7 -> x6, starting transfers between devices: 8.69 us -> 7.88 us  [shifted(): return lax.ppermute(value, 'ta', pairs)]
  transfers between devices with their start and end apart: 31 -> 30, of which waited for: 14 -> 13; matrix products, arithmetic and copies ran while one was open for 2% -> 2% of each run, Pallas kernels for 17% -> 14%
where the time goes in v4:
time: 107 us; the launch traced here: 105 us
  waiting for transfers between devices  45.9 us (43%)
  starting transfers between devices  34.8 us (33%)
  Pallas kernels  22.4 us (21%)
  other arithmetic  1.32 us (1%)
    ppermute x21, waiting for transfers between devices, exchanged(): return lax.ppermute(value, ('sec', 'ta'), pairs)  38.1 us
    ppermute x21, starting transfers between devices, exchanged(): return lax.ppermute(value, ('sec', 'ta'), pairs)  25.7 us
    pallas_call x4, Pallas kernels, sandwich(): pl.pallas_call(functools.partial(sandwich_kernel, 0.5 * order ** (-0.5),...  11.3 us
    pallas_call x3, Pallas kernels, products(): pl.pallas_call(functools.partial(product_kernel, sections, source, source...  11.1 us
    ppermute x6, starting transfers between devices, shifted(): return lax.ppermute(value, 'ta', pairs)  7.88 us
    ppermute x6, waiting for transfers between devices, shifted(): return lax.ppermute(value, 'ta', pairs)  7.78 us
  transfers between devices with their start and end apart: 30, of which 13 were waited for; matrix products, arithmetic and copies ran while one was open for 2% of the time, Pallas kernels for 14%

profile of v4, /device:TPU:0, one launch (start us, length us, event | category | flops | bytes accessed | tf_op | source)
XLA Modules:
  0.0 105.4 jit_solution(3247273785282832051)
XLA Ops:
  0.0 4.7 %shard_map.46 = (bf16[2,2,128,512]{3,2,1,0:T(8,128)(2,1)S(1)}, bf16[2,2,128,512]{3,2,1,0:T(8,128)(2,1)S(1)}, bf16[2,1024,512]{2,1,0:T(8,128)(2,1)S(1)}, bf16[2,1024,512]{2,1,0:T(8,128)(2,1)S(1)}) custom-call(s32[4]{0:T(128)} %refs_0_.3, s32[3]{0:T(128)} %refs_0_.5, bf16[2,1,1024,512]{3,2,1,0:T(8,128)(2,1)} %refs_2_, bf16[3,2,1,1024,512]{4,3,2,1,0:T(8,128)(2,1)} %refs_3_.5), custom_call_target="tpu_custom_call" | custom-call | flops 2147483648 | bytes 2097152 | tf_op jit(solution)/shard_map/pallas_call | solution.py:153
  4.7 3.0 %collective-permute-start = (bf16[2,2,128,512]{3,2,1,0:T(8,128)(2,1)S(1)}, bf16[2,2,128,512]{3,2,1,0:T(8,128)(2,1)S(1)}, u32[]{:S(2)}, u32[]{:S(2)}) collective-permute-start(bf16[2,2,128,512]{3,2,1,0:T(8,128)(2,1)S(1)} %get-tuple-element.22), channel_id=1, source_target_pairs={{0,8},{1,17},{2,10},{3,19},{4,12},{5,21},{6,14},{7,23},{8,0},{9,25... | collective-permute-start | bytes 1572872 | tf_op jit(solution)/shard_map/ppermute | solution.py:33
  7.7 3.3 %shard_map.47 = (bf16[2,2,128,512]{3,2,1,0:T(8,128)(2,1)S(1)}, bf16[2,2,128,512]{3,2,1,0:T(8,128)(2,1)S(1)}, bf16[2,1024,512]{2,1,0:T(8,128)(2,1)S(1)}) custom-call(s32[3]{0:T(128)} %refs_0_.5, bf16[2,1024,512]{2,1,0:T(8,128)(2,1)S(1)} %get-tuple-element.23.refs_1_, bf16[2,1024,512]{2,1,0:T(8,128)(2,1)S(1)} %get-tuple-element.24.refs_2_, ...), custom_call_target="tpu_custom_call" | custom-call | flops 2147483648 | bytes 2097152 | tf_op jit(solution)/shard_map/pallas_call | solution.py:153
  11.1 3.2 %shard_map.48 = (bf16[2,2,128,512]{3,2,1,0:T(8,128)(2,1)S(1)}, bf16[2,2,128,512]{3,2,1,0:T(8,128)(2,1)S(1)}) custom-call(s32[3]{0:T(128)} %refs_0_.5, bf16[2,1024,512]{2,1,0:T(8,128)(2,1)S(1)} %get-tuple-element.23.refs_1_, bf16[2,1024,512]{2,1,0:T(8,128)(2,1)S(1)} %get-tuple-element.27.refs_2_, bf16[3,2,1,1024,512]{4,3,2,1,0:T(8,128)(2,1)} %refs_3_.5), custom_call_target="tpu_custom_call" | custom-call | flops 2147483648 | bytes 2097152 | tf_op jit(solution)/shard_map/pallas_call | solution.py:153
  14.2 2.1 %collective-permute-start.4 = (bf16[2,2,128,512]{3,2,1,0:T(8,128)(2,1)S(1)}, bf16[2,2,128,512]{3,2,1,0:T(8,128)(2,1)S(1)}, u32[]{:S(2)}, u32[]{:S(2)}) collective-permute-start(bf16[2,2,128,512]{3,2,1,0:T(8,128)(2,1)S(1)} %get-tuple-element.29), channel_id=1, source_target_pairs={{0,8},{1,17},{2,10},{3,19},{4,12},{5,21},{6,14},{7,23},{8,0},{9,25... | collective-permute-start | bytes 1572872 | tf_op jit(solution)/shard_map/ppermute | solution.py:33
  16.5 1.7 %collective-permute-start.1 = (bf16[1,2,128,512]{3,2,1,0:T(8,128)(2,1)S(1)}, bf16[1,2,128,512]{3,2,1,0:T(8,128)(2,1)S(1)}, u32[]{:S(2)}, u32[]{:S(2)}) collective-permute-start(bf16[1,2,128,512]{3,2,1,0:T(8,128)(2,1)S(1)} %slice.35), channel_id=1, source_target_pairs={{0,16},{1,9},{2,18},{3,11},{4,20},{5,13},{6,22},{7,15},{8,24},{9,1... | collective-permute-start | bytes 786440 | tf_op jit(solution)/shard_map/ppermute | solution.py:33
  18.1 4.7 %collective-permute-done.2 = bf16[2,2,128,512]{3,2,1,0:T(8,128)(2,1)S(1)} collective-permute-done((bf16[2,2,128,512]{3,2,1,0:T(8,128)(2,1)S(1)}, bf16[2,2,128,512]{3,2,1,0:T(8,128)(2,1)S(1)}, u32[]{:S(2)}, u32[]{:S(2)}) %collective-permute-start.2) | collective-permute-done | bytes 524320 | tf_op jit(solution)/shard_map/ppermute | solution.py:33
  23.0 3.1 %collective-permute-start.3 = (bf16[1,2,128,512]{3,2,1,0:T(8,128)(2,1)S(1)}, bf16[1,2,128,512]{3,2,1,0:T(8,128)(2,1)S(1)}, u32[]{:S(2)}, u32[]{:S(2)}) collective-permute-start(bf16[1,2,128,512]{3,2,1,0:T(8,128)(2,1)S(1)} %slice.37), channel_id=1, source_target_pairs={{0,16},{1,9},{2,18},{3,11},{4,20},{5,13},{6,22},{7,15},{8,24},{9,1... | collective-permute-start | bytes 786440 | tf_op jit(solution)/shard_map/ppermute | solution.py:33
  26.1 5.6 %collective-permute-done.4 = bf16[2,2,128,512]{3,2,1,0:T(8,128)(2,1)S(1)} collective-permute-done((bf16[2,2,128,512]{3,2,1,0:T(8,128)(2,1)S(1)}, bf16[2,2,128,512]{3,2,1,0:T(8,128)(2,1)S(1)}, u32[]{:S(2)}, u32[]{:S(2)}) %collective-permute-start.4) | collective-permute-done | bytes 524320 | tf_op jit(solution)/shard_map/ppermute | solution.py:33
  31.9 2.9 %collective-permute-start.5 = (bf16[1,2,128,512]{3,2,1,0:T(8,128)(2,1)S(1)}, bf16[1,2,128,512]{3,2,1,0:T(8,128)(2,1)S(1)}, u32[]{:S(2)}, u32[]{:S(2)}) collective-permute-start(bf16[1,2,128,512]{3,2,1,0:T(8,128)(2,1)S(1)} %slice.39), channel_id=1, source_target_pairs={{0,16},{1,9},{2,18},{3,11},{4,20},{5,13},{6,22},{7,15},{8,24},{9,1... | collective-permute-start | bytes 786440 | tf_op jit(solution)/shard_map/ppermute | solution.py:33
  34.9 1.6 %collective-permute-start.16 = (bf16[2,128,512]{2,1,0:T(8,128)(2,1)S(1)}, bf16[2,128,512]{2,1,0:T(8,128)(2,1)S(1)}, u32[]{:S(2)}, u32[]{:S(2)}) collective-permute-start(bf16[2,128,512]{2,1,0:T(8,128)(2,1)S(1)} %bitcast.39), channel_id=1, source_target_pairs={{0,2},{1,3},{2,4},{3,5},{4,6},{5,7},{6,0},{7,1},{8,10},{9,11},{10,... | collective-permute-start | bytes 786440 | tf_op jit(solution)/shard_map/ppermute | solution.py:17
  36.6 1.6 %collective-permute-start.6 = (bf16[2,128,512]{2,1,0:T(8,128)(2,1)S(1)}, bf16[2,128,512]{2,1,0:T(8,128)(2,1)S(1)}, u32[]{:S(2)}, u32[]{:S(2)}) collective-permute-start(bf16[2,128,512]{2,1,0:T(8,128)(2,1)S(1)} %get-tuple-element.35), channel_id=1, source_target_pairs={{0,2},{1,3},{2,4},{3,5},{4,6},{5,7},{6,0},{7,1},{8,10},{9,11},{10,... | collective-permute-start | bytes 786440 | tf_op jit(solution)/shard_map/ppermute | solution.py:17
  38.3 0.9 collective-permute-done.5
  39.3 2.0 %collective-permute-start.7 = (bf16[2,128,512]{2,1,0:T(8,128)(2,1)S(1)}, bf16[2,128,512]{2,1,0:T(8,128)(2,1)S(1)}, u32[]{:S(2)}, u32[]{:S(2)}) collective-permute-start(bf16[2,128,512]{2,1,0:T(8,128)(2,1)S(1)} %get-tuple-element.37), channel_id=1, source_target_pairs={{0,2},{1,3},{2,4},{3,5},{4,6},{5,7},{6,0},{7,1},{8,10},{9,11},{10,... | collective-permute-start | bytes 786440 | tf_op jit(solution)/shard_map/ppermute | solution.py:17
  41.3 4.7 %collective-permute-done.16 = bf16[2,128,512]{2,1,0:T(8,128)(2,1)S(1)} collective-permute-done((bf16[2,128,512]{2,1,0:T(8,128)(2,1)S(1)}, bf16[2,128,512]{2,1,0:T(8,128)(2,1)S(1)}, u32[]{:S(2)}, u32[]{:S(2)}) %collective-permute-start.16) | collective-permute-done | bytes 262176 | tf_op jit(solution)/shard_map/ppermute | solution.py:17
  46.0 0.9 collective-permute-start.17
  46.9 0.5 collective-permute-start.18
  47.4 1.8 %collective-permute-done.6 = bf16[2,128,512]{2,1,0:T(8,128)(2,1)S(1)} collective-permute-done((bf16[2,128,512]{2,1,0:T(8,128)(2,1)S(1)}, bf16[2,128,512]{2,1,0:T(8,128)(2,1)S(1)}, u32[]{:S(2)}, u32[]{:S(2)}) %collective-permute-start.6) | collective-permute-done | bytes 262176 | tf_op jit(solution)/shard_map/ppermute | solution.py:17
  49.2 0.5 collective-permute-start.25
  49.7 1.0 collective-permute-start.26
  50.7 1.3 %collective-permute-done.7 = bf16[2,128,512]{2,1,0:T(8,128)(2,1)S(1)} collective-permute-done((bf16[2,128,512]{2,1,0:T(8,128)(2,1)S(1)}, bf16[2,128,512]{2,1,0:T(8,128)(2,1)S(1)}, u32[]{:S(2)}, u32[]{:S(2)}) %collective-permute-start.7) | collective-permute-done | bytes 262176 | tf_op jit(solution)/shard_map/ppermute | solution.py:17
  52.0 0.5 collective-permute-start.12
  52.5 0.5 collective-permute-done.17.refs_3_
  53.0 0.6 collective-permute-start.19
  53.6 5.0 %collective-permute-done.25.refs_3_ = bf16[1,2,128,512]{3,2,1,0:T(8,128)(2,1)S(1)} collective-permute-done((bf16[1,2,128,512]{3,2,1,0:T(8,128)(2,1)S(1)}, bf16[1,2,128,512]{3,2,1,0:T(8,128)(2,1)S(1)}, u32[]{:S(2)}, u32[]{:S(2)}) %collective-permute-start.25) | collective-permute-done | bytes 262176 | tf_op jit(solution)/shard_map/ppermute | solution.py:33
  58.6 0.9 collective-permute-start.27
  59.6 1.3 %collective-permute-start.21 = (bf16[1,2,128,512]{3,2,1,0:T(8,128)(2,1)S(1)}, bf16[1,2,128,512]{3,2,1,0:T(8,128)(2,1)S(1)}, u32[]{:S(2)}, u32[]{:S(2)}) collective-permute-start(bf16[1,2,128,512]{3,2,1,0:T(8,128)(2,1)S(1)} %add_convert_fusion.5), channel_id=1, source_target_pairs={{0,1},{2,3},{4,5},{6,7},{8,9},{10,11},{12,13},{14,15},{16,17},{18,... | collective-permute-start | bytes 786440 | tf_op jit(solution)/shard_map/ppermute | solution.py:17
  60.9 3.3 %collective-permute-done.12.refs_8_ = bf16[1,2,128,512]{3,2,1,0:T(8,128)(2,1)S(1)} collective-permute-done((bf16[1,2,128,512]{3,2,1,0:T(8,128)(2,1)S(1)}, bf16[1,2,128,512]{3,2,1,0:T(8,128)(2,1)S(1)}, u32[]{:S(2)}, u32[]{:S(2)}) %collective-permute-start.12) | collective-permute-done | bytes 262176 | tf_op jit(solution)/shard_map/ppermute | solution.py:33
  64.2 0.9 collective-permute-start.13
  65.2 1.1 %collective-permute-start.14 = (bf16[1,2,128,512]{3,2,1,0:T(8,128)(2,1)S(1)}, bf16[1,2,128,512]{3,2,1,0:T(8,128)(2,1)S(1)}, u32[]{:S(2)}, u32[]{:S(2)}) collective-permute-start(bf16[1,2,128,512]{3,2,1,0:T(8,128)(2,1)S(1)} %collective-permute-done.12.refs_8_), channel_id=1, source_target_pairs={{0,16},{1,9},{2,18},{3,11},{4,20},{5,13},{6,22},{7,15},{8,24},{9,1... | collective-permute-start | bytes 786440 | tf_op jit(solution)/shard_map/ppermute | solution.py:33
  66.7 0.6 collective-permute-start.28
  67.3 3.3 %collective-permute-done.13.refs_9_ = bf16[1,2,128,512]{3,2,1,0:T(8,128)(2,1)S(1)} collective-permute-done((bf16[1,2,128,512]{3,2,1,0:T(8,128)(2,1)S(1)}, bf16[1,2,128,512]{3,2,1,0:T(8,128)(2,1)S(1)}, u32[]{:S(2)}, u32[]{:S(2)}) %collective-permute-start.13) | collective-permute-done | bytes 262176 | tf_op jit(solution)/shard_map/ppermute | solution.py:33
  70.6 0.7 collective-permute-start.22
  71.3 3.8 %collective-permute-done.14.refs_10_ = bf16[1,2,128,512]{3,2,1,0:T(8,128)(2,1)S(1)} collective-permute-done((bf16[1,2,128,512]{3,2,1,0:T(8,128)(2,1)S(1)}, bf16[1,2,128,512]{3,2,1,0:T(8,128)(2,1)S(1)}, u32[]{:S(2)}, u32[]{:S(2)}) %collective-permute-start.14) | collective-permute-done | bytes 262176 | tf_op jit(solution)/shard_map/ppermute | solution.py:33
  75.0 0.7 collective-permute-start.23
  75.9 1.3 %collective-permute-start.20 = (bf16[4,2,128,512]{3,2,1,0:T(8,128)(2,1)S(1)}, bf16[4,2,128,512]{3,2,1,0:T(8,128)(2,1)S(1)}, u32[]{:S(2)}, u32[]{:S(2)}) collective-permute-start(bf16[4,2,128,512]{3,2,1,0:T(8,128)(2,1)S(1)} %pad_maximum_fusion.1), channel_id=1, source_target_pairs={{1,2},{3,4},{5,6},{7,0},{9,10},{11,12},{13,14},{15,8},{17,18},{19,... | collective-permute-start | bytes 3145736 | tf_op jit(solution)/shard_map/ppermute | solution.py:17
  77.2 0.6 collective-permute-start.15
  77.8 1.5 %collective-permute-start.9 = (bf16[2,2,128,512]{3,2,1,0:T(8,128)(2,1)S(1)}, bf16[2,2,128,512]{3,2,1,0:T(8,128)(2,1)S(1)}, u32[]{:S(2)}, u32[]{:S(2)}) collective-permute-start(bf16[2,2,128,512]{3,2,1,0:T(8,128)(2,1)S(1)} %collective-permute-done.8.refs_2_), channel_id=1, source_target_pairs={{0,8},{1,17},{2,10},{3,19},{4,12},{5,21},{6,14},{7,23},{8,0},{9,25... | collective-permute-start | bytes 1572872 | tf_op jit(solution)/shard_map/ppermute | solution.py:33
  79.4 0.4 constant_dynamic-slice_fusion.3
  79.9 7.0 %collective-permute-done.9.refs_3_ = bf16[2,2,128,512]{3,2,1,0:T(8,128)(2,1)S(1)} collective-permute-done((bf16[2,2,128,512]{3,2,1,0:T(8,128)(2,1)S(1)}, bf16[2,2,128,512]{3,2,1,0:T(8,128)(2,1)S(1)}, u32[]{:S(2)}, u32[]{:S(2)}) %collective-permute-start.9) | collective-permute-done | bytes 524320 | tf_op jit(solution)/shard_map/ppermute | solution.py:33
  86.9 0.8 collective-permute-start.24
  87.8 1.0 collective-permute-start.10
  88.8 1.1 %collective-permute-start.11 = (bf16[2,2,128,512]{3,2,1,0:T(8,128)(2,1)S(1)}, bf16[2,2,128,512]{3,2,1,0:T(8,128)(2,1)S(1)}, u32[]{:S(2)}, u32[]{:S(2)}) collective-permute-start(bf16[2,2,128,512]{3,2,1,0:T(8,128)(2,1)S(1)} %collective-permute-done.9.refs_3_), channel_id=1, source_target_pairs={{0,16},{1,9},{2,18},{3,11},{4,20},{5,13},{6,22},{7,15},{8,24},{9,1... | collective-permute-start | bytes 1572872 | tf_op jit(solution)/shard_map/ppermute | solution.py:33
  89.9 2.6 %shard_map.49.refs_11_ = bf16[3,3,3,2,1,128,512]{6,5,4,3,2,1,0:T(8,128)(2,1)} custom-call(bf16[384,512]{1,0:T(8,128)(2,1)S(1)} %bitcast.23, bf16[384,512]{1,0:T(8,128)(2,1)S(1)} %bitcast.19, bf16[1,2,128,512]{3,2,1,0:T(8,128)(2,1)S(1)} %bitcast.38, bf16[1,2,128,512]{3,2,1,0:T(8,128)(2,1)S(1)} %collective-permute-done.17.refs_3_, ...), custom_call_target="tpu_custom_call" | custom-call | flops 1610612736 | bytes 1572864 | tf_op jit(solution)/shard_map/pallas_call | solution.py:267
  92.5 3.4 %shard_map.50.refs_8_ = bf16[3,3,3,2,1,128,512]{6,5,4,3,2,1,0:T(8,128)(2,1)} custom-call(bf16[384,512]{1,0:T(8,128)(2,1)S(1)} %bitcast.24, bf16[384,512]{1,0:T(8,128)(2,1)S(1)} %bitcast.20, bf16[1,2,128,512]{3,2,1,0:T(8,128)(2,1)S(1)} %bitcast.30, bf16[1,2,128,512]{3,2,1,0:T(8,128)(2,1)S(1)} %collective-permute-done.25.refs_3_, ...), custom_call_target="tpu_custom_call", output_to_operand_aliasing={{}: (11, {})} | custom-call | flops 2415919104 | bytes 2359296 | tf_op jit(solution)/shard_map/pallas_call | solution.py:267
  95.9 2.8 %shard_map.51.refs_6_ = bf16[3,3,3,2,1,128,512]{6,5,4,3,2,1,0:T(8,128)(2,1)} custom-call(bf16[384,512]{1,0:T(8,128)(2,1)S(1)} %bitcast.25, bf16[384,512]{1,0:T(8,128)(2,1)S(1)} %bitcast.21, bf16[4,2,128,512]{3,2,1,0:T(8,128)(2,1)S(1)} %collective-permute-done.15.refs_2_, ...), custom_call_target="tpu_custom_call", output_to_operand_aliasing={{}: (8, {})} | custom-call | flops 1610612736 | bytes 1572864 | tf_op jit(solution)/shard_map/pallas_call | solution.py:267
  98.7 4.0 %collective-permute-done.11.refs_5_ = bf16[2,2,128,512]{3,2,1,0:T(8,128)(2,1)S(1)} collective-permute-done((bf16[2,2,128,512]{3,2,1,0:T(8,128)(2,1)S(1)}, bf16[2,2,128,512]{3,2,1,0:T(8,128)(2,1)S(1)}, u32[]{:S(2)}, u32[]{:S(2)}) %collective-permute-start.11) | collective-permute-done | bytes 524320 | tf_op jit(solution)/shard_map/ppermute | solution.py:33
  102.7 2.6 %shard_map.52 = bf16[3,3,3,2,1,128,512]{6,5,4,3,2,1,0:T(8,128)(2,1)} custom-call(bf16[384,512]{1,0:T(8,128)(2,1)S(1)} %bitcast.26, bf16[384,512]{1,0:T(8,128)(2,1)S(1)} %bitcast.22, bf16[2,2,128,512]{3,2,1,0:T(8,128)(2,1)S(1)} %collective-permute-done.8.refs_2_, ...), custom_call_target="tpu_custom_call", output_to_operand_aliasing={{}: (6, {})} | custom-call | flops 1610612736 | bytes 1572864 | tf_op jit(solution)/shard_map/pallas_call | solution.py:267
  (38 shorter events, 1.7 us)
Async XLA Ops:
  4.7 11.6 %collective-permute-start = (bf16[2,2,128,512]{3,2,1,0:T(8,128)(2,1)S(1)}, bf16[2,2,128,512]{3,2,1,0:T(8,128)(2,1)S(1)}, u32[]{:S(2)}, u32[]{:S(2)}) collective-permute-start(bf16[2,2,128,512]{3,2,1,0:T(8,128)(2,1)S(1)} %get-tuple-element.22), channel_id=1, source_target_pairs={{0,8},{1,17},{2,10},{3,19},{4,12},{5,21},{6,14},{7,23},{8,0},{9,25... | collective-permute-start | bytes 1572872 | tf_op jit(solution)/shard_map/ppermute | solution.py:33
  11.0 11.8 %collective-permute-start.2 = (bf16[2,2,128,512]{3,2,1,0:T(8,128)(2,1)S(1)}, bf16[2,2,128,512]{3,2,1,0:T(8,128)(2,1)S(1)}, u32[]{:S(2)}, u32[]{:S(2)}) collective-permute-start(bf16[2,2,128,512]{3,2,1,0:T(8,128)(2,1)S(1)} %get-tuple-element.26), channel_id=1, source_target_pairs={{0,8},{1,17},{2,10},{3,19},{4,12},{5,21},{6,14},{7,23},{8,0},{9,25... | collective-permute-start | bytes 1572872 | tf_op jit(solution)/shard_map/ppermute | solution.py:33
  14.2 17.5 %collective-permute-start.4 = (bf16[2,2,128,512]{3,2,1,0:T(8,128)(2,1)S(1)}, bf16[2,2,128,512]{3,2,1,0:T(8,128)(2,1)S(1)}, u32[]{:S(2)}, u32[]{:S(2)}) collective-permute-start(bf16[2,2,128,512]{3,2,1,0:T(8,128)(2,1)S(1)} %get-tuple-element.29), channel_id=1, source_target_pairs={{0,8},{1,17},{2,10},{3,19},{4,12},{5,21},{6,14},{7,23},{8,0},{9,25... | collective-permute-start | bytes 1572872 | tf_op jit(solution)/shard_map/ppermute | solution.py:33
  16.5 18.4 %collective-permute-start.1 = (bf16[1,2,128,512]{3,2,1,0:T(8,128)(2,1)S(1)}, bf16[1,2,128,512]{3,2,1,0:T(8,128)(2,1)S(1)}, u32[]{:S(2)}, u32[]{:S(2)}) collective-permute-start(bf16[1,2,128,512]{3,2,1,0:T(8,128)(2,1)S(1)} %slice.35), channel_id=1, source_target_pairs={{0,16},{1,9},{2,18},{3,11},{4,20},{5,13},{6,22},{7,15},{8,24},{9,1... | collective-permute-start | bytes 786440 | tf_op jit(solution)/shard_map/ppermute | solution.py:33
  23.0 13.6 %collective-permute-start.3 = (bf16[1,2,128,512]{3,2,1,0:T(8,128)(2,1)S(1)}, bf16[1,2,128,512]{3,2,1,0:T(8,128)(2,1)S(1)}, u32[]{:S(2)}, u32[]{:S(2)}) collective-permute-start(bf16[1,2,128,512]{3,2,1,0:T(8,128)(2,1)S(1)} %slice.37), channel_id=1, source_target_pairs={{0,16},{1,9},{2,18},{3,11},{4,20},{5,13},{6,22},{7,15},{8,24},{9,1... | collective-permute-start | bytes 786440 | tf_op jit(solution)/shard_map/ppermute | solution.py:33
  31.9 7.3 %collective-permute-start.5 = (bf16[1,2,128,512]{3,2,1,0:T(8,128)(2,1)S(1)}, bf16[1,2,128,512]{3,2,1,0:T(8,128)(2,1)S(1)}, u32[]{:S(2)}, u32[]{:S(2)}) collective-permute-start(bf16[1,2,128,512]{3,2,1,0:T(8,128)(2,1)S(1)} %slice.39), channel_id=1, source_target_pairs={{0,16},{1,9},{2,18},{3,11},{4,20},{5,13},{6,22},{7,15},{8,24},{9,1... | collective-permute-start | bytes 786440 | tf_op jit(solution)/shard_map/ppermute | solution.py:33
  34.9 11.0 %collective-permute-start.16 = (bf16[2,128,512]{2,1,0:T(8,128)(2,1)S(1)}, bf16[2,128,512]{2,1,0:T(8,128)(2,1)S(1)}, u32[]{:S(2)}, u32[]{:S(2)}) collective-permute-start(bf16[2,128,512]{2,1,0:T(8,128)(2,1)S(1)} %bitcast.39), channel_id=1, source_target_pairs={{0,2},{1,3},{2,4},{3,5},{4,6},{5,7},{6,0},{7,1},{8,10},{9,11},{10,... | collective-permute-start | bytes 786440 | tf_op jit(solution)/shard_map/ppermute | solution.py:17
  36.6 12.5 %collective-permute-start.6 = (bf16[2,128,512]{2,1,0:T(8,128)(2,1)S(1)}, bf16[2,128,512]{2,1,0:T(8,128)(2,1)S(1)}, u32[]{:S(2)}, u32[]{:S(2)}) collective-permute-start(bf16[2,128,512]{2,1,0:T(8,128)(2,1)S(1)} %get-tuple-element.35), channel_id=1, source_target_pairs={{0,2},{1,3},{2,4},{3,5},{4,6},{5,7},{6,0},{7,1},{8,10},{9,11},{10,... | collective-permute-start | bytes 786440 | tf_op jit(solution)/shard_map/ppermute | solution.py:17
  39.3 12.7 %collective-permute-start.7 = (bf16[2,128,512]{2,1,0:T(8,128)(2,1)S(1)}, bf16[2,128,512]{2,1,0:T(8,128)(2,1)S(1)}, u32[]{:S(2)}, u32[]{:S(2)}) collective-permute-start(bf16[2,128,512]{2,1,0:T(8,128)(2,1)S(1)} %get-tuple-element.37), channel_id=1, source_target_pairs={{0,2},{1,3},{2,4},{3,5},{4,6},{5,7},{6,0},{7,1},{8,10},{9,11},{10,... | collective-permute-start | bytes 786440 | tf_op jit(solution)/shard_map/ppermute | solution.py:17
  46.0 7.0 %collective-permute-start.17 = (bf16[1,2,128,512]{3,2,1,0:T(8,128)(2,1)S(1)}, bf16[1,2,128,512]{3,2,1,0:T(8,128)(2,1)S(1)}, u32[]{:S(2)}, u32[]{:S(2)}) collective-permute-start(bf16[1,2,128,512]{3,2,1,0:T(8,128)(2,1)S(1)} %bitcast.35), channel_id=1, source_target_pairs={{0,8},{1,17},{2,10},{3,19},{4,12},{5,21},{6,14},{7,23},{8,0},{9,25... | collective-permute-start | bytes 786440 | tf_op jit(solution)/shard_map/ppermute | solution.py:33
  46.9 12.8 %collective-permute-start.18 = (bf16[1,2,128,512]{3,2,1,0:T(8,128)(2,1)S(1)}, bf16[1,2,128,512]{3,2,1,0:T(8,128)(2,1)S(1)}, u32[]{:S(2)}, u32[]{:S(2)}) collective-permute-start(bf16[1,2,128,512]{3,2,1,0:T(8,128)(2,1)S(1)} %bitcast.36), channel_id=1, source_target_pairs={{0,16},{1,9},{2,18},{3,11},{4,20},{5,13},{6,22},{7,15},{8,24},{9,1... | collective-permute-start | bytes 786440 | tf_op jit(solution)/shard_map/ppermute | solution.py:33
  49.2 9.4 %collective-permute-start.25 = (bf16[1,2,128,512]{3,2,1,0:T(8,128)(2,1)S(1)}, bf16[1,2,128,512]{3,2,1,0:T(8,128)(2,1)S(1)}, u32[]{:S(2)}, u32[]{:S(2)}) collective-permute-start(bf16[1,2,128,512]{3,2,1,0:T(8,128)(2,1)S(1)} %bitcast.27), channel_id=1, source_target_pairs={{0,8},{1,17},{2,10},{3,19},{4,12},{5,21},{6,14},{7,23},{8,0},{9,25... | collective-permute-start | bytes 786440 | tf_op jit(solution)/shard_map/ppermute | solution.py:33
  49.7 16.7 %collective-permute-start.26 = (bf16[1,2,128,512]{3,2,1,0:T(8,128)(2,1)S(1)}, bf16[1,2,128,512]{3,2,1,0:T(8,128)(2,1)S(1)}, u32[]{:S(2)}, u32[]{:S(2)}) collective-permute-start(bf16[1,2,128,512]{3,2,1,0:T(8,128)(2,1)S(1)} %bitcast.28), channel_id=1, source_target_pairs={{0,16},{1,9},{2,18},{3,11},{4,20},{5,13},{6,22},{7,15},{8,24},{9,1... | collective-permute-start | bytes 786440 | tf_op jit(solution)/shard_map/ppermute | solution.py:33
  52.0 12.2 %collective-permute-start.12 = (bf16[1,2,128,512]{3,2,1,0:T(8,128)(2,1)S(1)}, bf16[1,2,128,512]{3,2,1,0:T(8,128)(2,1)S(1)}, u32[]{:S(2)}, u32[]{:S(2)}) collective-permute-start(bf16[1,2,128,512]{3,2,1,0:T(8,128)(2,1)S(1)} %bitcast.31), channel_id=1, source_target_pairs={{0,8},{1,17},{2,10},{3,19},{4,12},{5,21},{6,14},{7,23},{8,0},{9,25... | collective-permute-start | bytes 786440 | tf_op jit(solution)/shard_map/ppermute | solution.py:33
  53.0 12.2 %collective-permute-start.19 = (bf16[1,2,128,512]{3,2,1,0:T(8,128)(2,1)S(1)}, bf16[1,2,128,512]{3,2,1,0:T(8,128)(2,1)S(1)}, u32[]{:S(2)}, u32[]{:S(2)}) collective-permute-start(bf16[1,2,128,512]{3,2,1,0:T(8,128)(2,1)S(1)} %collective-permute-done.17.refs_3_), channel_id=1, source_target_pairs={{0,16},{1,9},{2,18},{3,11},{4,20},{5,13},{6,22},{7,15},{8,24},{9,1... | collective-permute-start | bytes 786440 | tf_op jit(solution)/shard_map/ppermute | solution.py:33
  58.6 7.9 %collective-permute-start.27 = (bf16[1,2,128,512]{3,2,1,0:T(8,128)(2,1)S(1)}, bf16[1,2,128,512]{3,2,1,0:T(8,128)(2,1)S(1)}, u32[]{:S(2)}, u32[]{:S(2)}) collective-permute-start(bf16[1,2,128,512]{3,2,1,0:T(8,128)(2,1)S(1)} %collective-permute-done.25.refs_3_), channel_id=1, source_target_pairs={{0,16},{1,9},{2,18},{3,11},{4,20},{5,13},{6,22},{7,15},{8,24},{9,1... | collective-permute-start | bytes 786440 | tf_op jit(solution)/shard_map/ppermute | solution.py:33
  59.6 7.1 %collective-permute-start.21 = (bf16[1,2,128,512]{3,2,1,0:T(8,128)(2,1)S(1)}, bf16[1,2,128,512]{3,2,1,0:T(8,128)(2,1)S(1)}, u32[]{:S(2)}, u32[]{:S(2)}) collective-permute-start(bf16[1,2,128,512]{3,2,1,0:T(8,128)(2,1)S(1)} %add_convert_fusion.5), channel_id=1, source_target_pairs={{0,1},{2,3},{4,5},{6,7},{8,9},{10,11},{12,13},{14,15},{16,17},{18,... | collective-permute-start | bytes 786440 | tf_op jit(solution)/shard_map/ppermute | solution.py:17
  64.2 6.4 %collective-permute-start.13 = (bf16[1,2,128,512]{3,2,1,0:T(8,128)(2,1)S(1)}, bf16[1,2,128,512]{3,2,1,0:T(8,128)(2,1)S(1)}, u32[]{:S(2)}, u32[]{:S(2)}) collective-permute-start(bf16[1,2,128,512]{3,2,1,0:T(8,128)(2,1)S(1)} %bitcast.32), channel_id=1, source_target_pairs={{0,16},{1,9},{2,18},{3,11},{4,20},{5,13},{6,22},{7,15},{8,24},{9,1... | collective-permute-start | bytes 786440 | tf_op jit(solution)/shard_map/ppermute | solution.py:33
  65.2 9.9 %collective-permute-start.14 = (bf16[1,2,128,512]{3,2,1,0:T(8,128)(2,1)S(1)}, bf16[1,2,128,512]{3,2,1,0:T(8,128)(2,1)S(1)}, u32[]{:S(2)}, u32[]{:S(2)}) collective-permute-start(bf16[1,2,128,512]{3,2,1,0:T(8,128)(2,1)S(1)} %collective-permute-done.12.refs_8_), channel_id=1, source_target_pairs={{0,16},{1,9},{2,18},{3,11},{4,20},{5,13},{6,22},{7,15},{8,24},{9,1... | collective-permute-start | bytes 786440 | tf_op jit(solution)/shard_map/ppermute | solution.py:33
  66.4 11.4 %collective-permute-start.8 = (bf16[2,2,128,512]{3,2,1,0:T(8,128)(2,1)S(1)}, bf16[2,2,128,512]{3,2,1,0:T(8,128)(2,1)S(1)}, u32[]{:S(2)}, u32[]{:S(2)}) collective-permute-start(bf16[2,2,128,512]{3,2,1,0:T(8,128)(2,1)S(1)} %pad_maximum_fusion.5), channel_id=1, source_target_pairs={{0,1},{1,2},{2,3},{3,4},{4,5},{5,6},{6,7},{7,0},{8,9},{9,10},{10,1... | collective-permute-start | bytes 1572872 | tf_op jit(solution)/shard_map/ppermute | solution.py:17
  66.5 21.3 %collective-permute-start.29 = (bf16[4,2,128,512]{3,2,1,0:T(8,128)(2,1)S(1)}, bf16[4,2,128,512]{3,2,1,0:T(8,128)(2,1)S(1)}, u32[]{:S(2)}, u32[]{:S(2)}) collective-permute-start(bf16[4,2,128,512]{3,2,1,0:T(8,128)(2,1)S(1)} %pad_maximum_fusion.1), channel_id=1, source_target_pairs={{0,1},{1,0},{2,3},{3,2},{4,5},{5,4},{6,7},{7,6},{8,9},{9,8},{10,11... | collective-permute-start | bytes 3145736 | tf_op jit(solution)/shard_map/ppermute | solution.py:22
  66.7 22.1 %collective-permute-start.28 = (bf16[4,2,128,512]{3,2,1,0:T(8,128)(2,1)S(1)}, bf16[4,2,128,512]{3,2,1,0:T(8,128)(2,1)S(1)}, u32[]{:S(2)}, u32[]{:S(2)}) collective-permute-start(bf16[4,2,128,512]{3,2,1,0:T(8,128)(2,1)S(1)} %pad_maximum_fusion.2), channel_id=1, source_target_pairs={{0,1},{1,0},{2,3},{3,2},{4,5},{5,4},{6,7},{7,6},{8,9},{9,8},{10,11... | collective-permute-start | bytes 3145736 | tf_op jit(solution)/shard_map/ppermute | solution.py:22
  70.6 5.3 %collective-permute-start.22 = (bf16[1,2,128,512]{3,2,1,0:T(8,128)(2,1)S(1)}, bf16[1,2,128,512]{3,2,1,0:T(8,128)(2,1)S(1)}, u32[]{:S(2)}, u32[]{:S(2)}) collective-permute-start(bf16[1,2,128,512]{3,2,1,0:T(8,128)(2,1)S(1)} %collective-permute-done.21.refs_4_), channel_id=1, source_target_pairs={{1,17},{3,19},{5,21},{7,23},{9,25},{11,27},{13,29},{15,31},{17,1},... | collective-permute-start | bytes 786440 | tf_op jit(solution)/shard_map/ppermute | solution.py:33
  75.0 2.1 %collective-permute-start.23 = (bf16[1,2,128,512]{3,2,1,0:T(8,128)(2,1)S(1)}, bf16[1,2,128,512]{3,2,1,0:T(8,128)(2,1)S(1)}, u32[]{:S(2)}, u32[]{:S(2)}) collective-permute-start(bf16[1,2,128,512]{3,2,1,0:T(8,128)(2,1)S(1)} %collective-permute-done.21.refs_4_), channel_id=1, source_target_pairs={{1,9},{3,11},{5,13},{7,15},{9,1},{11,3},{13,5},{15,7},{17,25},{19,... | collective-permute-start | bytes 786440 | tf_op jit(solution)/shard_map/ppermute | solution.py:33
  75.9 20.1 %collective-permute-start.20 = (bf16[4,2,128,512]{3,2,1,0:T(8,128)(2,1)S(1)}, bf16[4,2,128,512]{3,2,1,0:T(8,128)(2,1)S(1)}, u32[]{:S(2)}, u32[]{:S(2)}) collective-permute-start(bf16[4,2,128,512]{3,2,1,0:T(8,128)(2,1)S(1)} %pad_maximum_fusion.1), channel_id=1, source_target_pairs={{1,2},{3,4},{5,6},{7,0},{9,10},{11,12},{13,14},{15,8},{17,18},{19,... | collective-permute-start | bytes 3145736 | tf_op jit(solution)/shard_map/ppermute | solution.py:17
  77.2 18.8 %collective-permute-start.15 = (bf16[4,2,128,512]{3,2,1,0:T(8,128)(2,1)S(1)}, bf16[4,2,128,512]{3,2,1,0:T(8,128)(2,1)S(1)}, u32[]{:S(2)}, u32[]{:S(2)}) collective-permute-start(bf16[4,2,128,512]{3,2,1,0:T(8,128)(2,1)S(1)} %pad_maximum_fusion), channel_id=1, source_target_pairs={{0,1},{1,0},{2,3},{3,2},{4,5},{5,4},{6,7},{7,6},{8,9},{9,8},{10,11... | collective-permute-start | bytes 3145736 | tf_op jit(solution)/shard_map/ppermute | solution.py:22
  77.8 9.2 %collective-permute-start.9 = (bf16[2,2,128,512]{3,2,1,0:T(8,128)(2,1)S(1)}, bf16[2,2,128,512]{3,2,1,0:T(8,128)(2,1)S(1)}, u32[]{:S(2)}, u32[]{:S(2)}) collective-permute-start(bf16[2,2,128,512]{3,2,1,0:T(8,128)(2,1)S(1)} %collective-permute-done.8.refs_2_), channel_id=1, source_target_pairs={{0,8},{1,17},{2,10},{3,19},{4,12},{5,21},{6,14},{7,23},{8,0},{9,25... | collective-permute-start | bytes 1572872 | tf_op jit(solution)/shard_map/ppermute | solution.py:33
  86.9 9.0 %collective-permute-start.24 = (bf16[1,2,128,512]{3,2,1,0:T(8,128)(2,1)S(1)}, bf16[1,2,128,512]{3,2,1,0:T(8,128)(2,1)S(1)}, u32[]{:S(2)}, u32[]{:S(2)}) collective-permute-start(bf16[1,2,128,512]{3,2,1,0:T(8,128)(2,1)S(1)} %collective-permute-done.22.refs_5_), channel_id=1, source_target_pairs={{1,9},{3,11},{5,13},{7,15},{9,1},{11,3},{13,5},{15,7},{17,25},{19,... | collective-permute-start | bytes 786440 | tf_op jit(solution)/shard_map/ppermute | solution.py:33
  87.8 10.9 %collective-permute-start.10 = (bf16[2,2,128,512]{3,2,1,0:T(8,128)(2,1)S(1)}, bf16[2,2,128,512]{3,2,1,0:T(8,128)(2,1)S(1)}, u32[]{:S(2)}, u32[]{:S(2)}) collective-permute-start(bf16[2,2,128,512]{3,2,1,0:T(8,128)(2,1)S(1)} %collective-permute-done.8.refs_2_), channel_id=1, source_target_pairs={{0,16},{1,9},{2,18},{3,11},{4,20},{5,13},{6,22},{7,15},{8,24},{9,1... | collective-permute-start | bytes 1572872 | tf_op jit(solution)/shard_map/ppermute | solution.py:33
  88.8 13.9 %collective-permute-start.11 = (bf16[2,2,128,512]{3,2,1,0:T(8,128)(2,1)S(1)}, bf16[2,2,128,512]{3,2,1,0:T(8,128)(2,1)S(1)}, u32[]{:S(2)}, u32[]{:S(2)}) collective-permute-start(bf16[2,2,128,512]{3,2,1,0:T(8,128)(2,1)S(1)} %collective-permute-done.9.refs_3_), channel_id=1, source_target_pairs={{0,16},{1,9},{2,18},{3,11},{4,20},{5,13},{6,22},{7,15},{8,24},{9,1... | collective-permute-start | bytes 1572872 | tf_op jit(solution)/shard_map/ppermute | solution.py:33
